TPU v7x, 256 devices: a whole 4x4x8 slice. The times are simulated.
256 devices in a mesh: corpus: 64 (over x, z, core), rep: 4 (over y).
Axes of the slice: x: 4, y: 4, z: 8, core: 2. Of those that a mesh axis runs over, the one named last changes fastest.
Arguments:
- queries: bfloat16 [32768, 768], P(('corpus', 'rep')), may hold values from -18 to 18
- teacher: float32 [32768, 64], P(('corpus', 'rep')), may hold values from -15 to 305
- slab: bfloat16 [65536, 768], P('corpus'), may hold values from -12 to 12
- candidates: int32 [32768, 64], P(('corpus', 'rep')), may hold values from 0 to 65535, as said below
- hot_ids: int32 [2048], replicated, may hold values from 0 to 65535, as said below
- location: int32 [65536], replicated, may hold values from 0 to 65535, as said below
Outputs:
- loss: float32 [32768], P(('corpus', 'rep'))
- query_grad: float32 [32768, 768], P(('corpus', 'rep'))
- slab_grad: float32 [65536, 768], P(('corpus', 'rep'))
Inputs may be any that keep to these rules, and one draw needn't show every extreme that they name: `candidates`: every query names 64 passage ids, exactly 8 of them absent from hot_ids; ids may repeat. With the owner of id p being location[p] // 1024, the ids absent from hot_ids among one device's 128 queries (aligned blocks of 128 rows) fall at most 24 times on any owner; in each block some owner gets exactly 24, the same owner for all blocks whose block number has the same remainder modulo the number of rep devices. `hot_ids`: 2048 distinct ids; entries 32 * c to 32 * c + 31 are owned by corpus index c. `location`: A permutation of the passage ids onto slab rows.
All inputs are finite; a program needn't handle non-finite values.
Results may differ from a plain program's by a relative error of at most 0.0026.
Values may be sent and summed in bfloat16 or wider, within the bound.
No kernel may reach another device: no remote copies, remote signals or barrier semaphores. Data moves between devices by JAX's collectives and lax.ppermute only.
A program may use at most 128 MiB of HBM per device.

v0:
```python
import functools
import math

import jax
import jax.numpy as jnp
from jax import lax
from jax.experimental import pallas as pl
from jax.experimental.pallas import tpu as pltpu
from jax.sharding import PartitionSpec as P

COLD = 8
LANES = 128
RADIX = 256
PAD_SLOTS = 32
F32 = jnp.float32
BF16 = jnp.bfloat16
VMEM_SPEC = pl.BlockSpec(memory_space=pltpu.VMEM)
ROWS_DOT = (((1,), (1,)), ((), ()))


def iota(shape, axis):
    return lax.broadcasted_iota(jnp.int32, shape, axis)


def one_hot(mask, dtype=BF16):
    return jnp.where(mask, 1.0, 0.0).astype(dtype)


def pick_rows(mask, values):
    return jnp.sum(jnp.where(mask, values, jnp.zeros_like(values)), axis=0, keepdims=True)


def request_kernel(per_owner, capacity, groups, cand_t, hot_ref, loc_ref, req_ref, place_ref, sel_ref, hit_t):
    cand_count, q_rows = cand_t.shape
    hot_total = hot_ref.shape[1]
    high_rows = loc_ref.shape[0]
    hot = hot_ref[...]
    low_hot = one_hot(iota((RADIX, hot_total), 0) == (hot & (RADIX - 1)))
    high_hot = one_hot(iota((high_rows, hot_total), 0) == (hot // RADIX))
    marks = lax.dot_general(low_hot, high_hot, ROWS_DOT, preferred_element_type=F32).astype(BF16)
    low_iota = iota((RADIX, q_rows), 0)
    high_iota = iota((high_rows, q_rows), 0)

    def lookup(tables, ids):
        hots = jnp.concatenate([one_hot(high_iota == (i // RADIX)) for i in ids], axis=1)
        found = [jnp.dot(t, hots, preferred_element_type=F32) for t in tables]
        masks = [low_iota == (i & (RADIX - 1)) for i in ids]
        return [
            [pick_rows(m, f[:, n * q_rows : (n + 1) * q_rows]) for n, m in enumerate(masks)]
            for f in found
        ]

    def check(j, carry):
        start = pl.multiple_of(j * 8, 8)
        rows = cand_t[pl.ds(start, 8), :]
        hits = lookup([marks], [rows[n : n + 1, :] for n in range(8)])[0]
        hit_t[pl.ds(start, 8), :] = jnp.concatenate(hits, axis=0)
        return carry

    lax.fori_loop(0, cand_count // 8, check, 0)
    cold = hit_t[...] < 0.5
    earlier = one_hot(iota((cand_count, cand_count), 0) > iota((cand_count, cand_count), 1))
    order = jnp.dot(earlier, one_hot(cold), preferred_element_type=F32).astype(jnp.int32)
    sel = jnp.where(cold, order, -1)
    sel_ref[...] = sel
    cand = cand_t[...]
    ids = [pick_rows(sel == r, cand) for r in range(COLD)]
    loc = loc_ref[...]
    high_table = jnp.transpose((loc // RADIX).astype(F32)).astype(BF16)
    low_table = jnp.transpose((loc & (RADIX - 1)).astype(F32)).astype(BF16)
    high_part, low_part = lookup([high_table, low_table], ids)
    before = one_hot(iota((q_rows, q_rows), 0) < iota((q_rows, q_rows), 1))
    owner_iota = iota((groups, q_rows), 0)
    slot_iota = iota((LANES, q_rows), 0)
    query = iota((1, q_rows), 1).astype(F32)
    base = jnp.zeros((groups, 1), F32)
    owners, ranks, owner_hots, low_vals, high_vals, query_vals = [], [], [], [], [], []
    for r in range(COLD):
        row = high_part[r].astype(jnp.int32) * RADIX + low_part[r].astype(jnp.int32)
        owner = row // per_owner
        local = row & (per_owner - 1)
        owner_hot = one_hot(owner_iota == owner, F32)
        count = jnp.dot(owner_hot.astype(BF16), before, preferred_element_type=F32) + base
        rank = jnp.sum(owner_hot * count, axis=0, keepdims=True).astype(jnp.int32)
        base = base + jnp.sum(owner_hot, axis=1, keepdims=True)
        at_slot = slot_iota == rank
        owners.append(owner)
        ranks.append(rank)
        owner_hots.append(owner_hot.astype(BF16))
        low_vals.append(jnp.where(at_slot, (local & (RADIX - 1)).astype(F32), 0.0).astype(BF16))
        high_vals.append(jnp.where(at_slot, (local // RADIX + RADIX // 2).astype(F32), 0.0).astype(BF16))
        query_vals.append(jnp.where(at_slot, query, 0.0).astype(BF16))
    owner_all = jnp.concatenate(owner_hots, axis=1)

    def spread(vals):
        got = lax.dot_general(owner_all, jnp.concatenate(vals, axis=1), ROWS_DOT, preferred_element_type=F32)
        return got.astype(jnp.int32)

    low_got, high_got, query_got = spread(low_vals), spread(high_vals), spread(query_vals)
    packed = low_got + RADIX * (high_got - RADIX // 2) + per_owner * query_got
    req_ref[...] = jnp.where(high_got > 0, packed, -1)
    place_ref[...] = jnp.concatenate(owners + ranks, axis=0)


def count_kernel(cand_t, teacher_ref, hot_ref, sel_ref, count_ref, target_ref, misc_ref, soft_t):
    cand_count, q_rows = cand_t.shape
    teacher = teacher_ref[...]
    shifted = teacher - jnp.max(teacher, axis=0, keepdims=True)
    log_target = shifted - jnp.log(jnp.sum(jnp.exp(shifted), axis=0, keepdims=True))
    target = jnp.exp(log_target)
    soft_t[...] = target
    sel = sel_ref[...]
    entropy = jnp.sum(target * log_target, axis=0, keepdims=True)
    rows = [pick_rows(sel == r, target) for r in range(COLD)]
    misc_ref[...] = jnp.concatenate(rows + [jnp.broadcast_to(entropy, (8, q_rows))], axis=0)
    hot_cols = jnp.transpose(hot_ref[...])
    for a in range(hot_ref.shape[0]):
        column = jnp.broadcast_to(hot_cols[:, a : a + 1], (LANES, q_rows))

        def add(k, carry):
            count, total = carry
            match = column == cand_t[pl.ds(k, 1), :]
            count = count + jnp.where(match, 1.0, 0.0)
            total = total + jnp.where(match, soft_t[pl.ds(k, 1), :], 0.0)
            return count, total

        start = (jnp.ones((LANES, q_rows), F32), jnp.zeros((LANES, q_rows), F32))
        count, total = lax.fori_loop(0, cand_count, add, start, unroll=4)
        count_ref[a * LANES : (a + 1) * LANES, :] = count
        target_ref[a * LANES : (a + 1) * LANES, :] = total


def score_kernel(scale, capacity, q_ref, hot_ref, found_ref, count_ref, target_ref, place_ref, misc_ref, loss_ref, pay_ref, weight_ref, hot_scr, slot_scr):
    groups, hot_each, feat = hot_ref.shape
    slots = found_ref.shape[0]
    q_rows = q_ref.shape[0]
    q = q_ref[...]
    step = 8
    place = place_ref[...]
    dests = [place[r : r + 1] * capacity + place[COLD + r : COLD + r + 1] for r in range(COLD)]
    top = jnp.full((1, q_rows), -jnp.inf, F32)
    for j in range(groups // step):
        rows = hot_ref[j * step : (j + 1) * step].reshape(step * hot_each, feat)
        got = scale * lax.dot_general(rows, q, ROWS_DOT, preferred_element_type=F32)
        hot_scr[j * step * hot_each : (j + 1) * step * hot_each, :] = got
        top = jnp.maximum(top, jnp.max(got, axis=0, keepdims=True))
    colds = [jnp.zeros((1, q_rows), F32) for _ in range(COLD)]
    chunk = 256
    for j in range(slots // chunk):
        rows = found_ref[j * chunk : (j + 1) * chunk, :]
        got = scale * lax.dot_general(rows, q, ROWS_DOT, preferred_element_type=F32)
        ids = iota((chunk, q_rows), 0) + j * chunk
        for r in range(COLD):
            colds[r] = colds[r] + pick_rows(ids == dests[r], got)
    cold = jnp.concatenate(colds, axis=0)
    top = jnp.maximum(top, jnp.max(cold, axis=0, keepdims=True))
    total = jnp.sum(jnp.exp(cold - top), axis=0, keepdims=True)
    hot_dot = jnp.zeros((1, q_rows), F32)
    for j in range(groups // step):
        part = slice(j * step * hot_each, (j + 1) * step * hot_each)
        hot = hot_scr[part, :]
        total = total + jnp.sum(count_ref[part, :] * jnp.exp(hot - top), axis=0, keepdims=True)
        hot_dot = hot_dot + jnp.sum(target_ref[part, :] * hot, axis=0, keepdims=True)
    log_total = top + jnp.log(total)
    cold_target = misc_ref[0:COLD, :]
    entropy = misc_ref[COLD : COLD + 1, :]
    loss_ref[...] = entropy - hot_dot - jnp.sum(cold_target * cold, axis=0, keepdims=True) + log_total
    weight = (jnp.exp(cold - log_total) - cold_target).astype(BF16).astype(F32)
    owner_iota = iota((groups, q_rows), 0)
    slot_iota = iota((LANES, q_rows), 0)
    owner_all = jnp.concatenate([one_hot(owner_iota == place[r : r + 1]) for r in range(COLD)], axis=1)
    slot_all = jnp.concatenate(
        [
            jnp.where(slot_iota == place[COLD + r : COLD + r + 1], weight[r : r + 1], 0.0).astype(BF16)
            for r in range(COLD)
        ],
        axis=1,
    )
    slot_scr[...] = lax.dot_general(owner_all, slot_all, ROWS_DOT, preferred_element_type=F32)
    for g in range(groups):
        part = slice(g * hot_each, (g + 1) * hot_each)
        coef = count_ref[part, :] * jnp.exp(hot_scr[part, :] - log_total) - target_ref[part, :]
        slot_row = jnp.broadcast_to(slot_scr[g : g + 1, :], (8, q_rows))
        pay_ref[g] = jnp.concatenate([coef, slot_row], axis=0).astype(BF16)
    for j in range(slots // chunk):
        ids = iota((chunk, q_rows), 0) + j * chunk
        made = jnp.zeros((chunk, q_rows), F32)
        for r in range(COLD):
            made = jnp.where(ids == dests[r], weight[r : r + 1], made)
        weight_ref[j * chunk : (j + 1) * chunk, :] = made.astype(BF16)


def query_kernel(scale, hot_ref, pay_ref, found_ref, weight_ref, out_ref):
    groups, hot_each, feat = hot_ref.shape
    acc = jnp.zeros(out_ref.shape, F32)
    step = 8
    first = (((0,), (0,)), ((), ()))
    for j in range(groups // step):
        rows = hot_ref[j * step : (j + 1) * step].reshape(step * hot_each, feat)
        coef = jnp.concatenate([pay_ref[j * step + n, 0:hot_each, :] for n in range(step)], axis=0)
        acc = acc + lax.dot_general(coef, rows, first, preferred_element_type=F32)
    chunk = 256
    for j in range(found_ref.shape[0] // chunk):
        part = slice(j * chunk, (j + 1) * chunk)
        acc = acc + lax.dot_general(weight_ref[part, :], found_ref[part, :], first, preferred_element_type=F32)
    out_ref[...] = scale * acc


def slab_kernel(scale, pay_ref, query_ref, row_ref, loc_ref, out_ref, terms, hot_acc):
    step = pl.program_id(0)
    groups = pay_ref.shape[0]
    hot_each = hot_acc.shape[0]
    feat = out_ref.shape[1]

    @pl.when(step == 0)
    def _():
        hot_acc[...] = jnp.zeros_like(hot_acc)

    acc = hot_acc[...]
    for n in range(0, groups, 2):
        left = jnp.concatenate([pay_ref[n, 0:hot_each, :], pay_ref[n + 1, 0:hot_each, :]], axis=1)
        right = jnp.concatenate([query_ref[n], query_ref[n + 1]], axis=0)
        acc = acc + jnp.dot(left, right, preferred_element_type=F32)
    hot_acc[...] = acc
    sent = jnp.concatenate([pay_ref[n, hot_each : hot_each + 8, :].astype(F32)[0:1] for n in range(groups)], axis=0)
    cols = jnp.transpose(sent)
    made = []
    for n in range(groups):
        col = scale * jnp.broadcast_to(cols[0:PAD_SLOTS, n : n + 1], (PAD_SLOTS, LANES))
        wide = jnp.concatenate([col] * (feat // LANES), axis=1)
        rows = row_ref[n * PAD_SLOTS : (n + 1) * PAD_SLOTS, :].astype(F32)
        made.append((wide * rows).astype(BF16))
    size = groups * PAD_SLOTS
    terms[pl.ds(pl.multiple_of(step * size, size), size), :] = jnp.concatenate(made, axis=0)

    @pl.when(step == pl.num_programs(0) - 1)
    def _():
        full = scale * hot_acc[...]
        high = full.astype(BF16)
        rest = full - high.astype(F32)
        mid = rest.astype(BF16)
        low = (rest - mid.astype(F32)).astype(BF16)
        base = terms.shape[0] - LANES
        terms[base:, :] = jnp.concatenate([high, mid, low, jnp.zeros_like(low)], axis=0)
        loc = loc_ref[...]
        tile = 128

        def land(j, carry):
            start = pl.multiple_of(j * tile, tile)
            at = one_hot(iota((tile, loc.shape[1]), 0) + start == loc)
            got = jnp.dot(at, terms[...], preferred_element_type=F32)
            out_ref[pl.ds(start, tile), :] = got.astype(BF16)
            return carry

        lax.fori_loop(0, out_ref.shape[0] // tile, land, 0)


def shards(queries, teacher, slab, candidates, hot_ids, location):
    groups = lax.axis_size("corpus")
    reps = lax.axis_size("rep")
    corpus_idx = lax.axis_index("corpus")
    q_rows, feat = queries.shape
    per_owner = slab.shape[0]
    hot_total = hot_ids.shape[0]
    hot_each = hot_total // groups
    cand_count = candidates.shape[1]
    capacity = q_rows * COLD * 3 // (2 * groups)
    scale = 2.0 / math.sqrt(feat)
    mine = lax.dynamic_slice_in_dim(hot_ids, corpus_idx * hot_each, hot_each)
    own_hot = location[mine] - corpus_idx * per_owner
    sent_rows = jnp.concatenate([queries, slab[own_hot]], axis=0)
    cand_t, sent_rows = lax.optimization_barrier((candidates.T, sent_rows))
    gathered = lax.all_gather(sent_rows, "corpus", axis=0, tiled=False)
    req, place, sel = pl.pallas_call(
        functools.partial(request_kernel, per_owner, capacity, groups),
        out_shape=(
            jax.ShapeDtypeStruct((groups, LANES), jnp.int32),
            jax.ShapeDtypeStruct((2 * COLD, q_rows), jnp.int32),
            jax.ShapeDtypeStruct((cand_count, q_rows), jnp.int32),
        ),
        in_specs=[VMEM_SPEC] * 3,
        out_specs=(VMEM_SPEC,) * 3,
        scratch_shapes=[pltpu.VMEM((cand_count, q_rows), F32)],
        name="request",
    )(cand_t, hot_ids.reshape(1, hot_total), location.reshape(-1, RADIX))
    asked = lax.all_to_all(req.reshape(groups, 1, LANES), "corpus", split_axis=0, concat_axis=0, tiled=True)
    asked = asked.reshape(groups, LANES)
    asked_slots = jnp.maximum(asked[:, :capacity], 0)
    found = slab[asked_slots & (per_owner - 1)]
    found = lax.all_to_all(found, "corpus", split_axis=0, concat_axis=0, tiled=True)
    found = found.reshape(groups * capacity, feat)
    count, target, misc = pl.pallas_call(
        count_kernel,
        out_shape=(
            jax.ShapeDtypeStruct((hot_total, q_rows), F32),
            jax.ShapeDtypeStruct((hot_total, q_rows), F32),
            jax.ShapeDtypeStruct((2 * COLD, q_rows), F32),
        ),
        in_specs=[VMEM_SPEC] * 4,
        out_specs=(VMEM_SPEC,) * 3,
        scratch_shapes=[pltpu.VMEM((cand_count, q_rows), F32)],
        cost_estimate=pl.CostEstimate(flops=80_000_000, bytes_accessed=3_000_000, transcendentals=10_000),
        name="count",
    )(cand_t, teacher.T, hot_ids.reshape(-1, LANES), sel)
    hot_block = pl.BlockSpec((groups, hot_each, feat), lambda i: (0, q_rows // hot_each, 0))

    def whole(shape):
        return pl.BlockSpec(shape, lambda i: (0,) * len(shape))

    slots = groups * capacity
    pay_rows = hot_each + 8
    loss, pay, weight = pl.pallas_call(
        functools.partial(score_kernel, scale, capacity),
        grid=(1,),
        out_shape=(
            jax.ShapeDtypeStruct((1, q_rows), F32),
            jax.ShapeDtypeStruct((groups, pay_rows, q_rows), BF16),
            jax.ShapeDtypeStruct((slots, q_rows), BF16),
        ),
        in_specs=[
            whole((q_rows, feat)),
            hot_block,
            whole((slots, feat)),
            whole((hot_total, q_rows)),
            whole((hot_total, q_rows)),
            whole((2 * COLD, q_rows)),
            whole((2 * COLD, q_rows)),
        ],
        out_specs=(whole((1, q_rows)), whole((groups, pay_rows, q_rows)), whole((slots, q_rows))),
        scratch_shapes=[pltpu.VMEM((hot_total, q_rows), F32), pltpu.VMEM((groups, q_rows), F32)],
        name="score",
    )(queries, gathered, found, count, target, place, misc)
    got = lax.all_to_all(pay, "corpus", split_axis=0, concat_axis=0, tiled=True)
    query_grad = pl.pallas_call(
        functools.partial(query_kernel, scale),
        grid=(1,),
        out_shape=jax.ShapeDtypeStruct((q_rows, feat), F32),
        in_specs=[hot_block, whole((groups, pay_rows, q_rows)), whole((slots, feat)), whole((slots, q_rows))],
        out_specs=whole((q_rows, feat)),
        cost_estimate=pl.CostEstimate(flops=700_000_000, bytes_accessed=7_000_000, transcendentals=0),
        name="query_grad",
    )(gathered, pay, found, weight)
    padded = asked[:, :PAD_SLOTS]
    valid = padded >= 0
    source = jnp.arange(groups, dtype=jnp.int32)[:, None] * (q_rows + hot_each)
    query_rows = gathered.reshape(-1, feat)[(source + jnp.maximum(padded, 0) // per_owner).reshape(-1)]
    local = jnp.where(valid, padded & (per_owner - 1), -1).reshape(1, -1)
    tail = jnp.full((LANES - 3 * hot_each,), -1, jnp.int32)
    local = jnp.concatenate([local, jnp.concatenate([own_hot, own_hot, own_hot, tail])[None, :]], axis=1)
    step = 8
    partial_grad = pl.pallas_call(
        functools.partial(slab_kernel, scale),
        grid=(groups // step,),
        out_shape=jax.ShapeDtypeStruct((per_owner, feat), BF16),
        in_specs=[
            pl.BlockSpec((step, pay_rows, q_rows), lambda i: (i, 0, 0)),
            pl.BlockSpec((step, q_rows, feat), lambda i: (i, 0, 0)),
            pl.BlockSpec((step * PAD_SLOTS, feat), lambda i: (i, 0)),
            whole((1, groups * PAD_SLOTS + LANES)),
        ],
        out_specs=whole((per_owner, feat)),
        scratch_shapes=[
            pltpu.VMEM((groups * PAD_SLOTS + LANES, feat), BF16),
            pltpu.VMEM((hot_each, feat), F32),
        ],
        name="slab_grad",
    )(got, gathered, query_rows, local)
    parts = lax.all_to_all(
        partial_grad.reshape(reps, per_owner // reps, feat), "rep", split_axis=0, concat_axis=0, tiled=True
    )
    slab_grad = jnp.sum(parts.astype(F32), axis=0)
    return (loss.reshape(q_rows), query_grad, slab_grad)


def solution(mesh):
    return jax.shard_map(
        shards,
        mesh=mesh,
        in_specs=(
            P(("corpus", "rep"), None),
            P(("corpus", "rep"), None),
            P("corpus", None),
            P(("corpus", "rep"), None),
            P(),
            P(),
        ),
        out_specs=(P(("corpus", "rep")), P(("corpus", "rep"), None), P(("corpus", "rep"), None)),
        check_vma=False,
    )
```

profile of v0, /device:TPU:6, one launch (start us, length us, event | category | flops | bytes accessed | tf_op | source)
XLA Modules:
  0.0 230.9 jit_solution(8744967553770863335)
XLA Ops:
  7.2 0.9 compare_select_fusion.3
  8.1 1.6 gather_fusion
  9.8 0.6 gather_fusion.1
  10.4 1.6 pad_maximum_fusion
  12.1 1.7 reshape.91.loc_ref
  13.8 6.2 %request.1 = (s32[64,128]{1,0:T(8,128)}, s32[16,128]{1,0:T(8,128)}, s32[64,128]{1,0:T(8,128)}) custom-call(s32[64,128]{1,0:T(8,128)} %bitcast.27, s32[1,2048]{1,0:T(1,128)} %bitcast.31, s32[256,256]{1,0:T(8,128)} %reshape.91.loc_ref), custom_call_target="tpu_custom_call" | custom-call | tf_op jit(solution)/shard_map/request/pallas_call | solution.py:274
  20.0 19.8 %all_to_all.20 = s32[64,1,128]{2,1,0:T(1,128)S(1)} all-to-all(s32[64,1,128]{2,1,0:T(1,128)} %bitcast.29), channel_id=1, replica_groups=mesh['corpus'=64,'rep'=4] {'corpus'}, dimensions={0} | all-to-all | bytes 65536 | tf_op jit(solution)/shard_map/all_to_all | solution.py:286
  39.9 5.7 %gather_fusion.2 = bf16[1536,768]{1,0:T(8,128)(2,1)} fusion(bf16[1024,768]{1,0:T(8,128)(2,1)S(1)} %copy-done, s32[2048]{0:T(1024)S(1)} %pad_clamp_fusion), kind=kCustom, calls=%fused_computation.2 | custom fusion | bytes 4724736 | tf_op jit(solution)/shard_map/gather | solution.py:289
  45.6 7.4 %all-to-all-start.1 = ((bf16[64,24,768]{2,1,0:T(8,128)(2,1)}), bf16[64,24,768]{2,1,0:T(8,128)(2,1)}, u32[]{:S(2)}, u32[]{:S(2)}) async-start(bf16[64,24,768]{2,1,0:T(8,128)(2,1)} %bitcast.23), calls=%async_computation.1 | async-start | bytes 4718592 | tf_op jit(solution)/shard_map/all_to_all | solution.py:290
  53.0 18.5 %count.1 = (f32[2048,128]{1,0:T(8,128)}, f32[2048,128]{1,0:T(8,128)}, f32[16,128]{1,0:T(8,128)}) custom-call(s32[64,128]{1,0:T(8,128)} %bitcast.28, f32[64,128]{1,0:T(8,128)} %bitcast.33, s32[16,128]{1,0:T(8,128)} %bitcast.32, s32[64,128]{1,0:T(8,128)} %get-tuple-element.17.sel_ref), custom_call_target="tpu_custom_call" | custom-call | flops 80000000 | bytes 3000000 | tf_op jit(solution)/shard_map/count/pallas_call | solution.py:292
  71.5 54.3 %all-to-all-done.1 = bf16[64,24,768]{2,1,0:T(8,128)(2,1)} async-done(((bf16[64,24,768]{2,1,0:T(8,128)(2,1)}), bf16[64,24,768]{2,1,0:T(8,128)(2,1)}, u32[]{:S(2)}, u32[]{:S(2)}) %all-to-all-start.1) | async-done | bytes 2359328 | tf_op jit(solution)/shard_map/all_to_all | solution.py:290
  125.8 20.1 %all-gather.3.cloned.1.call-done = bf16[10240,768]{1,0:T(8,128)(2,1)} async-done(((bf16[160,768]{1,0:T(8,128)(2,1)}), bf16[10240,768]{1,0:T(8,128)(2,1)}) %all-gather.3.cloned.1.call-update) | async-done | bytes 15728656 | tf_op jit(solution)/shard_map/all_gather | solution.py:273
  145.9 7.8 %score.1 = (f32[1,128]{1,0:T(1,128)}, bf16[64,40,128]{2,1,0:T(8,128)(2,1)}, bf16[1536,128]{1,0:T(8,128)(2,1)}) custom-call(bf16[128,768]{1,0:T(8,128)(2,1)} %q_ref.1, bf16[64,160,768]{2,1,0:T(8,128)(2,1)} %bitcast.20, bf16[1536,768]{1,0:T(8,128)(2,1)} %bitcast.9.found_ref, f32[2048,128]{1,0:T(8,128)} %get-tuple-element.18.count_ref, ...), custom_call_target="tpu_custom_call" | custom-call | tf_op jit(solution)/shard_map/score/pallas_call | solution.py:312
  153.8 8.1 %all-to-all-start.2 = ((bf16[64,40,128]{2,1,0:T(8,128)(2,1)}), bf16[64,40,128]{2,1,0:T(8,128)(2,1)S(1)}, u32[]{:S(2)}, u32[]{:S(2)}) async-start(bf16[64,40,128]{2,1,0:T(8,128)(2,1)} %get-tuple-element.23.pay_ref), calls=%async_computation.2 | async-start | bytes 1310720 | tf_op jit(solution)/shard_map/all_to_all | solution.py:333
  162.0 0.1 reshape.98
  162.3 0.6 pad_add_fusion.loc_ref
  162.9 17.6 %gather_fusion.3 = bf16[2048,768]{1,0:T(8,128)(2,1)} fusion(bf16[10240,768]{1,0:T(8,128)(2,1)} %all-gather.3.cloned.1.call-done, s32[2048]{0:T(1024)S(1)} %broadcast_clamp_fusion), kind=kCustom, calls=%fused_computation.3 | custom fusion | bytes 6299648 | tf_op jit(solution)/shard_map/gather | solution.py:346
  180.4 0.7 all-to-all-done.2.pay_ref
  181.2 0.8 copy-done.1
  182.0 14.9 %slab_grad.1 = bf16[1024,768]{1,0:T(8,128)(2,1)} custom-call(bf16[64,40,128]{2,1,0:T(8,128)(2,1)} %copy-done.1, bf16[64,160,768]{2,1,0:T(8,128)(2,1)} %bitcast.21, bf16[2048,768]{1,0:T(8,128)(2,1)} %gather_fusion.3, s32[1,2176]{1,0:T(1,128)} %pad_add_fusion.loc_ref), custom_call_target="tpu_custom_call" | custom-call | tf_op jit(solution)/shard_map/slab_grad/pallas_call | solution.py:351
  196.9 4.4 %all-to-all-start.3 = ((bf16[4,256,768]{2,1,0:T(8,128)(2,1)}), bf16[4,256,768]{2,1,0:T(8,128)(2,1)S(1)}, u32[]{:S(2)}, u32[]{:S(2)}) async-start(bf16[4,256,768]{2,1,0:T(8,128)(2,1)} %bitcast.24), calls=%async_computation.3 | async-start | bytes 3145728 | tf_op jit(solution)/shard_map/all_to_all | solution.py:368
  201.3 4.5 %query_grad.1 = f32[128,768]{1,0:T(8,128)} custom-call(bf16[64,160,768]{2,1,0:T(8,128)(2,1)} %bitcast.22, bf16[64,40,128]{2,1,0:T(8,128)(2,1)} %get-tuple-element.23.pay_ref, bf16[1536,768]{1,0:T(8,128)(2,1)} %bitcast.9.found_ref, bf16[1536,128]{1,0:T(8,128)(2,1)} %get-tuple-element.24.weight_ref), custom_call_target="tpu_custom_call" | custom-call | flops 700000000 | bytes 7000000 | tf_op jit(solution)/shard_map/query_grad/pallas_call | solution.py:334
  205.8 17.2 %all-to-all-done.3 = bf16[4,256,768]{2,1,0:T(8,128)(2,1)S(1)} async-done(((bf16[4,256,768]{2,1,0:T(8,128)(2,1)}), bf16[4,256,768]{2,1,0:T(8,128)(2,1)S(1)}, u32[]{:S(2)}, u32[]{:S(2)}) %all-to-all-start.3) | async-done | bytes 1572896 | tf_op jit(solution)/shard_map/all_to_all | solution.py:368
  223.0 1.1 convert_reduce_fusion
  (18 shorter events, 0.4 us)
Async XLA Ops:
  7.2 2.6 %copy-start = (bf16[1024,768]{1,0:T(8,128)(2,1)S(1)}, bf16[1024,768]{1,0:T(8,128)(2,1)}, u32[]{:S(2)}) copy-start(bf16[1024,768]{1,0:T(8,128)(2,1)} %param.8) | copy-start | bytes 4718596
  7.2 138.7 %all-gather.3.cloned.1.call-start = ((), (), s32[]{:S(2)}) async-start(), calls=%async_computation.4 | async-start | bytes 15974400 | tf_op jit(solution)/shard_map/all_gather | solution.py:273
  45.6 80.3 %all-to-all-start.1 = ((bf16[64,24,768]{2,1,0:T(8,128)(2,1)}), bf16[64,24,768]{2,1,0:T(8,128)(2,1)}, u32[]{:S(2)}, u32[]{:S(2)}) async-start(bf16[64,24,768]{2,1,0:T(8,128)(2,1)} %bitcast.23), calls=%async_computation.1 | async-start | bytes 4718592 | tf_op jit(solution)/shard_map/all_to_all | solution.py:290
  153.8 27.4 %all-to-all-start.2 = ((bf16[64,40,128]{2,1,0:T(8,128)(2,1)}), bf16[64,40,128]{2,1,0:T(8,128)(2,1)S(1)}, u32[]{:S(2)}, u32[]{:S(2)}) async-start(bf16[64,40,128]{2,1,0:T(8,128)(2,1)} %get-tuple-element.23.pay_ref), calls=%async_computation.2 | async-start | bytes 1310720 | tf_op jit(solution)/shard_map/all_to_all | solution.py:333
  181.2 0.8 copy-start.1
  196.9 26.1 %all-to-all-start.3 = ((bf16[4,256,768]{2,1,0:T(8,128)(2,1)}), bf16[4,256,768]{2,1,0:T(8,128)(2,1)S(1)}, u32[]{:S(2)}, u32[]{:S(2)}) async-start(bf16[4,256,768]{2,1,0:T(8,128)(2,1)} %bitcast.24), calls=%async_computation.3 | async-start | bytes 3145728 | tf_op jit(solution)/shard_map/all_to_all | solution.py:368
Sparse Core Ops, SparseCore 0:
  12.2 133.6 all-gather.2
where the time goes:
time: 232 us; the launch traced here: 231 us
  waiting for transfers between devices  92.4 us (40%)
  Pallas kernels  51.9 us (22%)
  local copies, waits for them, and re-layouts  28.3 us (12%)
  starting transfers between devices  20 us (9%)
  blocking collectives  19.8 us (9%)
  between operations  14.1 us (6%)
  other arithmetic  4.42 us (2%)
    all_to_all x1, waiting for transfers between devices, shards(): lax.all_to_all(found, 'corpus', split_axis=0, concat_axis=0, tiled=True)  54.3 us
    all_gather x1, waiting for transfers between devices, shards(): gathered = lax.all_gather(sent_rows, 'corpus', axis=0, tiled=False)  20.1 us
    all_to_all x1, blocking collectives, shards(): lax.all_to_all(req.reshape(groups, 1, LANES), 'corpus', split_axis=0, con...  19.8 us
    pallas_call x1, Pallas kernels, shards(): pl.pallas_call(count_kernel, out_shape=(jax.ShapeDtypeStruct((hot_total,...  18.5 us
    gather x1, local copies, waits for them, and re-layouts, shards(): gathered.reshape(-1, feat)  17.6 us
    all_to_all x1, waiting for transfers between devices, shards(): lax.all_to_all(partial_grad.reshape(reps, per_owner // reps, feat), 'rep'...  17.2 us
    pallas_call x1, Pallas kernels, shards(): pl.pallas_call(functools.partial(slab_kernel, scale), grid=(groups // ste...  14.9 us
    all_to_all x1, starting transfers between devices, shards(): got = lax.all_to_all(pay, 'corpus', split_axis=0, concat_axis=0, tiled=True)  8.12 us
  transfers between devices with their start and end apart: 4, of which 4 were waited for; matrix products, arithmetic and copies ran while one was open for 11% of the time, Pallas kernels for 13%

commit v1 on v0

--- a/solution.py
+++ b/solution.py
@@ -8,13 +8,16 @@
 from jax.experimental.pallas import tpu as pltpu
 from jax.sharding import PartitionSpec as P
 
+
 COLD = 8
 LANES = 128
+X_SIZE, Z_SIZE, CORES = 4, 8, 2
 RADIX = 256
 PAD_SLOTS = 32
 F32 = jnp.float32
 BF16 = jnp.bfloat16
 VMEM_SPEC = pl.BlockSpec(memory_space=pltpu.VMEM)
+SMEM_SPEC = pl.BlockSpec(memory_space=pltpu.SMEM)
 ROWS_DOT = (((1,), (1,)), ((), ()))
 
 
@@ -30,7 +33,7 @@
     return jnp.sum(jnp.where(mask, values, jnp.zeros_like(values)), axis=0, keepdims=True)
 
 
-def request_kernel(per_owner, capacity, groups, cand_t, hot_ref, loc_ref, req_ref, place_ref, sel_ref, hit_t):
+def request_kernel(per_owner, groups, cand_t, hot_ref, loc_ref, req_ref, place_ref, sel_ref, hit_t):
     cand_count, q_rows = cand_t.shape
     hot_total = hot_ref.shape[1]
     high_rows = loc_ref.shape[0]
@@ -102,6 +105,28 @@
     place_ref[...] = jnp.concatenate(owners + ranks, axis=0)
 
 
+def owner_of(spot_ref, piece, z):
+    x = (spot_ref[0] - piece % X_SIZE) & (X_SIZE - 1)
+    core = spot_ref[1] ^ (piece // X_SIZE)
+    return (x * Z_SIZE + z) * CORES + core
+
+
+def fetch_kernel(capacity, asked_ref, slab_ref, out_ref):
+    groups = asked_ref.shape[0]
+    per_owner = slab_ref.shape[0]
+    asked = jnp.maximum(asked_ref[...], 0)
+    cols = jnp.transpose((asked & (per_owner - 1)).astype(F32))
+    step = 16
+    lane = iota((capacity, per_owner), 1).astype(F32)
+    for j in range(groups // step):
+        picks = [
+            one_hot(lane == jnp.broadcast_to(cols[0:capacity, n : n + 1], (capacity, per_owner)), F32)
+            for n in range(j * step, (j + 1) * step)
+        ]
+        got = jnp.dot(jnp.concatenate(picks, axis=0).astype(BF16), slab_ref[...], preferred_element_type=F32)
+        out_ref[j * step * capacity : (j + 1) * step * capacity, :] = got.astype(BF16)
+
+
 def count_kernel(cand_t, teacher_ref, hot_ref, sel_ref, count_ref, target_ref, misc_ref, soft_t):
     cand_count, q_rows = cand_t.shape
     teacher = teacher_ref[...]
@@ -130,8 +155,14 @@
         target_ref[a * LANES : (a + 1) * LANES, :] = total
 
 
-def score_kernel(scale, capacity, q_ref, hot_ref, found_ref, count_ref, target_ref, place_ref, misc_ref, loss_ref, pay_ref, weight_ref, hot_scr, slot_scr):
-    groups, hot_each, feat = hot_ref.shape
+def score_kernel(scale, capacity, spot_ref, q_ref, *refs):
+    hot_refs, refs = refs[: X_SIZE * CORES], refs[X_SIZE * CORES :]
+    score_body(scale, capacity, spot_ref, q_ref, hot_refs, *refs)
+
+
+def score_body(scale, capacity, spot_ref, q_ref, hot_refs, found_ref, count_ref, target_ref, place_ref, misc_ref, loss_ref, pay_ref, weight_ref, hot_scr, slot_scr):
+    groups = pay_ref.shape[0]
+    hot_each = hot_scr.shape[0] // groups
     slots = found_ref.shape[0]
     q_rows = q_ref.shape[0]
     q = q_ref[...]
@@ -139,10 +170,11 @@
     place = place_ref[...]
     dests = [place[r : r + 1] * capacity + place[COLD + r : COLD + r + 1] for r in range(COLD)]
     top = jnp.full((1, q_rows), -jnp.inf, F32)
-    for j in range(groups // step):
-        rows = hot_ref[j * step : (j + 1) * step].reshape(step * hot_each, feat)
-        got = scale * lax.dot_general(rows, q, ROWS_DOT, preferred_element_type=F32)
-        hot_scr[j * step * hot_each : (j + 1) * step * hot_each, :] = got
+    for piece, hot_ref in enumerate(hot_refs):
+        got = scale * lax.dot_general(hot_ref[...], q, ROWS_DOT, preferred_element_type=F32)
+        for z in range(Z_SIZE):
+            start = pl.multiple_of(owner_of(spot_ref, piece, z) * hot_each, hot_each)
+            hot_scr[pl.ds(start, hot_each), :] = got[z * hot_each : (z + 1) * hot_each]
         top = jnp.maximum(top, jnp.max(got, axis=0, keepdims=True))
     colds = [jnp.zeros((1, q_rows), F32) for _ in range(COLD)]
     chunk = 256
@@ -190,15 +222,16 @@
         weight_ref[j * chunk : (j + 1) * chunk, :] = made.astype(BF16)
 
 
-def query_kernel(scale, hot_ref, pay_ref, found_ref, weight_ref, out_ref):
-    groups, hot_each, feat = hot_ref.shape
+def query_kernel(scale, spot_ref, *refs):
+    hot_refs = refs[: X_SIZE * CORES]
+    pay_ref, found_ref, weight_ref, out_ref = refs[X_SIZE * CORES :]
+    hot_each = hot_refs[0].shape[0] // Z_SIZE
     acc = jnp.zeros(out_ref.shape, F32)
-    step = 8
     first = (((0,), (0,)), ((), ()))
-    for j in range(groups // step):
-        rows = hot_ref[j * step : (j + 1) * step].reshape(step * hot_each, feat)
-        coef = jnp.concatenate([pay_ref[j * step + n, 0:hot_each, :] for n in range(step)], axis=0)
-        acc = acc + lax.dot_general(coef, rows, first, preferred_element_type=F32)
+    for piece, hot_ref in enumerate(hot_refs):
+        owners = [owner_of(spot_ref, piece, z) for z in range(Z_SIZE)]
+        coef = jnp.concatenate([pay_ref[o, 0:hot_each, :] for o in owners], axis=0)
+        acc = acc + lax.dot_general(coef, hot_ref[...], first, preferred_element_type=F32)
     chunk = 256
     for j in range(found_ref.shape[0] // chunk):
         part = slice(j * chunk, (j + 1) * chunk)
@@ -243,7 +276,7 @@
         base = terms.shape[0] - LANES
         terms[base:, :] = jnp.concatenate([high, mid, low, jnp.zeros_like(low)], axis=0)
         loc = loc_ref[...]
-        tile = 128
+        tile = 512
 
         def land(j, carry):
             start = pl.multiple_of(j * tile, tile)
@@ -253,6 +286,21 @@
             return carry
 
         lax.fori_loop(0, out_ref.shape[0] // tile, land, 0)
+
+
+def gather_hot(rows):
+    def member(x, z, core):
+        return (x * Z_SIZE + z) * CORES + core
+
+    chips = [(x, z, c) for x in range(X_SIZE) for z in range(Z_SIZE) for c in range(CORES)]
+    along_z = [[member(x, z, c) for z in range(Z_SIZE)] for x in range(X_SIZE) for c in range(CORES)]
+    rows = lax.all_gather(rows, "corpus", axis=0, tiled=True, axis_index_groups=along_z)
+    pieces = [rows]
+    for d in range(1, X_SIZE):
+        moves = [(member(x, z, c), member((x + d) % X_SIZE, z, c)) for x, z, c in chips]
+        pieces.append(lax.ppermute(rows, "corpus", moves))
+    swap = [(member(x, z, c), member(x, z, CORES - 1 - c)) for x, z, c in chips]
+    return pieces + [lax.ppermute(p, "corpus", swap) for p in pieces]
 
 
 def shards(queries, teacher, slab, candidates, hot_ids, location):
@@ -266,13 +314,10 @@
     cand_count = candidates.shape[1]
     capacity = q_rows * COLD * 3 // (2 * groups)
     scale = 2.0 / math.sqrt(feat)
-    mine = lax.dynamic_slice_in_dim(hot_ids, corpus_idx * hot_each, hot_each)
-    own_hot = location[mine] - corpus_idx * per_owner
-    sent_rows = jnp.concatenate([queries, slab[own_hot]], axis=0)
-    cand_t, sent_rows = lax.optimization_barrier((candidates.T, sent_rows))
-    gathered = lax.all_gather(sent_rows, "corpus", axis=0, tiled=False)
+    gathered = lax.all_gather(queries, "corpus", axis=0, tiled=False)
+    cand_t = candidates.T
     req, place, sel = pl.pallas_call(
-        functools.partial(request_kernel, per_owner, capacity, groups),
+        functools.partial(request_kernel, per_owner, groups),
         out_shape=(
             jax.ShapeDtypeStruct((groups, LANES), jnp.int32),
             jax.ShapeDtypeStruct((2 * COLD, q_rows), jnp.int32),
@@ -285,10 +330,20 @@
     )(cand_t, hot_ids.reshape(1, hot_total), location.reshape(-1, RADIX))
     asked = lax.all_to_all(req.reshape(groups, 1, LANES), "corpus", split_axis=0, concat_axis=0, tiled=True)
     asked = asked.reshape(groups, LANES)
-    asked_slots = jnp.maximum(asked[:, :capacity], 0)
-    found = slab[asked_slots & (per_owner - 1)]
-    found = lax.all_to_all(found, "corpus", split_axis=0, concat_axis=0, tiled=True)
+    wanted = pl.pallas_call(
+        functools.partial(fetch_kernel, capacity),
+        out_shape=jax.ShapeDtypeStruct((groups * capacity, feat), BF16),
+        in_specs=[VMEM_SPEC] * 2,
+        out_specs=VMEM_SPEC,
+        name="fetch",
+    )(asked, slab)
+    mine = lax.dynamic_slice_in_dim(hot_ids, corpus_idx * hot_each, hot_each)
+    own_hot = location[mine] - corpus_idx * per_owner
+    own_rows, wanted = lax.optimization_barrier((slab[own_hot], wanted))
+    found = lax.all_to_all(wanted.reshape(groups, capacity, feat), "corpus", split_axis=0, concat_axis=0, tiled=True)
     found = found.reshape(groups * capacity, feat)
+    hot_rows = gather_hot(own_rows)
+    spot = jnp.stack([corpus_idx // (Z_SIZE * CORES), corpus_idx % CORES]).astype(jnp.int32)
     count, target, misc = pl.pallas_call(
         count_kernel,
         out_shape=(
@@ -302,7 +357,6 @@
         cost_estimate=pl.CostEstimate(flops=80_000_000, bytes_accessed=3_000_000, transcendentals=10_000),
         name="count",
     )(cand_t, teacher.T, hot_ids.reshape(-1, LANES), sel)
-    hot_block = pl.BlockSpec((groups, hot_each, feat), lambda i: (0, q_rows // hot_each, 0))
 
     def whole(shape):
         return pl.BlockSpec(shape, lambda i: (0,) * len(shape))
@@ -318,8 +372,9 @@
             jax.ShapeDtypeStruct((slots, q_rows), BF16),
         ),
         in_specs=[
+            SMEM_SPEC,
             whole((q_rows, feat)),
-            hot_block,
+            *[whole(h.shape) for h in hot_rows],
             whole((slots, feat)),
             whole((hot_total, q_rows)),
             whole((hot_total, q_rows)),
@@ -329,20 +384,20 @@
         out_specs=(whole((1, q_rows)), whole((groups, pay_rows, q_rows)), whole((slots, q_rows))),
         scratch_shapes=[pltpu.VMEM((hot_total, q_rows), F32), pltpu.VMEM((groups, q_rows), F32)],
         name="score",
-    )(queries, gathered, found, count, target, place, misc)
+    )(spot, queries, *hot_rows, found, count, target, place, misc)
     got = lax.all_to_all(pay, "corpus", split_axis=0, concat_axis=0, tiled=True)
     query_grad = pl.pallas_call(
         functools.partial(query_kernel, scale),
         grid=(1,),
         out_shape=jax.ShapeDtypeStruct((q_rows, feat), F32),
-        in_specs=[hot_block, whole((groups, pay_rows, q_rows)), whole((slots, feat)), whole((slots, q_rows))],
+        in_specs=[SMEM_SPEC, *[whole(h.shape) for h in hot_rows], whole((groups, pay_rows, q_rows)), whole((slots, feat)), whole((slots, q_rows))],
         out_specs=whole((q_rows, feat)),
         cost_estimate=pl.CostEstimate(flops=700_000_000, bytes_accessed=7_000_000, transcendentals=0),
         name="query_grad",
-    )(gathered, pay, found, weight)
+    )(spot, *hot_rows, pay, found, weight)
     padded = asked[:, :PAD_SLOTS]
     valid = padded >= 0
-    source = jnp.arange(groups, dtype=jnp.int32)[:, None] * (q_rows + hot_each)
+    source = jnp.arange(groups, dtype=jnp.int32)[:, None] * q_rows
     query_rows = gathered.reshape(-1, feat)[(source + jnp.maximum(padded, 0) // per_owner).reshape(-1)]
     local = jnp.where(valid, padded & (per_owner - 1), -1).reshape(1, -1)
     tail = jnp.full((LANES - 3 * hot_each,), -1, jnp.int32)

time: 232 us -> 266 us (1.15)
  blocking collectives: 19.8 us -> 92.6 us
  waiting for transfers between devices: 92.4 us -> 36.2 us
  starting transfers between devices: 20 us -> 37.2 us
  Pallas kernels: 51.9 us -> 56.2 us
  local copies, waits for them, and re-layouts: 28.3 us -> 25 us
    all_gather x0 -> x1, blocking collectives: none -> 92.6 us  [gather_hot(): lax.all_gather(rows, 'corpus', axis=0, tiled=True, axis_index_groups=alon...]
    all_to_all x1 -> x2, waiting for transfers between devices: 54.3 us -> 2.82 us  [the longest x1 2.82 us: shards(): lax.all_to_all(req.reshape(groups, 1, LANES), 'corpus', split_axis=0, con...]
    all_gather x1, waiting for transfers between devices: 20.1 us -> 0.01 us  [shards(): gathered = lax.all_gather(queries, 'corpus', axis=0, tiled=False)]
    all_to_all x1 -> x0, blocking collectives: 19.8 us -> none  [shards(): lax.all_to_all(req.reshape(groups, 1, LANES), 'corpus', split_axis=0, con...]
    ppermute x0 -> x7, waiting for transfers between devices: none -> 14.3 us  [the longest x3 14.3 us: gather_hot(): pieces.append(lax.ppermute(rows, 'corpus', moves))]
    all_to_all x1 -> x2, starting transfers between devices: 7.45 us -> 19.7 us  [the longest x1 12.2 us: shards(): lax.all_to_all(req.reshape(groups, 1, LANES), 'corpus', split_axis=0, con...]
    pallas_call x1 -> x2, Pallas kernels: 6.22 us -> 11.8 us  [the longest x1 6.23 us: shards(): pl.pallas_call(functools.partial(request_kernel, per_owner, groups), out_...]
    gather x2 -> x1, local copies, waits for them, and re-layouts: 6.28 us -> 2.27 us  [shards(): own_rows, wanted = lax.optimization_barrier((slab[own_hot], wanted))]
  transfers between devices with their start and end apart: 4 -> 12, of which waited for: 4 -> 6; matrix products, arithmetic and copies ran while one was open for 11% -> 9% of each run, Pallas kernels for 13% -> 16%
where the time goes in v1:
time: 266 us; the launch traced here: 265 us
  blocking collectives  92.6 us (35%)
  Pallas kernels  56.2 us (21%)
  starting transfers between devices  37.2 us (14%)
  waiting for transfers between devices  36.2 us (14%)
  local copies, waits for them, and re-layouts  25 us (9%)
  between operations  14.2 us (5%)
  other arithmetic  4.08 us (2%)
    all_gather x1, blocking collectives, gather_hot(): lax.all_gather(rows, 'corpus', axis=0, tiled=True, axis_index_groups=alon...  92.6 us
    pallas_call x1, Pallas kernels, shards(): pl.pallas_call(count_kernel, out_shape=(jax.ShapeDtypeStruct((hot_total,...  18.4 us
    all_to_all x1, waiting for transfers between devices, shards(): lax.all_to_all(partial_grad.reshape(reps, per_owner // reps, feat), 'rep'...  17.1 us
    gather x1, local copies, waits for them, and re-layouts, shards(): gathered.reshape(-1, feat)  16.4 us
    ppermute x3, waiting for transfers between devices, gather_hot(): pieces.append(lax.ppermute(rows, 'corpus', moves))  14.3 us
    pallas_call x1, Pallas kernels, shards(): pl.pallas_call(functools.partial(slab_kernel, scale), grid=(groups // ste...  14 us
    all_to_all x1, starting transfers between devices, shards(): lax.all_to_all(req.reshape(groups, 1, LANES), 'corpus', split_axis=0, con...  12.2 us
    all_to_all x1, starting transfers between devices, shards(): got = lax.all_to_all(pay, 'corpus', split_axis=0, concat_axis=0, tiled=True)  9.78 us
  transfers between devices with their start and end apart: 12, of which 6 were waited for; matrix products, arithmetic and copies ran while one was open for 9% of the time, Pallas kernels for 16%

profile of v1, /device:TPU:6, one launch (start us, length us, event | category | flops | bytes accessed | tf_op | source)
XLA Modules:
  0.0 265.3 jit_solution(2645852066103551046)
XLA Ops:
  7.9 1.7 reshape.94.loc_ref
  9.6 6.2 %request.1 = (s32[64,128]{1,0:T(8,128)}, s32[16,128]{1,0:T(8,128)}, s32[64,128]{1,0:T(8,128)}) custom-call(s32[64,128]{1,0:T(8,128)} %bitcast.29, s32[1,2048]{1,0:T(1,128)} %bitcast.33, s32[256,256]{1,0:T(8,128)} %reshape.94.loc_ref), custom_call_target="tpu_custom_call" | custom-call | tf_op jit(solution)/shard_map/request/pallas_call | solution.py:319
  15.9 12.2 %all-to-all-start = ((s32[64,1,128]{2,1,0:T(1,128)}), s32[64,1,128]{2,1,0:T(1,128)S(1)}, u32[]{:S(2)}, u32[]{:S(2)}) async-start(s32[64,1,128]{2,1,0:T(1,128)} %bitcast.31), calls=%async_computation | async-start | bytes 65536 | tf_op jit(solution)/shard_map/all_to_all | solution.py:331
  28.8 1.6 gather_fusion
  30.5 2.3 gather_fusion.1
  32.8 2.8 %all-to-all-done = s32[64,1,128]{2,1,0:T(1,128)S(1)} async-done(((s32[64,1,128]{2,1,0:T(1,128)}), s32[64,1,128]{2,1,0:T(1,128)S(1)}, u32[]{:S(2)}, u32[]{:S(2)}) %all-to-all-start) | async-done | bytes 32800 | tf_op jit(solution)/shard_map/all_to_all | solution.py:331
  36.2 5.5 %fetch.1 = bf16[1536,768]{1,0:T(8,128)(2,1)} custom-call(s32[64,128]{1,0:T(8,128)} %bitcast.27, bf16[1024,768]{1,0:T(8,128)(2,1)} %slab_ref.1), custom_call_target="tpu_custom_call" | custom-call | tf_op jit(solution)/shard_map/fetch/pallas_call | solution.py:333
  41.7 7.5 %all-to-all-start.1 = ((bf16[64,24,768]{2,1,0:T(8,128)(2,1)}), bf16[64,24,768]{2,1,0:T(8,128)(2,1)S(1)}, u32[]{:S(2)}, u32[]{:S(2)}) async-start(bf16[64,24,768]{2,1,0:T(8,128)(2,1)} %bitcast.25), calls=%async_computation.1 | async-start | bytes 4718592 | tf_op jit(solution)/shard_map/all_to_all | solution.py:343
  49.3 92.6 %all_gather.9.refs_0_ = bf16[256,768]{1,0:T(8,128)(2,1)S(1)} all-gather(bf16[32,768]{1,0:T(8,128)(2,1)S(1)} %gather_fusion.1), channel_id=1, replica_groups={{0,8,16,24,32,40,48,56},{4,12,20,28,36,44,52,60},{64,72,80,88,96,104,11..., dimensions={0}, use_global_device_ids=true | all-gather | bytes 442368 | tf_op jit(solution)/shard_map/all_gather | solution.py:297
  142.8 2.1 collective-permute-start.1
  145.0 8.0 %collective-permute-done.refs_1_ = bf16[256,768]{1,0:T(8,128)(2,1)S(1)} collective-permute-done((bf16[256,768]{1,0:T(8,128)(2,1)S(1)}, bf16[256,768]{1,0:T(8,128)(2,1)S(1)}, u32[]{:S(2)}, u32[]{:S(2)}) %collective-permute-start) | collective-permute-done | bytes 393248 | tf_op jit(solution)/shard_map/ppermute | solution.py:301
  153.0 2.1 collective-permute-done.1.refs_2_
  155.2 4.2 %collective-permute-done.2.refs_3_ = bf16[256,768]{1,0:T(8,128)(2,1)} collective-permute-done((bf16[256,768]{1,0:T(8,128)(2,1)S(1)}, bf16[256,768]{1,0:T(8,128)(2,1)}, u32[]{:S(2)}, u32[]{:S(2)}) %collective-permute-start.2) | collective-permute-done | bytes 393248 | tf_op jit(solution)/shard_map/ppermute | solution.py:301
  159.3 18.4 %count.1 = (f32[2048,128]{1,0:T(8,128)}, f32[2048,128]{1,0:T(8,128)}, f32[16,128]{1,0:T(8,128)}) custom-call(s32[64,128]{1,0:T(8,128)} %bitcast.30, f32[64,128]{1,0:T(8,128)} %bitcast.35, s32[16,128]{1,0:T(8,128)} %bitcast.34, s32[64,128]{1,0:T(8,128)} %get-tuple-element.17.sel_ref), custom_call_target="tpu_custom_call" | custom-call | flops 80000000 | bytes 3000000 | tf_op jit(solution)/shard_map/count/pallas_call | solution.py:347
  178.5 1.4 copy-done
  179.9 7.5 %score.1 = (f32[1,128]{1,0:T(1,128)}, bf16[64,40,128]{2,1,0:T(8,128)(2,1)}, bf16[1536,128]{1,0:T(8,128)(2,1)}) custom-call(s32[2]{0:T(128)} %pad_add_fusion.1.spot_ref, bf16[128,768]{1,0:T(8,128)(2,1)} %q_ref.1, bf16[256,768]{1,0:T(8,128)(2,1)} %copy-done.1, bf16[256,768]{1,0:T(8,128)(2,1)} %copy-done.3, bf16[256,768]{1,0:T(8,128)(2,1)} %copy-done.4, ...), custom_call_target="tpu_custom_call" | custom-call | tf_op jit(solution)/shard_map/score/pallas_call | solution.py:366
  187.3 9.8 %all-to-all-start.2 = ((bf16[64,40,128]{2,1,0:T(8,128)(2,1)}), bf16[64,40,128]{2,1,0:T(8,128)(2,1)S(1)}, u32[]{:S(2)}, u32[]{:S(2)}) async-start(bf16[64,40,128]{2,1,0:T(8,128)(2,1)} %get-tuple-element.23.refs_8_), calls=%async_computation.2 | async-start | bytes 1310720 | tf_op jit(solution)/shard_map/all_to_all | solution.py:388
  198.9 16.4 %gather_fusion.2 = bf16[2048,768]{1,0:T(8,128)(2,1)} fusion(bf16[8192,768]{1,0:T(8,128)(2,1)} %all-gather.3.cloned.1.call-done, s32[2048]{0:T(1024)S(1)} %broadcast_clamp_fusion), kind=kCustom, calls=%fused_computation.2 | custom fusion | bytes 6299648 | tf_op jit(solution)/shard_map/gather | solution.py:401
  215.2 1.2 all-to-all-done.2.pay_ref
  217.3 14.0 %slab_grad.1 = bf16[1024,768]{1,0:T(8,128)(2,1)} custom-call(bf16[64,40,128]{2,1,0:T(8,128)(2,1)} %copy-done.2, bf16[64,128,768]{2,1,0:T(8,128)(2,1)} %bitcast.22, bf16[2048,768]{1,0:T(8,128)(2,1)} %gather_fusion.2, s32[1,2176]{1,0:T(1,128)} %pad_add_fusion.loc_ref), custom_call_target="tpu_custom_call" | custom-call | tf_op jit(solution)/shard_map/slab_grad/pallas_call | solution.py:406
  231.2 4.5 %all-to-all-start.3 = ((bf16[4,256,768]{2,1,0:T(8,128)(2,1)}), bf16[4,256,768]{2,1,0:T(8,128)(2,1)S(1)}, u32[]{:S(2)}, u32[]{:S(2)}) async-start(bf16[4,256,768]{2,1,0:T(8,128)(2,1)} %bitcast.26), calls=%async_computation.3 | async-start | bytes 3145728 | tf_op jit(solution)/shard_map/all_to_all | solution.py:423
  235.7 4.5 %query_grad.1 = f32[128,768]{1,0:T(8,128)} custom-call(s32[2]{0:T(128)} %pad_add_fusion.1.spot_ref, bf16[256,768]{1,0:T(8,128)(2,1)} %copy-done.1, bf16[256,768]{1,0:T(8,128)(2,1)} %copy-done.3, bf16[256,768]{1,0:T(8,128)(2,1)} %copy-done.4, bf16[256,768]{1,0:T(8,128)(2,1)} %collective-permute-done.2.refs_3_, ...), custom_call_target="tpu_custom_call" | custom-call | flops 700000000 | bytes 7000000 | tf_op jit(solution)/shard_map/query_grad/pallas_call | solution.py:389
  240.3 17.1 %all-to-all-done.3 = bf16[4,256,768]{2,1,0:T(8,128)(2,1)S(1)} async-done(((bf16[4,256,768]{2,1,0:T(8,128)(2,1)}), bf16[4,256,768]{2,1,0:T(8,128)(2,1)S(1)}, u32[]{:S(2)}, u32[]{:S(2)}) %all-to-all-start.3) | async-done | bytes 1572896 | tf_op jit(solution)/shard_map/all_to_all | solution.py:423
  257.4 1.1 convert_reduce_fusion
  (39 shorter events, 6.4 us)
Async XLA Ops:
  7.2 191.7 %all-gather.3.cloned.1.call-start = ((), (), s32[]{:S(2)}) async-start(), calls=%async_computation.4 | async-start | bytes 12779520 | tf_op jit(solution)/shard_map/all_gather | solution.py:317
  15.9 19.7 %all-to-all-start = ((s32[64,1,128]{2,1,0:T(1,128)}), s32[64,1,128]{2,1,0:T(1,128)S(1)}, u32[]{:S(2)}, u32[]{:S(2)}) async-start(s32[64,1,128]{2,1,0:T(1,128)} %bitcast.31), calls=%async_computation | async-start | bytes 65536 | tf_op jit(solution)/shard_map/all_to_all | solution.py:331
  35.6 0.6 copy-start.5
  41.7 136.7 %all-to-all-start.1 = ((bf16[64,24,768]{2,1,0:T(8,128)(2,1)}), bf16[64,24,768]{2,1,0:T(8,128)(2,1)S(1)}, u32[]{:S(2)}, u32[]{:S(2)}) async-start(bf16[64,24,768]{2,1,0:T(8,128)(2,1)} %bitcast.25), calls=%async_computation.1 | async-start | bytes 4718592 | tf_op jit(solution)/shard_map/all_to_all | solution.py:343
  141.8 36.6 %copy-start.1 = (bf16[256,768]{1,0:T(8,128)(2,1)}, bf16[256,768]{1,0:T(8,128)(2,1)S(1)}, u32[]{:S(2)}) copy-start(bf16[256,768]{1,0:T(8,128)(2,1)S(1)} %all_gather.9.refs_0_) | copy-start | bytes 1179652
  141.9 11.2 %collective-permute-start = (bf16[256,768]{1,0:T(8,128)(2,1)S(1)}, bf16[256,768]{1,0:T(8,128)(2,1)S(1)}, u32[]{:S(2)}, u32[]{:S(2)}) collective-permute-start(bf16[256,768]{1,0:T(8,128)(2,1)S(1)} %all_gather.9.refs_0_), channel_id=1, source_target_pairs={{0,64},{4,68},{8,72},{12,76},{16,80},{20,84},{24,88},{28,92},{32,9... | collective-permute-start | bytes 1179656 | tf_op jit(solution)/shard_map/ppermute | solution.py:301
  142.8 12.3 %collective-permute-start.1 = (bf16[256,768]{1,0:T(8,128)(2,1)S(1)}, bf16[256,768]{1,0:T(8,128)(2,1)S(1)}, u32[]{:S(2)}, u32[]{:S(2)}) collective-permute-start(bf16[256,768]{1,0:T(8,128)(2,1)S(1)} %all_gather.9.refs_0_), channel_id=1, source_target_pairs={{0,128},{4,132},{8,136},{12,140},{16,144},{20,148},{24,152},{28,15... | collective-permute-start | bytes 1179656 | tf_op jit(solution)/shard_map/ppermute | solution.py:301
  145.0 14.4 %collective-permute-start.2 = (bf16[256,768]{1,0:T(8,128)(2,1)S(1)}, bf16[256,768]{1,0:T(8,128)(2,1)}, u32[]{:S(2)}, u32[]{:S(2)}) collective-permute-start(bf16[256,768]{1,0:T(8,128)(2,1)S(1)} %all_gather.9.refs_0_), channel_id=1, source_target_pairs={{0,192},{4,196},{8,200},{12,204},{16,208},{20,212},{24,216},{28,22... | collective-permute-start | bytes 1179656 | tf_op jit(solution)/shard_map/ppermute | solution.py:301
  145.0 33.4 %collective-permute-start.3 = (bf16[256,768]{1,0:T(8,128)(2,1)S(1)}, bf16[256,768]{1,0:T(8,128)(2,1)}, u32[]{:S(2)}, u32[]{:S(2)}) collective-permute-start(bf16[256,768]{1,0:T(8,128)(2,1)S(1)} %all_gather.9.refs_0_), channel_id=1, source_target_pairs={{0,4},{4,0},{8,12},{12,8},{16,20},{20,16},{24,28},{28,24},{32,36},... | collective-permute-start | bytes 1179656 | tf_op jit(solution)/shard_map/ppermute | solution.py:303
  153.0 25.5 %copy-start.3 = (bf16[256,768]{1,0:T(8,128)(2,1)}, bf16[256,768]{1,0:T(8,128)(2,1)S(1)}, u32[]{:S(2)}) copy-start(bf16[256,768]{1,0:T(8,128)(2,1)S(1)} %collective-permute-done.refs_1_) | copy-start | bytes 1179652
  153.0 25.4 %collective-permute-start.4 = (bf16[256,768]{1,0:T(8,128)(2,1)S(1)}, bf16[256,768]{1,0:T(8,128)(2,1)}, u32[]{:S(2)}, u32[]{:S(2)}) collective-permute-start(bf16[256,768]{1,0:T(8,128)(2,1)S(1)} %collective-permute-done.refs_1_), channel_id=1, source_target_pairs={{0,4},{4,0},{8,12},{12,8},{16,20},{20,16},{24,28},{28,24},{32,36},... | collective-permute-start | bytes 1179656 | tf_op jit(solution)/shard_map/ppermute | solution.py:303
  155.2 23.4 %copy-start.4 = (bf16[256,768]{1,0:T(8,128)(2,1)}, bf16[256,768]{1,0:T(8,128)(2,1)S(1)}, u32[]{:S(2)}) copy-start(bf16[256,768]{1,0:T(8,128)(2,1)S(1)} %collective-permute-done.1.refs_2_) | copy-start | bytes 1179652
  155.2 23.3 %collective-permute-start.5 = (bf16[256,768]{1,0:T(8,128)(2,1)S(1)}, bf16[256,768]{1,0:T(8,128)(2,1)}, u32[]{:S(2)}, u32[]{:S(2)}) collective-permute-start(bf16[256,768]{1,0:T(8,128)(2,1)S(1)} %collective-permute-done.1.refs_2_), channel_id=1, source_target_pairs={{0,4},{4,0},{8,12},{12,8},{16,20},{20,16},{24,28},{28,24},{32,36},... | collective-permute-start | bytes 1179656 | tf_op jit(solution)/shard_map/ppermute | solution.py:303
  159.3 19.1 %collective-permute-start.6 = (bf16[256,768]{1,0:T(8,128)(2,1)}, bf16[256,768]{1,0:T(8,128)(2,1)}, u32[]{:S(2)}, u32[]{:S(2)}) collective-permute-start(bf16[256,768]{1,0:T(8,128)(2,1)} %collective-permute-done.2.refs_3_), channel_id=1, source_target_pairs={{0,4},{4,0},{8,12},{12,8},{16,20},{20,16},{24,28},{28,24},{32,36},... | collective-permute-start | bytes 1179656 | tf_op jit(solution)/shard_map/ppermute | solution.py:303
  178.5 1.4 copy-start
  187.3 29.1 %all-to-all-start.2 = ((bf16[64,40,128]{2,1,0:T(8,128)(2,1)}), bf16[64,40,128]{2,1,0:T(8,128)(2,1)S(1)}, u32[]{:S(2)}, u32[]{:S(2)}) async-start(bf16[64,40,128]{2,1,0:T(8,128)(2,1)} %get-tuple-element.23.refs_8_), calls=%async_computation.2 | async-start | bytes 1310720 | tf_op jit(solution)/shard_map/all_to_all | solution.py:388
  216.4 0.8 copy-start.2
  231.2 26.2 %all-to-all-start.3 = ((bf16[4,256,768]{2,1,0:T(8,128)(2,1)}), bf16[4,256,768]{2,1,0:T(8,128)(2,1)S(1)}, u32[]{:S(2)}, u32[]{:S(2)}) async-start(bf16[4,256,768]{2,1,0:T(8,128)(2,1)} %bitcast.26), calls=%async_computation.3 | async-start | bytes 3145728 | tf_op jit(solution)/shard_map/all_to_all | solution.py:423
Sparse Core Ops, SparseCore 0:
  10.7 127.0 all-gather.2

commit v2 on v0

v2 whole, which is shorter than its diff:
```python
import functools
import math

import jax
import jax.numpy as jnp
from jax import lax
from jax.experimental import pallas as pl
from jax.experimental.pallas import tpu as pltpu
from jax.sharding import PartitionSpec as P

COLD = 8
LANES = 128
RADIX = 256
F32 = jnp.float32
BF16 = jnp.bfloat16
VMEM_SPEC = pl.BlockSpec(memory_space=pltpu.VMEM)
SMEM_SPEC = pl.BlockSpec(memory_space=pltpu.SMEM)
ROWS_DOT = (((1,), (1,)), ((), ()))


def iota(shape, axis):
    return lax.broadcasted_iota(jnp.int32, shape, axis)


def one_hot(mask, dtype=BF16):
    return jnp.where(mask, 1.0, 0.0).astype(dtype)


def pick_rows(mask, values):
    return jnp.sum(jnp.where(mask, values, jnp.zeros_like(values)), axis=0, keepdims=True)


def request_kernel(per_owner, capacity, groups, cand_t, hot_ref, loc_ref, req_ref, place_ref, sel_ref, hit_t):
    cand_count, q_rows = cand_t.shape
    hot_total = hot_ref.shape[1]
    high_rows = loc_ref.shape[0] // 2
    hot = hot_ref[...]
    low_hot = one_hot(iota((RADIX, hot_total), 0) == (hot & (RADIX - 1)))
    high_hot = one_hot(iota((high_rows, hot_total), 0) == (hot // RADIX))
    marks = lax.dot_general(low_hot, high_hot, ROWS_DOT, preferred_element_type=F32).astype(BF16)
    low_iota = iota((RADIX, q_rows), 0)
    high_iota = iota((high_rows, q_rows), 0)

    def lookup(tables, ids):
        hots = jnp.concatenate([one_hot(high_iota == (i // RADIX)) for i in ids], axis=1)
        found = [jnp.dot(t, hots, preferred_element_type=F32) for t in tables]
        masks = [low_iota == (i & (RADIX - 1)) for i in ids]
        return [
            [pick_rows(m, f[:, n * q_rows : (n + 1) * q_rows]) for n, m in enumerate(masks)]
            for f in found
        ]

    def check(j, carry):
        start = pl.multiple_of(j * 8, 8)
        rows = cand_t[pl.ds(start, 8), :]
        hits = lookup([marks], [rows[n : n + 1, :] for n in range(8)])[0]
        hit_t[pl.ds(start, 8), :] = jnp.concatenate(hits, axis=0)
        return carry

    lax.fori_loop(0, cand_count // 8, check, 0)
    cold = hit_t[...] < 0.5
    earlier = one_hot(iota((cand_count, cand_count), 0) > iota((cand_count, cand_count), 1))
    order = jnp.dot(earlier, one_hot(cold), preferred_element_type=F32).astype(jnp.int32)
    sel = jnp.where(cold, order, -1)
    sel_ref[...] = sel
    cand = cand_t[...]
    ids = [pick_rows(sel == r, cand) for r in range(COLD)]
    loc = jnp.concatenate([loc_ref[pl.ds(0, high_rows, stride=2), :], loc_ref[pl.ds(1, high_rows, stride=2), :]], axis=1)
    high_table = jnp.transpose((loc // RADIX).astype(F32)).astype(BF16)
    low_table = jnp.transpose((loc & (RADIX - 1)).astype(F32)).astype(BF16)
    high_part, low_part = lookup([high_table, low_table], ids)
    before = one_hot(iota((q_rows, q_rows), 0) < iota((q_rows, q_rows), 1))
    owner_iota = iota((groups, q_rows), 0)
    slot_iota = iota((LANES, q_rows), 0)
    query = iota((1, q_rows), 1).astype(F32)
    base = jnp.zeros((groups, 1), F32)
    owners, ranks, owner_hots, low_vals, high_vals, query_vals = [], [], [], [], [], []
    for r in range(COLD):
        row = high_part[r].astype(jnp.int32) * RADIX + low_part[r].astype(jnp.int32)
        owner = row // per_owner
        local = row & (per_owner - 1)
        owner_hot = one_hot(owner_iota == owner, F32)
        count = jnp.dot(owner_hot.astype(BF16), before, preferred_element_type=F32) + base
        rank = jnp.sum(owner_hot * count, axis=0, keepdims=True).astype(jnp.int32)
        base = base + jnp.sum(owner_hot, axis=1, keepdims=True)
        at_slot = slot_iota == rank
        owners.append(owner)
        ranks.append(rank)
        owner_hots.append(owner_hot.astype(BF16))
        low_vals.append(jnp.where(at_slot, (local & (RADIX - 1)).astype(F32), 0.0).astype(BF16))
        high_vals.append(jnp.where(at_slot, (local // RADIX + RADIX // 2).astype(F32), 0.0).astype(BF16))
        query_vals.append(jnp.where(at_slot, query, 0.0).astype(BF16))
    owner_all = jnp.concatenate(owner_hots, axis=1)

    def spread(vals):
        got = lax.dot_general(owner_all, jnp.concatenate(vals, axis=1), ROWS_DOT, preferred_element_type=F32)
        return got.astype(jnp.int32)

    low_got, high_got, query_got = spread(low_vals), spread(high_vals), spread(query_vals)
    packed = low_got + RADIX * (high_got - RADIX // 2) + per_owner * query_got
    req_ref[...] = jnp.where(high_got > 0, packed, -1)
    place_ref[...] = jnp.concatenate(owners + ranks, axis=0)


def prep_kernel(per_owner, spot_ref, q_ref, hot_ref, loc_ref, slab_ref, out_ref, col_scr):
    hot_each = out_ref.shape[0] - q_ref.shape[0]
    high_rows = loc_ref.shape[0]
    ids = hot_ref[pl.ds(spot_ref[0] * hot_each // LANES, 1), :]
    high_hot = one_hot(iota((high_rows, LANES), 0) == (ids // LANES))
    low_mask = iota((LANES, LANES), 0) == (ids & (LANES - 1))
    loc = loc_ref[...]
    first = (((0,), (0,)), ((), ()))
    high = jnp.transpose((loc // RADIX).astype(F32)).astype(BF16)
    low = jnp.transpose((loc & (RADIX - 1)).astype(F32)).astype(BF16)
    high = pick_rows(low_mask, jnp.dot(high, high_hot, preferred_element_type=F32))
    low = pick_rows(low_mask, jnp.dot(low, high_hot, preferred_element_type=F32))
    local = high * RADIX + low - (spot_ref[0] * per_owner).astype(F32)
    col_scr[...] = jnp.transpose(jnp.broadcast_to(local, (LANES, LANES)))
    start = pl.multiple_of(spot_ref[0] * hot_each % LANES, hot_each)
    cols = jnp.concatenate([col_scr[pl.ds(start, hot_each), :]] * (per_owner // LANES), axis=1)
    picks = one_hot(iota((hot_each, per_owner), 1).astype(F32) == cols)
    rows = jnp.dot(picks, slab_ref[...], preferred_element_type=F32).astype(BF16)
    out_ref[0 : q_ref.shape[0], :] = q_ref[...]
    out_ref[q_ref.shape[0] :, :] = rows


def fetch_kernel(capacity, asked_ref, slab_ref, out_ref):
    groups = asked_ref.shape[0]
    per_owner = slab_ref.shape[0]
    asked = jnp.maximum(asked_ref[...], 0)
    cols = jnp.transpose((asked & (per_owner - 1)).astype(F32))
    lane = iota((capacity, per_owner), 1).astype(F32)
    picks = [
        one_hot(lane == jnp.broadcast_to(cols[0:capacity, n : n + 1], (capacity, per_owner)), F32)
        for n in range(groups)
    ]
    got = jnp.dot(jnp.concatenate(picks, axis=0).astype(BF16), slab_ref[...], preferred_element_type=F32)
    out_ref[...] = got.astype(BF16)


def cold_kernel(scale, capacity, q_ref, found_ref, place_ref, cold_ref):
    q_rows = q_ref.shape[0]
    q = q_ref[...]
    place = place_ref[...]
    dests = [place[r : r + 1] * capacity + place[COLD + r : COLD + r + 1] for r in range(COLD)]
    colds = [jnp.zeros((1, q_rows), F32) for _ in range(COLD)]
    chunk = 256
    for j in range(found_ref.shape[0] // chunk):
        rows = found_ref[j * chunk : (j + 1) * chunk, :]
        got = scale * lax.dot_general(rows, q, ROWS_DOT, preferred_element_type=F32)
        ids = iota((chunk, q_rows), 0) + j * chunk
        for r in range(COLD):
            colds[r] = colds[r] + pick_rows(ids == dests[r], got)
    cold_ref[...] = jnp.concatenate(colds, axis=0)


def count_kernel(cand_t, teacher_ref, hot_ref, sel_ref, count_ref, target_ref, misc_ref, soft_t):
    cand_count, q_rows = cand_t.shape
    teacher = teacher_ref[...]
    shifted = teacher - jnp.max(teacher, axis=0, keepdims=True)
    log_target = shifted - jnp.log(jnp.sum(jnp.exp(shifted), axis=0, keepdims=True))
    target = jnp.exp(log_target)
    soft_t[...] = target
    sel = sel_ref[...]
    entropy = jnp.sum(target * log_target, axis=0, keepdims=True)
    rows = [pick_rows(sel == r, target) for r in range(COLD)]
    misc_ref[...] = jnp.concatenate(rows + [jnp.broadcast_to(entropy, (8, q_rows))], axis=0)
    hot_cols = jnp.transpose(hot_ref[...])
    for a in range(hot_ref.shape[0]):
        column = jnp.broadcast_to(hot_cols[:, a : a + 1], (LANES, q_rows))

        def add(k, carry):
            count, total = carry
            match = column == cand_t[pl.ds(k, 1), :]
            count = count + jnp.where(match, 1.0, 0.0)
            total = total + jnp.where(match, soft_t[pl.ds(k, 1), :], 0.0)
            return count, total

        start = (jnp.ones((LANES, q_rows), F32), jnp.zeros((LANES, q_rows), F32))
        count, total = lax.fori_loop(0, cand_count, add, start, unroll=4)
        count_ref[a * LANES : (a + 1) * LANES, :] = count
        target_ref[a * LANES : (a + 1) * LANES, :] = total


def score_kernel(scale, q_ref, hot_ref, cold_ref, count_ref, target_ref, place_ref, misc_ref, loss_ref, pay_ref, weight_ref, hot_scr, top_scr, slot_scr):
    step = pl.program_id(0)
    each, hot_each, feat = hot_ref.shape
    groups = pay_ref.shape[0]
    q_rows = q_ref.shape[0]
    size = each * hot_each

    @pl.when(step == 0)
    def _():
        top_scr[...] = jnp.max(cold_ref[...], axis=0, keepdims=True)

    got = scale * lax.dot_general(hot_ref[...].reshape(size, feat), q_ref[...], ROWS_DOT, preferred_element_type=F32)
    hot_scr[pl.ds(pl.multiple_of(step * size, size), size), :] = got
    top_scr[...] = jnp.maximum(top_scr[...], jnp.max(got, axis=0, keepdims=True))

    @pl.when(step == pl.num_programs(0) - 1)
    def _():
        cold = cold_ref[...]
        top = top_scr[...]
        place = place_ref[...]
        total = jnp.sum(jnp.exp(cold - top), axis=0, keepdims=True)
        hot_dot = jnp.zeros((1, q_rows), F32)
        for j in range(groups // 8):
            part = slice(j * 8 * hot_each, (j + 1) * 8 * hot_each)
            hot = hot_scr[part, :]
            total = total + jnp.sum(count_ref[part, :] * jnp.exp(hot - top), axis=0, keepdims=True)
            hot_dot = hot_dot + jnp.sum(target_ref[part, :] * hot, axis=0, keepdims=True)
        log_total = top + jnp.log(total)
        cold_target = misc_ref[0:COLD, :]
        entropy = misc_ref[COLD : COLD + 1, :]
        loss_ref[...] = entropy - hot_dot - jnp.sum(cold_target * cold, axis=0, keepdims=True) + log_total
        weight = (jnp.exp(cold - log_total) - cold_target).astype(BF16).astype(F32)
        weight_ref[...] = weight
        owner_iota = iota((groups, q_rows), 0)
        slot_iota = iota((LANES, q_rows), 0)
        owner_all = jnp.concatenate([one_hot(owner_iota == place[r : r + 1]) for r in range(COLD)], axis=1)
        slot_all = jnp.concatenate(
            [
                jnp.where(slot_iota == place[COLD + r : COLD + r + 1], weight[r : r + 1], 0.0).astype(BF16)
                for r in range(COLD)
            ],
            axis=1,
        )
        slot_scr[...] = lax.dot_general(owner_all, slot_all, ROWS_DOT, preferred_element_type=F32)
        for g in range(groups):
            part = slice(g * hot_each, (g + 1) * hot_each)
            coef = count_ref[part, :] * jnp.exp(hot_scr[part, :] - log_total) - target_ref[part, :]
            slot_row = jnp.broadcast_to(slot_scr[g : g + 1, :], (8, q_rows))
            pay_ref[g] = jnp.concatenate([coef, slot_row], axis=0).astype(BF16)


def query_kernel(scale, capacity, hot_ref, pay_ref, found_ref, weight_ref, place_ref, out_ref):
    groups, hot_each, feat = hot_ref.shape
    q_rows = out_ref.shape[0]
    acc = jnp.zeros(out_ref.shape, F32)
    step = 8
    first = (((0,), (0,)), ((), ()))
    for j in range(groups // step):
        rows = hot_ref[j * step : (j + 1) * step].reshape(step * hot_each, feat)
        coef = jnp.concatenate([pay_ref[j * step + n, 0:hot_each, :] for n in range(step)], axis=0)
        acc = acc + lax.dot_general(coef, rows, first, preferred_element_type=F32)
    chunk = 256
    place = place_ref[...]
    weight = weight_ref[...]
    dests = [place[r : r + 1] * capacity + place[COLD + r : COLD + r + 1] for r in range(COLD)]
    for j in range(found_ref.shape[0] // chunk):
        ids = iota((chunk, q_rows), 0) + j * chunk
        made = jnp.zeros((chunk, q_rows), F32)
        for r in range(COLD):
            made = jnp.where(ids == dests[r], weight[r : r + 1], made)
        rows = found_ref[j * chunk : (j + 1) * chunk, :]
        acc = acc + lax.dot_general(made.astype(BF16), rows, first, preferred_element_type=F32)
    out_ref[...] = scale * acc


def slab_kernel(scale, capacity, spot_ref, pay_ref, query_ref, row_ref, loc_ref, *refs):
    outs, (terms, hot_acc) = refs[:-2], refs[-2:]
    step = pl.program_id(0)
    groups = pay_ref.shape[0]
    hot_each, feat = hot_acc.shape

    @pl.when(step == 0)
    def _():
        hot_acc[...] = jnp.zeros_like(hot_acc)

    acc = hot_acc[...]
    for n in range(0, groups, 2):
        left = jnp.concatenate([pay_ref[n, 0:hot_each, :], pay_ref[n + 1, 0:hot_each, :]], axis=1)
        right = jnp.concatenate([query_ref[n], query_ref[n + 1]], axis=0)
        acc = acc + jnp.dot(left, right, preferred_element_type=F32)
    hot_acc[...] = acc
    sent = jnp.concatenate([pay_ref[n, hot_each : hot_each + 8, :].astype(F32)[0:1] for n in range(groups)], axis=0)
    cols = scale * jnp.transpose(sent)
    col = jnp.concatenate(
        [jnp.broadcast_to(cols[0:capacity, n : n + 1], (capacity, LANES)) for n in range(groups)], axis=0
    )
    size = groups * capacity
    wide = jnp.concatenate([col] * (feat // LANES), axis=1)
    made = (wide * row_ref[...].astype(F32)).astype(BF16)
    terms[pl.ds(pl.multiple_of(step * size, size), size), :] = made

    @pl.when(step == pl.num_programs(0) - 1)
    def _():
        full = scale * hot_acc[...]
        high = full.astype(BF16)
        rest = full - high.astype(F32)
        mid = rest.astype(BF16)
        low = (rest - mid.astype(F32)).astype(BF16)
        base = terms.shape[0] - LANES
        terms[base:, :] = jnp.concatenate([high, mid, low, jnp.zeros_like(low)], axis=0)
        loc = loc_ref[...]
        rows = outs[0].shape[0]
        ids = iota((rows, loc.shape[1]), 0)
        for d in range(0, len(outs), 2):
            starts = [(spot_ref[1] + e) % len(outs) * rows for e in (d, d + 1)]
            at = jnp.concatenate([one_hot(ids + start == loc) for start in starts], axis=0)
            got = jnp.dot(at, terms[...], preferred_element_type=F32)
            outs[d][...] = got[:rows].astype(outs[d].dtype)
            outs[d + 1][...] = got[rows:].astype(outs[d + 1].dtype)


def shards(queries, teacher, slab, candidates, hot_ids, location):
    groups = lax.axis_size("corpus")
    reps = lax.axis_size("rep")
    corpus_idx = lax.axis_index("corpus")
    q_rows, feat = queries.shape
    per_owner = slab.shape[0]
    hot_total = hot_ids.shape[0]
    hot_each = hot_total // groups
    cand_count = candidates.shape[1]
    capacity = q_rows * COLD * 3 // (2 * groups)
    scale = 2.0 / math.sqrt(feat)
    rep_idx = lax.axis_index("rep")
    spot = jnp.stack([corpus_idx, rep_idx]).astype(jnp.int32)
    loc_table = location.reshape(-1, LANES)
    hot_table = hot_ids.reshape(-1, LANES)
    sent_rows = pl.pallas_call(
        functools.partial(prep_kernel, per_owner),
        out_shape=jax.ShapeDtypeStruct((q_rows + hot_each, feat), BF16),
        in_specs=[SMEM_SPEC] + [VMEM_SPEC] * 4,
        out_specs=VMEM_SPEC,
        scratch_shapes=[pltpu.VMEM((LANES, LANES), F32)],
        name="prep",
    )(spot, queries, hot_table, loc_table, slab)
    cand_t, sent_rows = lax.optimization_barrier((candidates.T, sent_rows))
    gathered = lax.all_gather(sent_rows, "corpus", axis=0, tiled=False)
    req, place, sel = pl.pallas_call(
        functools.partial(request_kernel, per_owner, capacity, groups),
        out_shape=(
            jax.ShapeDtypeStruct((groups, LANES), jnp.int32),
            jax.ShapeDtypeStruct((2 * COLD, q_rows), jnp.int32),
            jax.ShapeDtypeStruct((cand_count, q_rows), jnp.int32),
        ),
        in_specs=[VMEM_SPEC] * 3,
        out_specs=(VMEM_SPEC,) * 3,
        scratch_shapes=[pltpu.VMEM((cand_count, q_rows), F32)],
        name="request",
    )(cand_t, hot_ids.reshape(1, hot_total), loc_table)
    asked = lax.all_to_all(req.reshape(groups, 1, LANES), "corpus", split_axis=0, concat_axis=0, tiled=True)
    asked = asked.reshape(groups, LANES)
    slots = groups * capacity
    parts = 4
    wanted = pl.pallas_call(
        functools.partial(fetch_kernel, capacity),
        grid=(parts,),
        out_shape=jax.ShapeDtypeStruct((slots, feat), BF16),
        in_specs=[pl.BlockSpec((groups // parts, LANES), lambda i: (i, 0)), pl.BlockSpec((per_owner, feat), lambda i: (0, 0))],
        out_specs=pl.BlockSpec((slots // parts, feat), lambda i: (i, 0)),
        name="fetch",
    )(asked, slab)
    found = lax.all_to_all(wanted.reshape(groups, capacity, feat), "corpus", split_axis=0, concat_axis=0, tiled=True)
    found = found.reshape(groups * capacity, feat)
    count, target, misc = pl.pallas_call(
        count_kernel,
        out_shape=(
            jax.ShapeDtypeStruct((hot_total, q_rows), F32),
            jax.ShapeDtypeStruct((hot_total, q_rows), F32),
            jax.ShapeDtypeStruct((2 * COLD, q_rows), F32),
        ),
        in_specs=[VMEM_SPEC] * 4,
        out_specs=(VMEM_SPEC,) * 3,
        scratch_shapes=[pltpu.VMEM((cand_count, q_rows), F32)],
        cost_estimate=pl.CostEstimate(flops=80_000_000, bytes_accessed=3_000_000, transcendentals=10_000),
        name="count",
    )(cand_t, teacher.T, hot_table, sel)
    hot_block = pl.BlockSpec((groups, hot_each, feat), lambda i: (0, q_rows // hot_each, 0))

    def whole(shape):
        return pl.BlockSpec(shape, lambda i: (0,) * len(shape))

    pay_rows = hot_each + 8
    cold = pl.pallas_call(
        functools.partial(cold_kernel, scale, capacity),
        out_shape=jax.ShapeDtypeStruct((COLD, q_rows), F32),
        in_specs=[VMEM_SPEC] * 3,
        out_specs=VMEM_SPEC,
        name="cold",
    )(queries, found, place)
    each = 8
    loss, pay, weight = pl.pallas_call(
        functools.partial(score_kernel, scale),
        grid=(groups // each,),
        out_shape=(
            jax.ShapeDtypeStruct((1, q_rows), F32),
            jax.ShapeDtypeStruct((groups, pay_rows, q_rows), BF16),
            jax.ShapeDtypeStruct((COLD, q_rows), F32),
        ),
        in_specs=[
            whole((q_rows, feat)),
            pl.BlockSpec((each, hot_each, feat), lambda i: (i, q_rows // hot_each, 0)),
            whole((COLD, q_rows)),
            whole((hot_total, q_rows)),
            whole((hot_total, q_rows)),
            whole((2 * COLD, q_rows)),
            whole((2 * COLD, q_rows)),
        ],
        out_specs=(whole((1, q_rows)), whole((groups, pay_rows, q_rows)), whole((COLD, q_rows))),
        scratch_shapes=[
            pltpu.VMEM((hot_total, q_rows), F32),
            pltpu.VMEM((1, q_rows), F32),
            pltpu.VMEM((groups, q_rows), F32),
        ],
        name="score",
    )(queries, gathered, cold, count, target, place, misc)
    got = lax.all_to_all(pay, "corpus", split_axis=0, concat_axis=0, tiled=True)
    query_grad = pl.pallas_call(
        functools.partial(query_kernel, scale, capacity),
        grid=(1,),
        out_shape=jax.ShapeDtypeStruct((q_rows, feat), F32),
        in_specs=[hot_block, whole((groups, pay_rows, q_rows)), whole((slots, feat)), whole((COLD, q_rows)), whole((2 * COLD, q_rows))],
        out_specs=whole((q_rows, feat)),
        cost_estimate=pl.CostEstimate(flops=700_000_000, bytes_accessed=7_000_000, transcendentals=0),
        name="query_grad",
    )(gathered, pay, found, weight, place)
    padded = asked[:, :capacity]
    source = jnp.arange(groups, dtype=jnp.int32)[:, None] * (q_rows + hot_each)
    query_rows = gathered.reshape(-1, feat)[(source + jnp.maximum(padded, 0) // per_owner).reshape(-1)]
    local = jnp.where(padded >= 0, padded & (per_owner - 1), -1).reshape(1, -1)
    mine = lax.dynamic_slice_in_dim(hot_ids, corpus_idx * hot_each, hot_each)
    own_hot = location[mine] - corpus_idx * per_owner
    tail = jnp.full((LANES - 3 * hot_each,), -1, jnp.int32)
    local = jnp.concatenate([local, jnp.concatenate([own_hot, own_hot, own_hot, tail])[None, :]], axis=1)
    step = 8
    quarter = (per_owner // reps, feat)
    quarters = pl.pallas_call(
        functools.partial(slab_kernel, scale, capacity),
        grid=(groups // step,),
        out_shape=tuple(jax.ShapeDtypeStruct(quarter, F32 if d == 0 else BF16) for d in range(reps)),
        in_specs=[
            SMEM_SPEC,
            pl.BlockSpec((step, pay_rows, q_rows), lambda i: (i, 0, 0)),
            pl.BlockSpec((step, q_rows, feat), lambda i: (i, 0, 0)),
            pl.BlockSpec((step * capacity, feat), lambda i: (i, 0)),
            whole((1, slots + LANES)),
        ],
        out_specs=tuple(whole(quarter) for _ in range(reps)),
        scratch_shapes=[pltpu.VMEM((slots + LANES, feat), BF16), pltpu.VMEM((hot_each, feat), F32)],
        name="slab_grad",
    )(spot, got, gathered, query_rows, local)
    slab_grad = quarters[0]
    received = [
        lax.ppermute(quarters[d], "rep", [(r, (r + d) % reps) for r in range(reps)]) for d in range(1, reps)
    ]
    slab_grad = slab_grad + sum(r.astype(F32) for r in received)
    return (loss.reshape(q_rows), query_grad, slab_grad)


def solution(mesh):
    return jax.shard_map(
        shards,
        mesh=mesh,
        in_specs=(
            P(("corpus", "rep"), None),
            P(("corpus", "rep"), None),
            P("corpus", None),
            P(("corpus", "rep"), None),
            P(),
            P(),
        ),
        out_specs=(P(("corpus", "rep")), P(("corpus", "rep"), None), P(("corpus", "rep"), None)),
        check_vma=False,
    )
```

time: 232 us -> 226 us (0.974)
  local copies, waits for them, and re-layouts: 28.3 us -> 17.3 us
  Pallas kernels: 51.9 us -> 62.5 us
  waiting for transfers between devices: 92.4 us -> 88.1 us
    all_to_all x2 -> x1, waiting for transfers between devices: 71.5 us -> 53.2 us  [shards(): lax.all_to_all(wanted.reshape(groups, capacity, feat), 'corpus', split_ax...]
    ppermute x0 -> x3, waiting for transfers between devices: none -> 15.4 us  [shards(): lax.ppermute(quarters[d], 'rep', [(r, (r + d) % reps) for r in range(reps)])]
    pallas_call x3 -> x6, Pallas kernels: 27.2 us -> 37.8 us  [the longest x1 12.7 us: shards(): pl.pallas_call(functools.partial(slab_kernel, scale, capacity), grid=(gro...]
    gather x2 -> x0, local copies, waits for them, and re-layouts: 6.28 us -> none  [the longest x1 5.65 us: shards(): found = slab[asked_slots & per_owner - 1]]
    all_to_all x2 -> x1, starting transfers between devices: 11.9 us -> 6.6 us  [shards(): lax.all_to_all(wanted.reshape(groups, capacity, feat), 'corpus', split_ax...]
    ppermute x0 -> x3, starting transfers between devices: none -> 4.65 us  [shards(): lax.ppermute(quarters[d], 'rep', [(r, (r + d) % reps) for r in range(reps)])]
    gather x1, local copies, waits for them, and re-layouts: 17.6 us -> 14.2 us  [shards(): gathered.reshape(-1, feat)]
    all_gather x1, waiting for transfers between devices: 20.1 us -> 16.8 us  [shards(): gathered = lax.all_gather(sent_rows, 'corpus', axis=0, tiled=False)]
  transfers between devices with their start and end apart: 4 -> 6, of which waited for: 4 -> 5; matrix products, arithmetic and copies ran while one was open for 11% -> 7% of each run, Pallas kernels for 13% -> 17%
where the time goes in v2:
time: 226 us; the launch traced here: 224 us
  waiting for transfers between devices  88.1 us (39%)
  Pallas kernels  62.5 us (28%)
  blocking collectives  19.8 us (9%)
  starting transfers between devices  19.3 us (9%)
  local copies, waits for them, and re-layouts  17.3 us (8%)
  between operations  14.1 us (6%)
  other arithmetic  3.24 us (1%)
    all_to_all x1, waiting for transfers between devices, shards(): lax.all_to_all(wanted.reshape(groups, capacity, feat), 'corpus', split_ax...  53.2 us
    all_to_all x1, blocking collectives, shards(): lax.all_to_all(req.reshape(groups, 1, LANES), 'corpus', split_axis=0, con...  19.8 us
    pallas_call x1, Pallas kernels, shards(): pl.pallas_call(count_kernel, out_shape=(jax.ShapeDtypeStruct((hot_total,...  18.4 us
    all_gather x1, waiting for transfers between devices, shards(): gathered = lax.all_gather(sent_rows, 'corpus', axis=0, tiled=False)  16.8 us
    ppermute x3, waiting for transfers between devices, shards(): lax.ppermute(quarters[d], 'rep', [(r, (r + d) % reps) for r in range(reps)])  15.4 us
    gather x1, local copies, waits for them, and re-layouts, shards(): gathered.reshape(-1, feat)  14.2 us
    pallas_call x1, Pallas kernels, shards(): pl.pallas_call(functools.partial(slab_kernel, scale, capacity), grid=(gro...  12.7 us
    all_to_all x1, starting transfers between devices, shards(): got = lax.all_to_all(pay, 'corpus', split_axis=0, concat_axis=0, tiled=True)  8.01 us
  transfers between devices with their start and end apart: 6, of which 5 were waited for; matrix products, arithmetic and copies ran while one was open for 7% of the time, Pallas kernels for 17%

profile of v2, /device:TPU:6, one launch (start us, length us, event | category | flops | bytes accessed | tf_op | source)
XLA Modules:
  0.0 224.3 jit_solution(936394951604779315)
XLA Ops:
  7.9 3.2 %prep.1 = bf16[160,768]{1,0:T(8,128)(2,1)} custom-call(s32[2]{0:T(128)} %pad_add_fusion.1.spot_ref, bf16[128,768]{1,0:T(8,128)(2,1)} %q_ref.5, s32[16,128]{1,0:T(8,128)} %bitcast.27, s32[512,128]{1,0:T(8,128)} %bitcast.23, bf16[1024,768]{1,0:T(8,128)(2,1)} %slab_ref.3), custom_call_target="tpu_custom_call" | custom-call | tf_op jit(solution)/shard_map/prep/pallas_call | solution.py:321
  11.1 6.2 %request.1 = (s32[64,128]{1,0:T(8,128)}, s32[16,128]{1,0:T(8,128)}, s32[64,128]{1,0:T(8,128)}) custom-call(s32[64,128]{1,0:T(8,128)} %bitcast.30, s32[1,2048]{1,0:T(1,128)} %bitcast.28, s32[512,128]{1,0:T(8,128)} %bitcast.24), custom_call_target="tpu_custom_call" | custom-call | tf_op jit(solution)/shard_map/request/pallas_call | solution.py:331
  17.3 19.8 %all_to_all.15 = s32[64,1,128]{2,1,0:T(1,128)} all-to-all(s32[64,1,128]{2,1,0:T(1,128)} %bitcast.32), channel_id=1, replica_groups=mesh['corpus'=64,'rep'=4] {'corpus'}, dimensions={0} | all-to-all | bytes 65536 | tf_op jit(solution)/shard_map/all_to_all | solution.py:343
  37.1 5.9 %fetch.1 = bf16[1536,768]{1,0:T(8,128)(2,1)} custom-call(s32[64,128]{1,0:T(8,128)} %bitcast.25, bf16[1024,768]{1,0:T(8,128)(2,1)} %slab_ref.3), custom_call_target="tpu_custom_call" | custom-call | tf_op jit(solution)/shard_map/fetch/pallas_call | solution.py:347
  43.0 6.6 %all-to-all-start.1 = ((bf16[64,24,768]{2,1,0:T(8,128)(2,1)}), bf16[64,24,768]{2,1,0:T(8,128)(2,1)S(1)}, u32[]{:S(2)}, u32[]{:S(2)}) async-start(bf16[64,24,768]{2,1,0:T(8,128)(2,1)} %bitcast.22), calls=%async_computation.1 | async-start | bytes 4718592 | tf_op jit(solution)/shard_map/all_to_all | solution.py:355
  49.6 18.4 %count.1 = (f32[2048,128]{1,0:T(8,128)}, f32[2048,128]{1,0:T(8,128)}, f32[16,128]{1,0:T(8,128)}) custom-call(s32[64,128]{1,0:T(8,128)} %bitcast.31, f32[64,128]{1,0:T(8,128)} %bitcast.33, s32[16,128]{1,0:T(8,128)} %bitcast.29, s32[64,128]{1,0:T(8,128)} %get-tuple-element.22.sel_ref), custom_call_target="tpu_custom_call" | custom-call | flops 80000000 | bytes 3000000 | tf_op jit(solution)/shard_map/count/pallas_call | solution.py:357
  68.1 53.2 %all-to-all-done.1 = bf16[64,24,768]{2,1,0:T(8,128)(2,1)S(1)} async-done(((bf16[64,24,768]{2,1,0:T(8,128)(2,1)}), bf16[64,24,768]{2,1,0:T(8,128)(2,1)S(1)}, u32[]{:S(2)}, u32[]{:S(2)}) %all-to-all-start.1) | async-done | bytes 2359328 | tf_op jit(solution)/shard_map/all_to_all | solution.py:355
  121.3 1.4 copy-done
  122.7 3.5 %cold.1.cold_ref = f32[8,128]{1,0:T(8,128)} custom-call(bf16[128,768]{1,0:T(8,128)(2,1)} %q_ref.5, bf16[1536,768]{1,0:T(8,128)(2,1)} %bitcast.20, s32[16,128]{1,0:T(8,128)} %get-tuple-element.21.place_ref), custom_call_target="tpu_custom_call" | custom-call | tf_op jit(solution)/shard_map/cold/pallas_call | solution.py:376
  126.2 16.8 %all-gather.3.cloned.1.call-done = bf16[10240,768]{1,0:T(8,128)(2,1)} async-done(((bf16[160,768]{1,0:T(8,128)(2,1)}), bf16[10240,768]{1,0:T(8,128)(2,1)}) %all-gather.3.cloned.1.call-update) | async-done | bytes 15728656 | tf_op jit(solution)/shard_map/all_gather | solution.py:330
  143.0 7.9 %score.1 = (f32[1,128]{1,0:T(1,128)}, bf16[64,40,128]{2,1,0:T(8,128)(2,1)}, f32[8,128]{1,0:T(8,128)}) custom-call(bf16[128,768]{1,0:T(8,128)(2,1)} %q_ref.5, bf16[64,160,768]{2,1,0:T(8,128)(2,1)} %bitcast.17, f32[8,128]{1,0:T(8,128)} %cold.1.cold_ref, f32[2048,128]{1,0:T(8,128)} %get-tuple-element.23.count_ref, f32[2048,128]{1,0:T(8,128)} %get-tuple-element.24.target_ref, ...), custom_call_target="tpu_custom_call" | custom-call | tf_op jit(solution)/shard_map/score/pallas_call | solution.py:384
  150.9 8.0 %all-to-all-start.2 = ((bf16[64,40,128]{2,1,0:T(8,128)(2,1)}), bf16[64,40,128]{2,1,0:T(8,128)(2,1)S(1)}, u32[]{:S(2)}, u32[]{:S(2)}) async-start(bf16[64,40,128]{2,1,0:T(8,128)(2,1)} %get-tuple-element.27.pay_ref), calls=%async_computation.2 | async-start | bytes 1310720 | tf_op jit(solution)/shard_map/all_to_all | solution.py:409
  158.9 0.8 compare_select_fusion.1
  159.7 0.7 gather_fusion.1
  161.4 14.2 %gather_fusion = bf16[1536,768]{1,0:T(8,128)(2,1)} fusion(bf16[10240,768]{1,0:T(8,128)(2,1)} %all-gather.3.cloned.1.call-done, s32[2048]{0:T(1024)S(1)} %pad_clamp_fusion), kind=kCustom, calls=%fused_computation | custom fusion | bytes 4724736 | tf_op jit(solution)/shard_map/gather | solution.py:421
  175.6 2.6 %all-to-all-done.2.pay_ref = bf16[64,40,128]{2,1,0:T(8,128)(2,1)S(1)} async-done(((bf16[64,40,128]{2,1,0:T(8,128)(2,1)}), bf16[64,40,128]{2,1,0:T(8,128)(2,1)S(1)}, u32[]{:S(2)}, u32[]{:S(2)}) %all-to-all-start.2) | async-done | bytes 655392 | tf_op jit(solution)/shard_map/all_to_all | solution.py:409
  178.2 0.8 copy-done.2
  179.1 12.7 %slab_grad.1 = (f32[256,768]{1,0:T(8,128)}, bf16[256,768]{1,0:T(8,128)(2,1)}, bf16[256,768]{1,0:T(8,128)(2,1)}, bf16[256,768]{1,0:T(8,128)(2,1)}) custom-call(s32[2]{0:T(128)} %pad_add_fusion.1.spot_ref, bf16[64,40,128]{2,1,0:T(8,128)(2,1)} %copy-done.2, bf16[64,160,768]{2,1,0:T(8,128)(2,1)} %bitcast.18, bf16[1536,768]{1,0:T(8,128)(2,1)} %gather_fusion, ...), custom_call_target="tpu_custom_call" | custom-call | tf_op jit(solution)/shard_map/slab_grad/pallas_call | solution.py:429
  191.8 3.0 %collective-permute-start.2 = (bf16[256,768]{1,0:T(8,128)(2,1)}, bf16[256,768]{1,0:T(8,128)(2,1)S(1)}, u32[]{:S(2)}, u32[]{:S(2)}) collective-permute-start(bf16[256,768]{1,0:T(8,128)(2,1)} %get-tuple-element.32), channel_id=1, source_target_pairs={{0,3},{1,0},{2,1},{3,2},{4,7},{5,4},{6,5},{7,6},{8,11},{9,8},{10,9... | collective-permute-start | bytes 1179656 | tf_op jit(solution)/shard_map/ppermute | solution.py:446
  195.4 1.1 collective-permute-start
  196.4 4.6 %query_grad.1 = f32[128,768]{1,0:T(8,128)} custom-call(bf16[64,160,768]{2,1,0:T(8,128)(2,1)} %bitcast.19, bf16[64,40,128]{2,1,0:T(8,128)(2,1)} %get-tuple-element.27.pay_ref, bf16[1536,768]{1,0:T(8,128)(2,1)} %bitcast.21, f32[8,128]{1,0:T(8,128)} %get-tuple-element.28.weight_ref, s32[16,128]{1,0:T(8,128)} %get-tuple-element.21.place_ref), custom_call_target="tpu_custom_call" | custom-call | flops 700000000 | bytes 7000000 | tf_op jit(solution)/shard_map/query_grad/pallas_call | solution.py:410
  201.1 11.8 %collective-permute-done.2 = bf16[256,768]{1,0:T(8,128)(2,1)S(1)} collective-permute-done((bf16[256,768]{1,0:T(8,128)(2,1)}, bf16[256,768]{1,0:T(8,128)(2,1)S(1)}, u32[]{:S(2)}, u32[]{:S(2)}) %collective-permute-start.2) | collective-permute-done | bytes 393248 | tf_op jit(solution)/shard_map/ppermute | solution.py:446
  212.9 3.6 %collective-permute-done = bf16[256,768]{1,0:T(8,128)(2,1)S(1)} collective-permute-done((bf16[256,768]{1,0:T(8,128)(2,1)}, bf16[256,768]{1,0:T(8,128)(2,1)S(1)}, u32[]{:S(2)}, u32[]{:S(2)}) %collective-permute-start) | collective-permute-done | bytes 393248 | tf_op jit(solution)/shard_map/ppermute | solution.py:446
  216.5 1.0 add_add_fusion
  (24 shorter events, 2.3 us)
Async XLA Ops:
  7.2 135.9 %all-gather.3.cloned.1.call-start = ((), (), s32[]{:S(2)}) async-start(), calls=%async_computation.3 | async-start | bytes 15974400 | tf_op jit(solution)/shard_map/all_gather | solution.py:330
  43.0 78.3 %all-to-all-start.1 = ((bf16[64,24,768]{2,1,0:T(8,128)(2,1)}), bf16[64,24,768]{2,1,0:T(8,128)(2,1)S(1)}, u32[]{:S(2)}, u32[]{:S(2)}) async-start(bf16[64,24,768]{2,1,0:T(8,128)(2,1)} %bitcast.22), calls=%async_computation.1 | async-start | bytes 4718592 | tf_op jit(solution)/shard_map/all_to_all | solution.py:355
  121.3 1.4 copy-start
  143.0 16.7 %copy-start.1 = (s32[65536]{0:T(1024)S(1)}, s32[65536]{0:T(1024)}, u32[]{:S(2)}) copy-start(s32[65536]{0:T(1024)} %param.11) | copy-start | bytes 786436
  143.0 17.5 %copy-start.4 = (s32[64,1,128]{2,1,0:T(1,128)S(1)}, s32[64,1,128]{2,1,0:T(1,128)}, u32[]{:S(2)}) copy-start(s32[64,1,128]{2,1,0:T(1,128)} %all_to_all.15) | copy-start | bytes 98308
  150.9 27.3 %all-to-all-start.2 = ((bf16[64,40,128]{2,1,0:T(8,128)(2,1)}), bf16[64,40,128]{2,1,0:T(8,128)(2,1)S(1)}, u32[]{:S(2)}, u32[]{:S(2)}) async-start(bf16[64,40,128]{2,1,0:T(8,128)(2,1)} %get-tuple-element.27.pay_ref), calls=%async_computation.2 | async-start | bytes 1310720 | tf_op jit(solution)/shard_map/all_to_all | solution.py:409
  178.2 0.8 copy-start.2
  191.8 21.1 %collective-permute-start.2 = (bf16[256,768]{1,0:T(8,128)(2,1)}, bf16[256,768]{1,0:T(8,128)(2,1)S(1)}, u32[]{:S(2)}, u32[]{:S(2)}) collective-permute-start(bf16[256,768]{1,0:T(8,128)(2,1)} %get-tuple-element.32), channel_id=1, source_target_pairs={{0,3},{1,0},{2,1},{3,2},{4,7},{5,4},{6,5},{7,6},{8,11},{9,8},{10,9... | collective-permute-start | bytes 1179656 | tf_op jit(solution)/shard_map/ppermute | solution.py:446
  194.8 18.1 %collective-permute-start.1 = (bf16[256,768]{1,0:T(8,128)(2,1)}, bf16[256,768]{1,0:T(8,128)(2,1)S(1)}, u32[]{:S(2)}, u32[]{:S(2)}) collective-permute-start(bf16[256,768]{1,0:T(8,128)(2,1)} %get-tuple-element.31), channel_id=1, source_target_pairs={{0,2},{1,3},{2,0},{3,1},{4,6},{5,7},{6,4},{7,5},{8,10},{9,11},{10,... | collective-permute-start | bytes 1179656 | tf_op jit(solution)/shard_map/ppermute | solution.py:446
  195.4 21.1 %collective-permute-start = (bf16[256,768]{1,0:T(8,128)(2,1)}, bf16[256,768]{1,0:T(8,128)(2,1)S(1)}, u32[]{:S(2)}, u32[]{:S(2)}) collective-permute-start(bf16[256,768]{1,0:T(8,128)(2,1)} %get-tuple-element.30), channel_id=1, source_target_pairs={{0,1},{1,2},{2,3},{3,0},{4,5},{5,6},{6,7},{7,4},{8,9},{9,10},{10,1... | collective-permute-start | bytes 1179656 | tf_op jit(solution)/shard_map/ppermute | solution.py:446
  196.4 20.0 %copy-start.3 = (f32[256,768]{1,0:T(8,128)S(1)}, f32[256,768]{1,0:T(8,128)}, u32[]{:S(2)}) copy-start(f32[256,768]{1,0:T(8,128)} %get-tuple-element.29) | copy-start | bytes 2359300
Sparse Core Ops, SparseCore 0:
  11.3 131.6 all-gather.2

commit v3 on v2

--- a/solution.py
+++ b/solution.py
@@ -7,6 +7,7 @@
 from jax.experimental import pallas as pl
 from jax.experimental.pallas import tpu as pltpu
 from jax.sharding import PartitionSpec as P
+
 
 COLD = 8
 LANES = 128
@@ -30,7 +31,7 @@
     return jnp.sum(jnp.where(mask, values, jnp.zeros_like(values)), axis=0, keepdims=True)
 
 
-def request_kernel(per_owner, capacity, groups, cand_t, hot_ref, loc_ref, req_ref, place_ref, sel_ref, hit_t):
+def request_kernel(per_owner, groups, cand_t, hot_ref, loc_ref, req_ref, place_ref, sel_ref, hit_t):
     cand_count, q_rows = cand_t.shape
     hot_total = hot_ref.shape[1]
     high_rows = loc_ref.shape[0] // 2
@@ -109,7 +110,6 @@
     high_hot = one_hot(iota((high_rows, LANES), 0) == (ids // LANES))
     low_mask = iota((LANES, LANES), 0) == (ids & (LANES - 1))
     loc = loc_ref[...]
-    first = (((0,), (0,)), ((), ()))
     high = jnp.transpose((loc // RADIX).astype(F32)).astype(BF16)
     low = jnp.transpose((loc & (RADIX - 1)).astype(F32)).astype(BF16)
     high = pick_rows(low_mask, jnp.dot(high, high_hot, preferred_element_type=F32))
@@ -124,18 +124,23 @@
     out_ref[q_ref.shape[0] :, :] = rows
 
 
-def fetch_kernel(capacity, asked_ref, slab_ref, out_ref):
+def fetch_kernel(capacity, asked_ref, slab_ref, out_ref, picks):
     groups = asked_ref.shape[0]
     per_owner = slab_ref.shape[0]
-    asked = jnp.maximum(asked_ref[...], 0)
-    cols = jnp.transpose((asked & (per_owner - 1)).astype(F32))
-    lane = iota((capacity, per_owner), 1).astype(F32)
-    picks = [
-        one_hot(lane == jnp.broadcast_to(cols[0:capacity, n : n + 1], (capacity, per_owner)), F32)
-        for n in range(groups)
-    ]
-    got = jnp.dot(jnp.concatenate(picks, axis=0).astype(BF16), slab_ref[...], preferred_element_type=F32)
-    out_ref[...] = got.astype(BF16)
+
+    @pl.when(pl.program_id(0) == 0)
+    def _():
+        asked = jnp.maximum(asked_ref[...], 0)
+        cols = jnp.transpose((asked & (per_owner - 1)).astype(F32))
+        lane = iota((capacity, per_owner), 1).astype(F32)
+        for n in range(0, groups, 2):
+            pair = [
+                one_hot(lane == jnp.broadcast_to(cols[0:capacity, m : m + 1], (capacity, per_owner)), F32)
+                for m in (n, n + 1)
+            ]
+            picks[n * capacity : (n + 2) * capacity, :] = jnp.concatenate(pair, axis=0).astype(BF16)
+
+    out_ref[...] = jnp.dot(picks[...], slab_ref[...], preferred_element_type=F32).astype(BF16)
 
 
 def cold_kernel(scale, capacity, q_ref, found_ref, place_ref, cold_ref):
@@ -257,8 +262,7 @@
     out_ref[...] = scale * acc
 
 
-def slab_kernel(scale, capacity, spot_ref, pay_ref, query_ref, row_ref, loc_ref, *refs):
-    outs, (terms, hot_acc) = refs[:-2], refs[-2:]
+def slab_kernel(scale, capacity, reps, spot_ref, pay_ref, query_ref, row_ref, loc_ref, first_ref, second_ref, terms, hot_acc):
     step = pl.program_id(0)
     groups = pay_ref.shape[0]
     hot_each, feat = hot_acc.shape
@@ -293,14 +297,23 @@
         base = terms.shape[0] - LANES
         terms[base:, :] = jnp.concatenate([high, mid, low, jnp.zeros_like(low)], axis=0)
         loc = loc_ref[...]
-        rows = outs[0].shape[0]
-        ids = iota((rows, loc.shape[1]), 0)
-        for d in range(0, len(outs), 2):
-            starts = [(spot_ref[1] + e) % len(outs) * rows for e in (d, d + 1)]
-            at = jnp.concatenate([one_hot(ids + start == loc) for start in starts], axis=0)
-            got = jnp.dot(at, terms[...], preferred_element_type=F32)
-            outs[d][...] = got[:rows].astype(outs[d].dtype)
-            outs[d + 1][...] = got[rows:].astype(outs[d + 1].dtype)
+        rows = first_ref.shape[0]
+        start = (spot_ref[1] + reps // 2) % reps * (2 * rows)
+        at = one_hot(iota((2 * rows, loc.shape[1]), 0) + start == loc)
+        got = jnp.dot(at, terms[...], preferred_element_type=F32).astype(BF16)
+        first_ref[...] = got[:rows]
+        second_ref[...] = got[rows:]
+
+
+def near_kernel(reps, spot_ref, terms_ref, loc_ref, *outs):
+    rows = outs[0].shape[0]
+    loc = loc_ref[...]
+    ids = iota((rows, loc.shape[1]), 0)
+    starts = [(spot_ref[1] + d) % reps * rows for d in (0, 1, reps - 1)]
+    at = jnp.concatenate([one_hot(ids + start == loc) for start in starts], axis=0)
+    got = jnp.dot(at, terms_ref[...], preferred_element_type=F32)
+    for n, out in enumerate(outs):
+        out[...] = got[n * rows : (n + 1) * rows]
 
 
 def shards(queries, teacher, slab, candidates, hot_ids, location):
@@ -318,18 +331,9 @@
     spot = jnp.stack([corpus_idx, rep_idx]).astype(jnp.int32)
     loc_table = location.reshape(-1, LANES)
     hot_table = hot_ids.reshape(-1, LANES)
-    sent_rows = pl.pallas_call(
-        functools.partial(prep_kernel, per_owner),
-        out_shape=jax.ShapeDtypeStruct((q_rows + hot_each, feat), BF16),
-        in_specs=[SMEM_SPEC] + [VMEM_SPEC] * 4,
-        out_specs=VMEM_SPEC,
-        scratch_shapes=[pltpu.VMEM((LANES, LANES), F32)],
-        name="prep",
-    )(spot, queries, hot_table, loc_table, slab)
-    cand_t, sent_rows = lax.optimization_barrier((candidates.T, sent_rows))
-    gathered = lax.all_gather(sent_rows, "corpus", axis=0, tiled=False)
+    cand_t = candidates.T
     req, place, sel = pl.pallas_call(
-        functools.partial(request_kernel, per_owner, capacity, groups),
+        functools.partial(request_kernel, per_owner, groups),
         out_shape=(
             jax.ShapeDtypeStruct((groups, LANES), jnp.int32),
             jax.ShapeDtypeStruct((2 * COLD, q_rows), jnp.int32),
@@ -340,16 +344,26 @@
         scratch_shapes=[pltpu.VMEM((cand_count, q_rows), F32)],
         name="request",
     )(cand_t, hot_ids.reshape(1, hot_total), loc_table)
+    sent_rows = pl.pallas_call(
+        functools.partial(prep_kernel, per_owner),
+        out_shape=jax.ShapeDtypeStruct((q_rows + hot_each, feat), BF16),
+        in_specs=[SMEM_SPEC] + [VMEM_SPEC] * 4,
+        out_specs=VMEM_SPEC,
+        scratch_shapes=[pltpu.VMEM((LANES, LANES), F32)],
+        name="prep",
+    )(spot, queries, hot_table, loc_table, slab)
+    gathered = lax.all_gather(sent_rows, "corpus", axis=0, tiled=False)
     asked = lax.all_to_all(req.reshape(groups, 1, LANES), "corpus", split_axis=0, concat_axis=0, tiled=True)
     asked = asked.reshape(groups, LANES)
     slots = groups * capacity
-    parts = 4
+    block = 256
     wanted = pl.pallas_call(
         functools.partial(fetch_kernel, capacity),
-        grid=(parts,),
+        grid=(feat // block,),
         out_shape=jax.ShapeDtypeStruct((slots, feat), BF16),
-        in_specs=[pl.BlockSpec((groups // parts, LANES), lambda i: (i, 0)), pl.BlockSpec((per_owner, feat), lambda i: (0, 0))],
-        out_specs=pl.BlockSpec((slots // parts, feat), lambda i: (i, 0)),
+        in_specs=[pl.BlockSpec((groups, LANES), lambda i: (0, 0)), pl.BlockSpec((per_owner, block), lambda i: (0, i))],
+        out_specs=pl.BlockSpec((slots, block), lambda i: (0, i)),
+        scratch_shapes=[pltpu.VMEM((slots, per_owner), BF16)],
         name="fetch",
     )(asked, slab)
     found = lax.all_to_all(wanted.reshape(groups, capacity, feat), "corpus", split_axis=0, concat_axis=0, tiled=True)
@@ -425,27 +439,41 @@
     tail = jnp.full((LANES - 3 * hot_each,), -1, jnp.int32)
     local = jnp.concatenate([local, jnp.concatenate([own_hot, own_hot, own_hot, tail])[None, :]], axis=1)
     step = 8
-    quarter = (per_owner // reps, feat)
-    quarters = pl.pallas_call(
-        functools.partial(slab_kernel, scale, capacity),
+    rows = per_owner // reps
+    half = jax.ShapeDtypeStruct((rows // 2, feat), BF16)
+    depth = slots + LANES
+    first, second, terms = pl.pallas_call(
+        functools.partial(slab_kernel, scale, capacity, reps),
         grid=(groups // step,),
-        out_shape=tuple(jax.ShapeDtypeStruct(quarter, F32 if d == 0 else BF16) for d in range(reps)),
+        out_shape=(half, half, jax.ShapeDtypeStruct((depth, feat), BF16)),
         in_specs=[
             SMEM_SPEC,
             pl.BlockSpec((step, pay_rows, q_rows), lambda i: (i, 0, 0)),
             pl.BlockSpec((step, q_rows, feat), lambda i: (i, 0, 0)),
             pl.BlockSpec((step * capacity, feat), lambda i: (i, 0)),
-            whole((1, slots + LANES)),
+            whole((1, depth)),
         ],
-        out_specs=tuple(whole(quarter) for _ in range(reps)),
-        scratch_shapes=[pltpu.VMEM((slots + LANES, feat), BF16), pltpu.VMEM((hot_each, feat), F32)],
+        out_specs=(whole(half.shape), whole(half.shape), whole((depth, feat))),
+        scratch_shapes=[pltpu.VMEM((hot_each, feat), F32)],
         name="slab_grad",
     )(spot, got, gathered, query_rows, local)
-    slab_grad = quarters[0]
-    received = [
-        lax.ppermute(quarters[d], "rep", [(r, (r + d) % reps) for r in range(reps)]) for d in range(1, reps)
-    ]
-    slab_grad = slab_grad + sum(r.astype(F32) for r in received)
+    ahead = [(r, (r + 1) % reps) for r in range(reps)]
+    behind = [(r, (r - 1) % reps) for r in range(reps)]
+    first = lax.ppermute(first, "rep", ahead)
+    second = lax.ppermute(second, "rep", behind)
+    own, after, before = pl.pallas_call(
+        functools.partial(near_kernel, reps),
+        out_shape=(jax.ShapeDtypeStruct((rows, feat), F32),) * 3,
+        in_specs=[SMEM_SPEC, VMEM_SPEC, VMEM_SPEC],
+        out_specs=(VMEM_SPEC,) * 3,
+        cost_estimate=pl.CostEstimate(flops=2_000_000_000, bytes_accessed=6_000_000, transcendentals=0),
+        name="near",
+    )(spot, terms, local)
+    after = (after + jnp.pad(first.astype(F32), ((0, rows // 2), (0, 0)))).astype(BF16)
+    before = (before + jnp.pad(second.astype(F32), ((rows // 2, 0), (0, 0)))).astype(BF16)
+    after = lax.ppermute(after, "rep", ahead)
+    before = lax.ppermute(before, "rep", behind)
+    slab_grad = own + after.astype(F32) + before.astype(F32)
     return (loss.reshape(q_rows), query_grad, slab_grad)
 
 

time: 226 us -> 225 us (level)
  waiting for transfers between devices: 88.1 us -> 80 us
  Pallas kernels: 62.5 us -> 66.2 us
  other arithmetic: 3.24 us -> 5.52 us
    ppermute x3 -> x4, waiting for transfers between devices: 15.4 us -> 7.32 us  [the longest x1 4.68 us: shards(): after = lax.ppermute(after, 'rep', ahead)]
    pallas_call x3 -> x4, Pallas kernels: 24.8 us -> 28.4 us  [the longest x1 10.9 us: shards(): pl.pallas_call(functools.partial(slab_kernel, scale, capacity, reps), gri...]
    convert_element_type x0 -> x2, other arithmetic: none -> 2.37 us  [the longest x1 1.19 us: shards(): (before + jnp.pad(second.astype(F32), ((rows // 2, 0), (0, 0)))).astype(B...]
    ppermute x3 -> x4, starting transfers between devices: 4.65 us -> 6.71 us  [the longest x1 3.66 us: shards(): before = lax.ppermute(before, 'rep', behind)]
  transfers between devices with their start and end apart: 6 -> 7, of which waited for: 5 -> 6; matrix products, arithmetic and copies ran while one was open for 7% -> 8% of each run, Pallas kernels for 17% -> 20%
where the time goes in v3:
time: 225 us; the launch traced here: 224 us
  waiting for transfers between devices  80 us (36%)
  Pallas kernels  66.2 us (29%)
  starting transfers between devices  21.4 us (10%)
  blocking collectives  19.7 us (9%)
  local copies, waits for them, and re-layouts  17.3 us (8%)
  between operations  14.1 us (6%)
  other arithmetic  5.52 us (2%)
    all_to_all x1, waiting for transfers between devices, shards(): lax.all_to_all(wanted.reshape(groups, capacity, feat), 'corpus', split_ax...  53 us
    all_to_all x1, blocking collectives, shards(): lax.all_to_all(req.reshape(groups, 1, LANES), 'corpus', split_axis=0, con...  19.7 us
    pallas_call x1, Pallas kernels, shards(): pl.pallas_call(count_kernel, out_shape=(jax.ShapeDtypeStruct((hot_total,...  18.5 us
    all_gather x1, waiting for transfers between devices, shards(): gathered = lax.all_gather(sent_rows, 'corpus', axis=0, tiled=False)  17 us
    gather x1, local copies, waits for them, and re-layouts, shards(): gathered.reshape(-1, feat)  14.2 us
    pallas_call x1, Pallas kernels, shards(): pl.pallas_call(functools.partial(slab_kernel, scale, capacity, reps), gri...  10.9 us
    all_to_all x1, starting transfers between devices, shards(): got = lax.all_to_all(pay, 'corpus', split_axis=0, concat_axis=0, tiled=True)  8.07 us
    pallas_call x1, Pallas kernels, shards(): pl.pallas_call(functools.partial(score_kernel, scale), grid=(groups // ea...  7.89 us
  transfers between devices with their start and end apart: 7, of which 6 were waited for; matrix products, arithmetic and copies ran while one was open for 8% of the time, Pallas kernels for 20%

profile of v3, /device:TPU:6, one launch (start us, length us, event | category | flops | bytes accessed | tf_op | source)
XLA Modules:
  0.0 224.2 jit_solution(8976230257404537094)
XLA Ops:
  7.8 3.2 %prep.1 = bf16[160,768]{1,0:T(8,128)(2,1)} custom-call(s32[2]{0:T(128)} %pad_add_fusion.1.spot_ref, bf16[128,768]{1,0:T(8,128)(2,1)} %q_ref.5, s32[16,128]{1,0:T(8,128)} %bitcast.27, s32[512,128]{1,0:T(8,128)} %bitcast.23, bf16[1024,768]{1,0:T(8,128)(2,1)} %slab_ref.3), custom_call_target="tpu_custom_call" | custom-call | tf_op jit(solution)/shard_map/prep/pallas_call | solution.py:347
  11.1 6.2 %request.1 = (s32[64,128]{1,0:T(8,128)}, s32[16,128]{1,0:T(8,128)}, s32[64,128]{1,0:T(8,128)}) custom-call(s32[64,128]{1,0:T(8,128)} %bitcast.30, s32[1,2048]{1,0:T(1,128)} %bitcast.28, s32[512,128]{1,0:T(8,128)} %bitcast.24), custom_call_target="tpu_custom_call" | custom-call | tf_op jit(solution)/shard_map/request/pallas_call | solution.py:335
  17.3 19.7 %all_to_all.15 = s32[64,1,128]{2,1,0:T(1,128)} all-to-all(s32[64,1,128]{2,1,0:T(1,128)} %bitcast.32), channel_id=1, replica_groups=mesh['corpus'=64,'rep'=4] {'corpus'}, dimensions={0} | all-to-all | bytes 65536 | tf_op jit(solution)/shard_map/all_to_all | solution.py:356
  37.0 6.0 %fetch.1 = bf16[1536,768]{1,0:T(8,128)(2,1)} custom-call(s32[64,128]{1,0:T(8,128)} %bitcast.25, bf16[1024,768]{1,0:T(8,128)(2,1)} %slab_ref.3), custom_call_target="tpu_custom_call" | custom-call | tf_op jit(solution)/shard_map/fetch/pallas_call | solution.py:360
  42.9 6.6 %all-to-all-start.1 = ((bf16[64,24,768]{2,1,0:T(8,128)(2,1)}), bf16[64,24,768]{2,1,0:T(8,128)(2,1)S(1)}, u32[]{:S(2)}, u32[]{:S(2)}) async-start(bf16[64,24,768]{2,1,0:T(8,128)(2,1)} %bitcast.22), calls=%async_computation.1 | async-start | bytes 4718592 | tf_op jit(solution)/shard_map/all_to_all | solution.py:369
  49.5 18.5 %count.1 = (f32[2048,128]{1,0:T(8,128)}, f32[2048,128]{1,0:T(8,128)}, f32[16,128]{1,0:T(8,128)}) custom-call(s32[64,128]{1,0:T(8,128)} %bitcast.31, f32[64,128]{1,0:T(8,128)} %bitcast.33, s32[16,128]{1,0:T(8,128)} %bitcast.29, s32[64,128]{1,0:T(8,128)} %get-tuple-element.20.sel_ref), custom_call_target="tpu_custom_call" | custom-call | flops 80000000 | bytes 3000000 | tf_op jit(solution)/shard_map/count/pallas_call | solution.py:371
  68.0 53.0 %all-to-all-done.1 = bf16[64,24,768]{2,1,0:T(8,128)(2,1)S(1)} async-done(((bf16[64,24,768]{2,1,0:T(8,128)(2,1)}), bf16[64,24,768]{2,1,0:T(8,128)(2,1)S(1)}, u32[]{:S(2)}, u32[]{:S(2)}) %all-to-all-start.1) | async-done | bytes 2359328 | tf_op jit(solution)/shard_map/all_to_all | solution.py:369
  121.0 1.4 copy-done
  122.4 3.5 %cold.1.cold_ref = f32[8,128]{1,0:T(8,128)} custom-call(bf16[128,768]{1,0:T(8,128)(2,1)} %q_ref.5, bf16[1536,768]{1,0:T(8,128)(2,1)} %bitcast.20, s32[16,128]{1,0:T(8,128)} %get-tuple-element.19.place_ref), custom_call_target="tpu_custom_call" | custom-call | tf_op jit(solution)/shard_map/cold/pallas_call | solution.py:390
  125.9 17.0 %all-gather.3.cloned.1.call-done = bf16[10240,768]{1,0:T(8,128)(2,1)} async-done(((bf16[160,768]{1,0:T(8,128)(2,1)}), bf16[10240,768]{1,0:T(8,128)(2,1)}) %all-gather.3.cloned.1.call-update) | async-done | bytes 15728656 | tf_op jit(solution)/shard_map/all_gather | solution.py:355
  142.9 7.9 %score.1 = (f32[1,128]{1,0:T(1,128)}, bf16[64,40,128]{2,1,0:T(8,128)(2,1)}, f32[8,128]{1,0:T(8,128)}) custom-call(bf16[128,768]{1,0:T(8,128)(2,1)} %q_ref.5, bf16[64,160,768]{2,1,0:T(8,128)(2,1)} %bitcast.17, f32[8,128]{1,0:T(8,128)} %cold.1.cold_ref, f32[2048,128]{1,0:T(8,128)} %get-tuple-element.21.count_ref, f32[2048,128]{1,0:T(8,128)} %get-tuple-element.22.target_ref, ...), custom_call_target="tpu_custom_call" | custom-call | tf_op jit(solution)/shard_map/score/pallas_call | solution.py:398
  150.8 8.1 %all-to-all-start.2 = ((bf16[64,40,128]{2,1,0:T(8,128)(2,1)}), bf16[64,40,128]{2,1,0:T(8,128)(2,1)S(1)}, u32[]{:S(2)}, u32[]{:S(2)}) async-start(bf16[64,40,128]{2,1,0:T(8,128)(2,1)} %get-tuple-element.25.pay_ref), calls=%async_computation.2 | async-start | bytes 1310720 | tf_op jit(solution)/shard_map/all_to_all | solution.py:423
  161.4 14.2 %gather_fusion = bf16[1536,768]{1,0:T(8,128)(2,1)} fusion(bf16[10240,768]{1,0:T(8,128)(2,1)} %all-gather.3.cloned.1.call-done, s32[2048]{0:T(1024)S(1)} %pad_clamp_fusion), kind=kCustom, calls=%fused_computation | custom fusion | bytes 4724736 | tf_op jit(solution)/shard_map/gather | solution.py:435
  175.6 2.6 %all-to-all-done.2.pay_ref = bf16[64,40,128]{2,1,0:T(8,128)(2,1)S(1)} async-done(((bf16[64,40,128]{2,1,0:T(8,128)(2,1)}), bf16[64,40,128]{2,1,0:T(8,128)(2,1)S(1)}, u32[]{:S(2)}, u32[]{:S(2)}) %all-to-all-start.2) | async-done | bytes 655392 | tf_op jit(solution)/shard_map/all_to_all | solution.py:423
  179.0 10.9 %slab_grad.1 = (bf16[128,768]{1,0:T(8,128)(2,1)}, bf16[128,768]{1,0:T(8,128)(2,1)}, bf16[1664,768]{1,0:T(8,128)(2,1)}) custom-call(s32[2]{0:T(128)} %pad_add_fusion.1.spot_ref, bf16[64,40,128]{2,1,0:T(8,128)(2,1)} %copy-done.2, bf16[64,160,768]{2,1,0:T(8,128)(2,1)} %bitcast.18, bf16[1536,768]{1,0:T(8,128)(2,1)} %gather_fusion, s32[1,1664]{1,0:T(1,128)} %pad_add_fusion.loc_ref), custom_call_target="tpu_custom_call" | custom-call | tf_op jit(solution)/shard_map/slab_grad/pallas_call | solution.py:445
  190.0 3.0 %collective-permute-start.2 = (bf16[128,768]{1,0:T(8,128)(2,1)}, bf16[128,768]{1,0:T(8,128)(2,1)S(1)}, u32[]{:S(2)}, u32[]{:S(2)}) collective-permute-start(bf16[128,768]{1,0:T(8,128)(2,1)} %get-tuple-element.32), channel_id=1, source_target_pairs={{0,3},{1,0},{2,1},{3,2},{4,7},{5,4},{6,5},{7,6},{8,11},{9,8},{10,9... | collective-permute-start | bytes 589832 | tf_op jit(solution)/shard_map/ppermute | solution.py:463
  192.9 5.3 %near.1 = (f32[256,768]{1,0:T(8,128)}, f32[256,768]{1,0:T(8,128)}, f32[256,768]{1,0:T(8,128)}) custom-call(s32[2]{0:T(128)} %pad_add_fusion.1.spot_ref, bf16[1664,768]{1,0:T(8,128)(2,1)} %get-tuple-element.27.terms_ref, s32[1,1664]{1,0:T(1,128)} %pad_add_fusion.loc_ref), custom_call_target="tpu_custom_call" | custom-call | flops 2000000000 | bytes 6000000 | tf_op jit(solution)/shard_map/near/pallas_call | solution.py:464
  198.4 1.2 add_convert_fusion
  199.5 3.7 %collective-permute-start.3 = (bf16[256,768]{1,0:T(8,128)(2,1)S(1)}, bf16[256,768]{1,0:T(8,128)(2,1)S(1)}, u32[]{:S(2)}, u32[]{:S(2)}) collective-permute-start(bf16[256,768]{1,0:T(8,128)(2,1)S(1)} %add_convert_fusion), channel_id=1, source_target_pairs={{0,3},{1,0},{2,1},{3,2},{4,7},{5,4},{6,5},{7,6},{8,11},{9,8},{10,9... | collective-permute-start | bytes 1179656 | tf_op jit(solution)/shard_map/ppermute | solution.py:475
  203.2 1.2 add_convert_fusion.1
  204.5 4.7 %query_grad.1 = f32[128,768]{1,0:T(8,128)} custom-call(bf16[64,160,768]{2,1,0:T(8,128)(2,1)} %bitcast.19, bf16[64,40,128]{2,1,0:T(8,128)(2,1)} %get-tuple-element.25.pay_ref, bf16[1536,768]{1,0:T(8,128)(2,1)} %bitcast.21, f32[8,128]{1,0:T(8,128)} %get-tuple-element.26.weight_ref, s32[16,128]{1,0:T(8,128)} %get-tuple-element.19.place_ref), custom_call_target="tpu_custom_call" | custom-call | flops 700000000 | bytes 7000000 | tf_op jit(solution)/shard_map/query_grad/pallas_call | solution.py:424
  209.2 2.5 %collective-permute-done.3 = bf16[256,768]{1,0:T(8,128)(2,1)S(1)} collective-permute-done((bf16[256,768]{1,0:T(8,128)(2,1)S(1)}, bf16[256,768]{1,0:T(8,128)(2,1)S(1)}, u32[]{:S(2)}, u32[]{:S(2)}) %collective-permute-start.3) | collective-permute-done | bytes 393248 | tf_op jit(solution)/shard_map/ppermute | solution.py:475
  211.7 4.7 %collective-permute-done.1 = bf16[256,768]{1,0:T(8,128)(2,1)S(1)} collective-permute-done((bf16[256,768]{1,0:T(8,128)(2,1)S(1)}, bf16[256,768]{1,0:T(8,128)(2,1)S(1)}, u32[]{:S(2)}, u32[]{:S(2)}) %collective-permute-start.1) | collective-permute-done | bytes 393248 | tf_op jit(solution)/shard_map/ppermute | solution.py:474
  216.4 1.0 convert_add_fusion
  (29 shorter events, 4.2 us)
Async XLA Ops:
  7.2 135.8 %all-gather.3.cloned.1.call-start = ((), (), s32[]{:S(2)}) async-start(), calls=%async_computation.3 | async-start | bytes 15974400 | tf_op jit(solution)/shard_map/all_gather | solution.py:355
  42.9 78.1 %all-to-all-start.1 = ((bf16[64,24,768]{2,1,0:T(8,128)(2,1)}), bf16[64,24,768]{2,1,0:T(8,128)(2,1)S(1)}, u32[]{:S(2)}, u32[]{:S(2)}) async-start(bf16[64,24,768]{2,1,0:T(8,128)(2,1)} %bitcast.22), calls=%async_computation.1 | async-start | bytes 4718592 | tf_op jit(solution)/shard_map/all_to_all | solution.py:369
  121.0 1.4 copy-start
  142.9 16.8 %copy-start.1 = (s32[65536]{0:T(1024)S(1)}, s32[65536]{0:T(1024)}, u32[]{:S(2)}) copy-start(s32[65536]{0:T(1024)} %param.11) | copy-start | bytes 786436
  142.9 17.6 %copy-start.4 = (s32[64,1,128]{2,1,0:T(1,128)S(1)}, s32[64,1,128]{2,1,0:T(1,128)}, u32[]{:S(2)}) copy-start(s32[64,1,128]{2,1,0:T(1,128)} %all_to_all.15) | copy-start | bytes 98308
  150.8 27.4 %all-to-all-start.2 = ((bf16[64,40,128]{2,1,0:T(8,128)(2,1)}), bf16[64,40,128]{2,1,0:T(8,128)(2,1)S(1)}, u32[]{:S(2)}, u32[]{:S(2)}) async-start(bf16[64,40,128]{2,1,0:T(8,128)(2,1)} %get-tuple-element.25.pay_ref), calls=%async_computation.2 | async-start | bytes 1310720 | tf_op jit(solution)/shard_map/all_to_all | solution.py:423
  178.2 0.8 copy-start.2
  190.0 8.4 %collective-permute-start.2 = (bf16[128,768]{1,0:T(8,128)(2,1)}, bf16[128,768]{1,0:T(8,128)(2,1)S(1)}, u32[]{:S(2)}, u32[]{:S(2)}) collective-permute-start(bf16[128,768]{1,0:T(8,128)(2,1)} %get-tuple-element.32), channel_id=1, source_target_pairs={{0,3},{1,0},{2,1},{3,2},{4,7},{5,4},{6,5},{7,6},{8,11},{9,8},{10,9... | collective-permute-start | bytes 589832 | tf_op jit(solution)/shard_map/ppermute | solution.py:463
  192.9 10.3 %collective-permute-start = (bf16[128,768]{1,0:T(8,128)(2,1)}, bf16[128,768]{1,0:T(8,128)(2,1)S(1)}, u32[]{:S(2)}, u32[]{:S(2)}) collective-permute-start(bf16[128,768]{1,0:T(8,128)(2,1)} %get-tuple-element.30), channel_id=1, source_target_pairs={{0,1},{1,2},{2,3},{3,0},{4,5},{5,6},{6,7},{7,4},{8,9},{9,10},{10,1... | collective-permute-start | bytes 589832 | tf_op jit(solution)/shard_map/ppermute | solution.py:462
  199.5 12.1 %collective-permute-start.3 = (bf16[256,768]{1,0:T(8,128)(2,1)S(1)}, bf16[256,768]{1,0:T(8,128)(2,1)S(1)}, u32[]{:S(2)}, u32[]{:S(2)}) collective-permute-start(bf16[256,768]{1,0:T(8,128)(2,1)S(1)} %add_convert_fusion), channel_id=1, source_target_pairs={{0,3},{1,0},{2,1},{3,2},{4,7},{5,4},{6,5},{7,6},{8,11},{9,8},{10,9... | collective-permute-start | bytes 1179656 | tf_op jit(solution)/shard_map/ppermute | solution.py:475
  204.4 12.0 %collective-permute-start.1 = (bf16[256,768]{1,0:T(8,128)(2,1)S(1)}, bf16[256,768]{1,0:T(8,128)(2,1)S(1)}, u32[]{:S(2)}, u32[]{:S(2)}) collective-permute-start(bf16[256,768]{1,0:T(8,128)(2,1)S(1)} %add_convert_fusion.1), channel_id=1, source_target_pairs={{0,1},{1,2},{2,3},{3,0},{4,5},{5,6},{6,7},{7,4},{8,9},{9,10},{10,1... | collective-permute-start | bytes 1179656 | tf_op jit(solution)/shard_map/ppermute | solution.py:474
  204.5 11.9 %copy-start.3 = (f32[256,768]{1,0:T(8,128)S(1)}, f32[256,768]{1,0:T(8,128)}, u32[]{:S(2)}) copy-start(f32[256,768]{1,0:T(8,128)} %get-tuple-element.28) | copy-start | bytes 2359300
Sparse Core Ops, SparseCore 0:
  11.3 131.6 all-gather.2

commit v4 on v3

--- a/solution.py
+++ b/solution.py
@@ -11,6 +11,8 @@
 
 COLD = 8
 LANES = 128
+X_SIZE, Z_SIZE, CORES = 4, 8, 2
+PIECES = X_SIZE * CORES
 RADIX = 256
 F32 = jnp.float32
 BF16 = jnp.bfloat16
@@ -103,8 +105,8 @@
     place_ref[...] = jnp.concatenate(owners + ranks, axis=0)
 
 
-def prep_kernel(per_owner, spot_ref, q_ref, hot_ref, loc_ref, slab_ref, out_ref, col_scr):
-    hot_each = out_ref.shape[0] - q_ref.shape[0]
+def prep_kernel(per_owner, spot_ref, hot_ref, loc_ref, slab_ref, out_ref, col_scr):
+    hot_each = out_ref.shape[0]
     high_rows = loc_ref.shape[0]
     ids = hot_ref[pl.ds(spot_ref[0] * hot_each // LANES, 1), :]
     high_hot = one_hot(iota((high_rows, LANES), 0) == (ids // LANES))
@@ -119,9 +121,14 @@
     start = pl.multiple_of(spot_ref[0] * hot_each % LANES, hot_each)
     cols = jnp.concatenate([col_scr[pl.ds(start, hot_each), :]] * (per_owner // LANES), axis=1)
     picks = one_hot(iota((hot_each, per_owner), 1).astype(F32) == cols)
-    rows = jnp.dot(picks, slab_ref[...], preferred_element_type=F32).astype(BF16)
-    out_ref[0 : q_ref.shape[0], :] = q_ref[...]
-    out_ref[q_ref.shape[0] :, :] = rows
+    out_ref[...] = jnp.dot(picks, slab_ref[...], preferred_element_type=F32).astype(BF16)
+
+
+def owner_of(spot_ref, piece, d):
+    x = (spot_ref[0] // (Z_SIZE * CORES) - piece % X_SIZE) & (X_SIZE - 1)
+    z = (spot_ref[0] // CORES - d) & (Z_SIZE - 1)
+    core = (spot_ref[0] + piece // X_SIZE) & (CORES - 1)
+    return (x * Z_SIZE + z) * CORES + core
 
 
 def fetch_kernel(capacity, asked_ref, slab_ref, out_ref, picks):
@@ -148,15 +155,20 @@
     q = q_ref[...]
     place = place_ref[...]
     dests = [place[r : r + 1] * capacity + place[COLD + r : COLD + r + 1] for r in range(COLD)]
-    colds = [jnp.zeros((1, q_rows), F32) for _ in range(COLD)]
     chunk = 256
-    for j in range(found_ref.shape[0] // chunk):
-        rows = found_ref[j * chunk : (j + 1) * chunk, :]
-        got = scale * lax.dot_general(rows, q, ROWS_DOT, preferred_element_type=F32)
-        ids = iota((chunk, q_rows), 0) + j * chunk
-        for r in range(COLD):
-            colds[r] = colds[r] + pick_rows(ids == dests[r], got)
-    cold_ref[...] = jnp.concatenate(colds, axis=0)
+
+    def score(j, sums):
+        start = pl.multiple_of(j * chunk, chunk)
+        got = scale * lax.dot_general(found_ref[pl.ds(start, chunk), :], q, ROWS_DOT, preferred_element_type=F32)
+        ids = iota((chunk, q_rows), 0) + start
+        return [
+            total + jnp.sum(jnp.where(ids == dest, got, 0.0).reshape(-1, 8, q_rows), axis=0)
+            for total, dest in zip(sums, dests)
+        ]
+
+    sums = [jnp.zeros((8, q_rows), F32) for _ in range(COLD)]
+    sums = lax.fori_loop(0, found_ref.shape[0] // chunk, score, sums)
+    cold_ref[...] = jnp.concatenate([jnp.sum(total, axis=0, keepdims=True) for total in sums], axis=0)
 
 
 def count_kernel(cand_t, teacher_ref, hot_ref, sel_ref, count_ref, target_ref, misc_ref, soft_t):
@@ -187,67 +199,66 @@
         target_ref[a * LANES : (a + 1) * LANES, :] = total
 
 
-def score_kernel(scale, q_ref, hot_ref, cold_ref, count_ref, target_ref, place_ref, misc_ref, loss_ref, pay_ref, weight_ref, hot_scr, top_scr, slot_scr):
-    step = pl.program_id(0)
-    each, hot_each, feat = hot_ref.shape
+def score_kernel(scale, spot_ref, q_ref, *refs):
+    score_body(scale, spot_ref, q_ref, refs[:PIECES], *refs[PIECES:])
+
+
+def score_body(scale, spot_ref, q_ref, hot_refs, cold_ref, count_ref, target_ref, place_ref, misc_ref, loss_ref, pay_ref, weight_ref, hot_scr, slot_scr):
     groups = pay_ref.shape[0]
     q_rows = q_ref.shape[0]
-    size = each * hot_each
-
-    @pl.when(step == 0)
-    def _():
-        top_scr[...] = jnp.max(cold_ref[...], axis=0, keepdims=True)
-
-    got = scale * lax.dot_general(hot_ref[...].reshape(size, feat), q_ref[...], ROWS_DOT, preferred_element_type=F32)
-    hot_scr[pl.ds(pl.multiple_of(step * size, size), size), :] = got
-    top_scr[...] = jnp.maximum(top_scr[...], jnp.max(got, axis=0, keepdims=True))
-
-    @pl.when(step == pl.num_programs(0) - 1)
-    def _():
-        cold = cold_ref[...]
-        top = top_scr[...]
-        place = place_ref[...]
-        total = jnp.sum(jnp.exp(cold - top), axis=0, keepdims=True)
-        hot_dot = jnp.zeros((1, q_rows), F32)
-        for j in range(groups // 8):
-            part = slice(j * 8 * hot_each, (j + 1) * 8 * hot_each)
-            hot = hot_scr[part, :]
-            total = total + jnp.sum(count_ref[part, :] * jnp.exp(hot - top), axis=0, keepdims=True)
-            hot_dot = hot_dot + jnp.sum(target_ref[part, :] * hot, axis=0, keepdims=True)
-        log_total = top + jnp.log(total)
-        cold_target = misc_ref[0:COLD, :]
-        entropy = misc_ref[COLD : COLD + 1, :]
-        loss_ref[...] = entropy - hot_dot - jnp.sum(cold_target * cold, axis=0, keepdims=True) + log_total
-        weight = (jnp.exp(cold - log_total) - cold_target).astype(BF16).astype(F32)
-        weight_ref[...] = weight
-        owner_iota = iota((groups, q_rows), 0)
-        slot_iota = iota((LANES, q_rows), 0)
-        owner_all = jnp.concatenate([one_hot(owner_iota == place[r : r + 1]) for r in range(COLD)], axis=1)
-        slot_all = jnp.concatenate(
-            [
-                jnp.where(slot_iota == place[COLD + r : COLD + r + 1], weight[r : r + 1], 0.0).astype(BF16)
-                for r in range(COLD)
-            ],
-            axis=1,
-        )
-        slot_scr[...] = lax.dot_general(owner_all, slot_all, ROWS_DOT, preferred_element_type=F32)
-        for g in range(groups):
-            part = slice(g * hot_each, (g + 1) * hot_each)
-            coef = count_ref[part, :] * jnp.exp(hot_scr[part, :] - log_total) - target_ref[part, :]
-            slot_row = jnp.broadcast_to(slot_scr[g : g + 1, :], (8, q_rows))
-            pay_ref[g] = jnp.concatenate([coef, slot_row], axis=0).astype(BF16)
-
-
-def query_kernel(scale, capacity, hot_ref, pay_ref, found_ref, weight_ref, place_ref, out_ref):
-    groups, hot_each, feat = hot_ref.shape
+    hot_each = hot_scr.shape[0] // groups
+    q = q_ref[...]
+    top = jnp.max(cold_ref[...], axis=0, keepdims=True)
+    for piece, hot_ref in enumerate(hot_refs):
+        got = scale * lax.dot_general(hot_ref[...], q, ROWS_DOT, preferred_element_type=F32)
+        for d in range(Z_SIZE):
+            start = pl.multiple_of(owner_of(spot_ref, piece, d) * hot_each, hot_each)
+            hot_scr[pl.ds(start, hot_each), :] = got[d * hot_each : (d + 1) * hot_each]
+        top = jnp.maximum(top, jnp.max(got, axis=0, keepdims=True))
+    cold = cold_ref[...]
+    place = place_ref[...]
+    total = jnp.sum(jnp.exp(cold - top), axis=0, keepdims=True)
+    hot_dot = jnp.zeros((1, q_rows), F32)
+    for j in range(groups // 8):
+        part = slice(j * 8 * hot_each, (j + 1) * 8 * hot_each)
+        hot = hot_scr[part, :]
+        total = total + jnp.sum(count_ref[part, :] * jnp.exp(hot - top), axis=0, keepdims=True)
+        hot_dot = hot_dot + jnp.sum(target_ref[part, :] * hot, axis=0, keepdims=True)
+    log_total = top + jnp.log(total)
+    cold_target = misc_ref[0:COLD, :]
+    entropy = misc_ref[COLD : COLD + 1, :]
+    loss_ref[...] = entropy - hot_dot - jnp.sum(cold_target * cold, axis=0, keepdims=True) + log_total
+    weight = (jnp.exp(cold - log_total) - cold_target).astype(BF16).astype(F32)
+    weight_ref[...] = weight
+    owner_iota = iota((groups, q_rows), 0)
+    slot_iota = iota((LANES, q_rows), 0)
+    owner_all = jnp.concatenate([one_hot(owner_iota == place[r : r + 1]) for r in range(COLD)], axis=1)
+    slot_all = jnp.concatenate(
+        [
+            jnp.where(slot_iota == place[COLD + r : COLD + r + 1], weight[r : r + 1], 0.0).astype(BF16)
+            for r in range(COLD)
+        ],
+        axis=1,
+    )
+    slot_scr[...] = lax.dot_general(owner_all, slot_all, ROWS_DOT, preferred_element_type=F32)
+    for g in range(groups):
+        part = slice(g * hot_each, (g + 1) * hot_each)
+        coef = count_ref[part, :] * jnp.exp(hot_scr[part, :] - log_total) - target_ref[part, :]
+        slot_row = jnp.broadcast_to(slot_scr[g : g + 1, :], (8, q_rows))
+        pay_ref[g] = jnp.concatenate([coef, slot_row], axis=0).astype(BF16)
+
+
+def query_kernel(scale, capacity, spot_ref, *refs):
+    hot_refs = refs[:PIECES]
+    pay_ref, found_ref, weight_ref, place_ref, out_ref = refs[PIECES:]
     q_rows = out_ref.shape[0]
+    hot_each = hot_refs[0].shape[0] // Z_SIZE
     acc = jnp.zeros(out_ref.shape, F32)
-    step = 8
     first = (((0,), (0,)), ((), ()))
-    for j in range(groups // step):
-        rows = hot_ref[j * step : (j + 1) * step].reshape(step * hot_each, feat)
-        coef = jnp.concatenate([pay_ref[j * step + n, 0:hot_each, :] for n in range(step)], axis=0)
-        acc = acc + lax.dot_general(coef, rows, first, preferred_element_type=F32)
+    for piece, hot_ref in enumerate(hot_refs):
+        owners = [owner_of(spot_ref, piece, d) for d in range(Z_SIZE)]
+        coef = jnp.concatenate([pay_ref[o, 0:hot_each, :] for o in owners], axis=0)
+        acc = acc + lax.dot_general(coef, hot_ref[...], first, preferred_element_type=F32)
     chunk = 256
     place = place_ref[...]
     weight = weight_ref[...]
@@ -305,15 +316,49 @@
         second_ref[...] = got[rows:]
 
 
-def near_kernel(reps, spot_ref, terms_ref, loc_ref, *outs):
-    rows = outs[0].shape[0]
+def near_kernel(reps, shifts, spot_ref, terms_ref, loc_ref, out_ref):
+    rows = out_ref.shape[0] // len(shifts)
     loc = loc_ref[...]
     ids = iota((rows, loc.shape[1]), 0)
-    starts = [(spot_ref[1] + d) % reps * rows for d in (0, 1, reps - 1)]
+    starts = [(spot_ref[1] + d) % reps * rows for d in shifts]
     at = jnp.concatenate([one_hot(ids + start == loc) for start in starts], axis=0)
-    got = jnp.dot(at, terms_ref[...], preferred_element_type=F32)
-    for n, out in enumerate(outs):
-        out[...] = got[n * rows : (n + 1) * rows]
+    out_ref[...] = jnp.dot(at, terms_ref[...], preferred_element_type=F32)
+
+
+def stack_kernel(*refs):
+    out_ref = refs[-1]
+    size = refs[0].shape[0]
+    for n, ref in enumerate(refs[:-1]):
+        out_ref[n * size : (n + 1) * size, :] = ref[...]
+
+
+def merge_kernel(near_ref, first_ref, second_ref, after_ref, before_ref):
+    half = first_ref.shape[0]
+    after_ref[0:half, :] = (near_ref[0:half, :] + first_ref[...].astype(F32)).astype(BF16)
+    after_ref[half:, :] = near_ref[half : 2 * half, :].astype(BF16)
+    before_ref[0:half, :] = near_ref[2 * half : 3 * half, :].astype(BF16)
+    before_ref[half:, :] = (near_ref[3 * half :, :] + second_ref[...].astype(F32)).astype(BF16)
+
+
+def gather_hot(rows):
+    def member(x, z, core):
+        return (x % X_SIZE * Z_SIZE + z % Z_SIZE) * CORES + core % CORES
+
+    spots = [(x, z, c) for x in range(X_SIZE) for z in range(Z_SIZE) for c in range(CORES)]
+
+    def shift(array, dx, dz, dc):
+        return lax.ppermute(array, "corpus", [(member(x, z, c), member(x + dx, z + dz, c + dc)) for x, z, c in spots])
+
+    pieces = [rows] + [shift(rows, 0, d, 0) for d in range(1, Z_SIZE)]
+    rows = pl.pallas_call(
+        stack_kernel,
+        out_shape=jax.ShapeDtypeStruct((Z_SIZE * rows.shape[0], rows.shape[1]), BF16),
+        in_specs=[VMEM_SPEC] * Z_SIZE,
+        out_specs=VMEM_SPEC,
+        name="stack",
+    )(*pieces)
+    pieces = [rows] + [shift(rows, d, 0, 0) for d in range(1, X_SIZE)]
+    return pieces + [shift(p, 0, 0, 1) for p in pieces]
 
 
 def shards(queries, teacher, slab, candidates, hot_ids, location):
@@ -331,6 +376,7 @@
     spot = jnp.stack([corpus_idx, rep_idx]).astype(jnp.int32)
     loc_table = location.reshape(-1, LANES)
     hot_table = hot_ids.reshape(-1, LANES)
+    gathered = lax.all_gather(queries, "corpus", axis=0, tiled=False)
     cand_t = candidates.T
     req, place, sel = pl.pallas_call(
         functools.partial(request_kernel, per_owner, groups),
@@ -344,15 +390,15 @@
         scratch_shapes=[pltpu.VMEM((cand_count, q_rows), F32)],
         name="request",
     )(cand_t, hot_ids.reshape(1, hot_total), loc_table)
-    sent_rows = pl.pallas_call(
+    own_rows = pl.pallas_call(
         functools.partial(prep_kernel, per_owner),
-        out_shape=jax.ShapeDtypeStruct((q_rows + hot_each, feat), BF16),
-        in_specs=[SMEM_SPEC] + [VMEM_SPEC] * 4,
+        out_shape=jax.ShapeDtypeStruct((hot_each, feat), BF16),
+        in_specs=[SMEM_SPEC] + [VMEM_SPEC] * 3,
         out_specs=VMEM_SPEC,
         scratch_shapes=[pltpu.VMEM((LANES, LANES), F32)],
         name="prep",
-    )(spot, queries, hot_table, loc_table, slab)
-    gathered = lax.all_gather(sent_rows, "corpus", axis=0, tiled=False)
+    )(spot, hot_table, loc_table, slab)
+    hot_rows = gather_hot(own_rows)
     asked = lax.all_to_all(req.reshape(groups, 1, LANES), "corpus", split_axis=0, concat_axis=0, tiled=True)
     asked = asked.reshape(groups, LANES)
     slots = groups * capacity
@@ -381,7 +427,6 @@
         cost_estimate=pl.CostEstimate(flops=80_000_000, bytes_accessed=3_000_000, transcendentals=10_000),
         name="count",
     )(cand_t, teacher.T, hot_table, sel)
-    hot_block = pl.BlockSpec((groups, hot_each, feat), lambda i: (0, q_rows // hot_each, 0))
 
     def whole(shape):
         return pl.BlockSpec(shape, lambda i: (0,) * len(shape))
@@ -394,44 +439,29 @@
         out_specs=VMEM_SPEC,
         name="cold",
     )(queries, found, place)
-    each = 8
     loss, pay, weight = pl.pallas_call(
         functools.partial(score_kernel, scale),
-        grid=(groups // each,),
         out_shape=(
             jax.ShapeDtypeStruct((1, q_rows), F32),
             jax.ShapeDtypeStruct((groups, pay_rows, q_rows), BF16),
             jax.ShapeDtypeStruct((COLD, q_rows), F32),
         ),
-        in_specs=[
-            whole((q_rows, feat)),
-            pl.BlockSpec((each, hot_each, feat), lambda i: (i, q_rows // hot_each, 0)),
-            whole((COLD, q_rows)),
-            whole((hot_total, q_rows)),
-            whole((hot_total, q_rows)),
-            whole((2 * COLD, q_rows)),
-            whole((2 * COLD, q_rows)),
-        ],
-        out_specs=(whole((1, q_rows)), whole((groups, pay_rows, q_rows)), whole((COLD, q_rows))),
-        scratch_shapes=[
-            pltpu.VMEM((hot_total, q_rows), F32),
-            pltpu.VMEM((1, q_rows), F32),
-            pltpu.VMEM((groups, q_rows), F32),
-        ],
+        in_specs=[SMEM_SPEC] + [VMEM_SPEC] * (PIECES + 6),
+        out_specs=(VMEM_SPEC,) * 3,
+        scratch_shapes=[pltpu.VMEM((hot_total, q_rows), F32), pltpu.VMEM((groups, q_rows), F32)],
         name="score",
-    )(queries, gathered, cold, count, target, place, misc)
+    )(spot, queries, *hot_rows, cold, count, target, place, misc)
     got = lax.all_to_all(pay, "corpus", split_axis=0, concat_axis=0, tiled=True)
     query_grad = pl.pallas_call(
         functools.partial(query_kernel, scale, capacity),
-        grid=(1,),
         out_shape=jax.ShapeDtypeStruct((q_rows, feat), F32),
-        in_specs=[hot_block, whole((groups, pay_rows, q_rows)), whole((slots, feat)), whole((COLD, q_rows)), whole((2 * COLD, q_rows))],
-        out_specs=whole((q_rows, feat)),
+        in_specs=[SMEM_SPEC] + [VMEM_SPEC] * (PIECES + 4),
+        out_specs=VMEM_SPEC,
         cost_estimate=pl.CostEstimate(flops=700_000_000, bytes_accessed=7_000_000, transcendentals=0),
         name="query_grad",
-    )(gathered, pay, found, weight, place)
+    )(spot, *hot_rows, pay, found, weight, place)
     padded = asked[:, :capacity]
-    source = jnp.arange(groups, dtype=jnp.int32)[:, None] * (q_rows + hot_each)
+    source = jnp.arange(groups, dtype=jnp.int32)[:, None] * q_rows
     query_rows = gathered.reshape(-1, feat)[(source + jnp.maximum(padded, 0) // per_owner).reshape(-1)]
     local = jnp.where(padded >= 0, padded & (per_owner - 1), -1).reshape(1, -1)
     mine = lax.dynamic_slice_in_dim(hot_ids, corpus_idx * hot_each, hot_each)
@@ -461,19 +491,27 @@
     behind = [(r, (r - 1) % reps) for r in range(reps)]
     first = lax.ppermute(first, "rep", ahead)
     second = lax.ppermute(second, "rep", behind)
-    own, after, before = pl.pallas_call(
-        functools.partial(near_kernel, reps),
-        out_shape=(jax.ShapeDtypeStruct((rows, feat), F32),) * 3,
-        in_specs=[SMEM_SPEC, VMEM_SPEC, VMEM_SPEC],
-        out_specs=(VMEM_SPEC,) * 3,
-        cost_estimate=pl.CostEstimate(flops=2_000_000_000, bytes_accessed=6_000_000, transcendentals=0),
-        name="near",
-    )(spot, terms, local)
-    after = (after + jnp.pad(first.astype(F32), ((0, rows // 2), (0, 0)))).astype(BF16)
-    before = (before + jnp.pad(second.astype(F32), ((rows // 2, 0), (0, 0)))).astype(BF16)
+
+    def land(shifts):
+        return pl.pallas_call(
+            functools.partial(near_kernel, reps, shifts),
+            out_shape=jax.ShapeDtypeStruct((len(shifts) * rows, feat), F32),
+            in_specs=[SMEM_SPEC, VMEM_SPEC, VMEM_SPEC],
+            out_specs=VMEM_SPEC,
+            cost_estimate=pl.CostEstimate(flops=2_000_000_000, bytes_accessed=6_000_000, transcendentals=0),
+        )(spot, terms, local)
+
+    near = land((1, reps - 1))
+    after, before = pl.pallas_call(
+        merge_kernel,
+        out_shape=(jax.ShapeDtypeStruct((rows, feat), BF16),) * 2,
+        in_specs=[VMEM_SPEC] * 3,
+        out_specs=(VMEM_SPEC,) * 2,
+        name="merge",
+    )(near, first, second)
     after = lax.ppermute(after, "rep", ahead)
     before = lax.ppermute(before, "rep", behind)
-    slab_grad = own + after.astype(F32) + before.astype(F32)
+    slab_grad = land((0,)) + after.astype(F32) + before.astype(F32)
     return (loss.reshape(q_rows), query_grad, slab_grad)
 
 

time: 225 us -> 260 us (1.16)
  starting transfers between devices: 21.4 us -> 39.1 us
  waiting for transfers between devices: 80 us -> 92.2 us
  Pallas kernels: 66.2 us -> 71 us
    ppermute x0 -> x14, waiting for transfers between devices: none -> 82.5 us  [shift(): lax.ppermute(array, 'corpus', [(member(x, z, c), member(x + dx, z + dz, c...]
    all_to_all x1, waiting for transfers between devices: 53 us -> 0.01 us  [shards(): lax.all_to_all(wanted.reshape(groups, capacity, feat), 'corpus', split_ax...]
    ppermute x0 -> x14, starting transfers between devices: none -> 18.8 us  [shift(): lax.ppermute(array, 'corpus', [(member(x, z, c), member(x + dx, z + dz, c...]
    all_gather x1, waiting for transfers between devices: 17 us -> 0.01 us  [shards(): gathered = lax.all_gather(queries, 'corpus', axis=0, tiled=False)]
    pallas_call x3 -> x6, Pallas kernels: 17.9 us -> 21.8 us  [the longest x2 7.99 us: land(): pl.pallas_call(functools.partial(near_kernel, reps, shifts), out_shape=ja...]
    unnamed x10 -> x32, local copies, waits for them, and re-layouts: 2.22 us -> 4.82 us
  transfers between devices with their start and end apart: 7 -> 21, of which waited for: 6 -> 10; matrix products, arithmetic and copies ran while one was open for 8% -> 6% of each run, Pallas kernels for 20% -> 22%
where the time goes in v4:
time: 260 us; the launch traced here: 259 us
  waiting for transfers between devices  92.2 us (35%)
  Pallas kernels  71 us (27%)
  starting transfers between devices  39.1 us (15%)
  blocking collectives  19.7 us (8%)
  local copies, waits for them, and re-layouts  18.6 us (7%)
  between operations  14.2 us (5%)
  other arithmetic  4.29 us (2%)
    ppermute x14, waiting for transfers between devices, shift(): lax.ppermute(array, 'corpus', [(member(x, z, c), member(x + dx, z + dz, c...  82.5 us
    all_to_all x1, blocking collectives, shards(): lax.all_to_all(req.reshape(groups, 1, LANES), 'corpus', split_axis=0, con...  19.7 us
    ppermute x14, starting transfers between devices, shift(): lax.ppermute(array, 'corpus', [(member(x, z, c), member(x + dx, z + dz, c...  18.8 us
    pallas_call x1, Pallas kernels, shards(): pl.pallas_call(count_kernel, out_shape=(jax.ShapeDtypeStruct((hot_total,...  18.6 us
    gather x1, local copies, waits for them, and re-layouts, shards(): gathered.reshape(-1, feat)  12.9 us
    pallas_call x1, Pallas kernels, shards(): pl.pallas_call(functools.partial(slab_kernel, scale, capacity, reps), gri...  11.1 us
    all_to_all x1, starting transfers between devices, shards(): got = lax.all_to_all(pay, 'corpus', split_axis=0, concat_axis=0, tiled=True)  8.09 us
    pallas_call x2, Pallas kernels, land(): pl.pallas_call(functools.partial(near_kernel, reps, shifts), out_shape=ja...  7.99 us
  transfers between devices with their start and end apart: 21, of which 10 were waited for; matrix products, arithmetic and copies ran while one was open for 6% of the time, Pallas kernels for 22%

profile of v4, /device:TPU:6, one launch (start us, length us, event | category | flops | bytes accessed | tf_op | source)
XLA Modules:
  0.0 259.0 jit_solution(14383066689843138452)
XLA Ops:
  7.9 6.2 %request.1 = (s32[64,128]{1,0:T(8,128)}, s32[16,128]{1,0:T(8,128)}, s32[64,128]{1,0:T(8,128)}) custom-call(s32[64,128]{1,0:T(8,128)} %bitcast.28, s32[1,2048]{1,0:T(1,128)} %bitcast.25, s32[512,128]{1,0:T(8,128)} %bitcast.21), custom_call_target="tpu_custom_call" | custom-call | tf_op jit(solution)/shard_map/request/pallas_call | solution.py:381
  14.1 19.7 %all_to_all.15 = s32[64,1,128]{2,1,0:T(1,128)} all-to-all(s32[64,1,128]{2,1,0:T(1,128)} %bitcast.30), channel_id=1, replica_groups=mesh['corpus'=64,'rep'=4] {'corpus'}, dimensions={0} | all-to-all | bytes 65536 | tf_op jit(solution)/shard_map/all_to_all | solution.py:402
  33.8 5.9 %fetch.1 = bf16[1536,768]{1,0:T(8,128)(2,1)} custom-call(s32[64,128]{1,0:T(8,128)} %bitcast.23, bf16[1024,768]{1,0:T(8,128)(2,1)} %slab_ref.3), custom_call_target="tpu_custom_call" | custom-call | tf_op jit(solution)/shard_map/fetch/pallas_call | solution.py:406
  39.7 6.6 %all-to-all-start.1 = ((bf16[64,24,768]{2,1,0:T(8,128)(2,1)}), bf16[64,24,768]{2,1,0:T(8,128)(2,1)S(1)}, u32[]{:S(2)}, u32[]{:S(2)}) async-start(bf16[64,24,768]{2,1,0:T(8,128)(2,1)} %bitcast.20), calls=%async_computation.1 | async-start | bytes 4718592 | tf_op jit(solution)/shard_map/all_to_all | solution.py:415
  47.0 3.1 %prep.1.refs_0_ = bf16[32,768]{1,0:T(8,128)(2,1)} custom-call(s32[2]{0:T(128)} %pad_add_fusion.1.spot_ref, s32[16,128]{1,0:T(8,128)} %bitcast.26, s32[512,128]{1,0:T(8,128)} %bitcast.22, bf16[1024,768]{1,0:T(8,128)(2,1)} %slab_ref.3), custom_call_target="tpu_custom_call" | custom-call | tf_op jit(solution)/shard_map/prep/pallas_call | solution.py:393
  53.9 2.7 %collective-permute-start.2 = (bf16[32,768]{1,0:T(8,128)(2,1)}, bf16[32,768]{1,0:T(8,128)(2,1)S(1)}, u32[]{:S(2)}, u32[]{:S(2)}) collective-permute-start(bf16[32,768]{1,0:T(8,128)(2,1)} %prep.1.refs_0_), channel_id=1, source_target_pairs={{0,24},{4,28},{8,32},{12,36},{16,40},{20,44},{24,48},{28,52},{32,5... | collective-permute-start | bytes 147464 | tf_op jit(solution)/shard_map/ppermute | solution.py:350
  58.9 2.7 %collective-permute-start.4 = (bf16[32,768]{1,0:T(8,128)(2,1)}, bf16[32,768]{1,0:T(8,128)(2,1)S(1)}, u32[]{:S(2)}, u32[]{:S(2)}) collective-permute-start(bf16[32,768]{1,0:T(8,128)(2,1)} %prep.1.refs_0_), channel_id=1, source_target_pairs={{0,40},{4,44},{8,48},{12,52},{16,56},{20,60},{24,0},{28,4},{32,8},... | collective-permute-start | bytes 147464 | tf_op jit(solution)/shard_map/ppermute | solution.py:350
  61.6 55.7 %collective-permute-done.refs_1_ = bf16[32,768]{1,0:T(8,128)(2,1)S(1)} collective-permute-done((bf16[32,768]{1,0:T(8,128)(2,1)}, bf16[32,768]{1,0:T(8,128)(2,1)S(1)}, u32[]{:S(2)}, u32[]{:S(2)}) %collective-permute-start) | collective-permute-done | bytes 49184 | tf_op jit(solution)/shard_map/ppermute | solution.py:350
  117.4 4.5 %collective-permute-start.5 = (bf16[32,768]{1,0:T(8,128)(2,1)}, bf16[32,768]{1,0:T(8,128)(2,1)S(1)}, u32[]{:S(2)}, u32[]{:S(2)}) collective-permute-start(bf16[32,768]{1,0:T(8,128)(2,1)} %prep.1.refs_0_), channel_id=1, source_target_pairs={{0,48},{4,52},{8,56},{12,60},{16,0},{20,4},{24,8},{28,12},{32,16},... | collective-permute-start | bytes 147464 | tf_op jit(solution)/shard_map/ppermute | solution.py:350
  124.8 6.7 %collective-permute-done.3.refs_4_ = bf16[32,768]{1,0:T(8,128)(2,1)S(1)} collective-permute-done((bf16[32,768]{1,0:T(8,128)(2,1)}, bf16[32,768]{1,0:T(8,128)(2,1)S(1)}, u32[]{:S(2)}, u32[]{:S(2)}) %collective-permute-start.3) | collective-permute-done | bytes 49184 | tf_op jit(solution)/shard_map/ppermute | solution.py:350
  136.8 10.0 %collective-permute-done.7.refs_1_ = bf16[256,768]{1,0:T(8,128)(2,1)S(1)} collective-permute-done((bf16[256,768]{1,0:T(8,128)(2,1)}, bf16[256,768]{1,0:T(8,128)(2,1)S(1)}, u32[]{:S(2)}, u32[]{:S(2)}) %collective-permute-start.7) | collective-permute-done | bytes 393248 | tf_op jit(solution)/shard_map/ppermute | solution.py:350
  149.1 5.3 %collective-permute-done.9.refs_3_ = bf16[256,768]{1,0:T(8,128)(2,1)S(1)} collective-permute-done((bf16[256,768]{1,0:T(8,128)(2,1)}, bf16[256,768]{1,0:T(8,128)(2,1)S(1)}, u32[]{:S(2)}, u32[]{:S(2)}) %collective-permute-start.9) | collective-permute-done | bytes 393248 | tf_op jit(solution)/shard_map/ppermute | solution.py:350
  154.4 18.6 %count.1 = (f32[2048,128]{1,0:T(8,128)}, f32[2048,128]{1,0:T(8,128)}, f32[16,128]{1,0:T(8,128)}) custom-call(s32[64,128]{1,0:T(8,128)} %bitcast.29, f32[64,128]{1,0:T(8,128)} %bitcast.31, s32[16,128]{1,0:T(8,128)} %bitcast.27, s32[64,128]{1,0:T(8,128)} %get-tuple-element.19.sel_ref), custom_call_target="tpu_custom_call" | custom-call | flops 80000000 | bytes 3000000 | tf_op jit(solution)/shard_map/count/pallas_call | solution.py:417
  174.4 4.2 %cold.1.refs_8_ = f32[8,128]{1,0:T(8,128)} custom-call(bf16[128,768]{1,0:T(8,128)(2,1)} %q_ref.3, bf16[1536,768]{1,0:T(8,128)(2,1)} %bitcast.18, s32[16,128]{1,0:T(8,128)} %get-tuple-element.18.place_ref.refs_11_), custom_call_target="tpu_custom_call" | custom-call | tf_op jit(solution)/shard_map/cold/pallas_call | solution.py:435
  178.7 5.1 %score.1 = (f32[1,128]{1,0:T(1,128)}, bf16[64,40,128]{2,1,0:T(8,128)(2,1)}, f32[8,128]{1,0:T(8,128)}) custom-call(s32[2]{0:T(128)} %pad_add_fusion.1.spot_ref, bf16[128,768]{1,0:T(8,128)(2,1)} %q_ref.3, bf16[256,768]{1,0:T(8,128)(2,1)} %stack.13.refs_0_, bf16[256,768]{1,0:T(8,128)(2,1)} %copy-done.3, bf16[256,768]{1,0:T(8,128)(2,1)} %copy-done.4, ...), custom_call_target="tpu_custom_call" | custom-call | tf_op jit(solution)/shard_map/score/pallas_call | solution.py:442
  183.7 8.1 %all-to-all-start.2 = ((bf16[64,40,128]{2,1,0:T(8,128)(2,1)}), bf16[64,40,128]{2,1,0:T(8,128)(2,1)S(1)}, u32[]{:S(2)}, u32[]{:S(2)}) async-start(bf16[64,40,128]{2,1,0:T(8,128)(2,1)} %get-tuple-element.24.refs_8_), calls=%async_computation.2 | async-start | bytes 1310720 | tf_op jit(solution)/shard_map/all_to_all | solution.py:454
  194.3 12.9 %gather_fusion = bf16[1536,768]{1,0:T(8,128)(2,1)} fusion(bf16[8192,768]{1,0:T(8,128)(2,1)} %all-gather.3.cloned.1.call-done, s32[2048]{0:T(1024)S(1)} %pad_clamp_fusion), kind=kCustom, calls=%fused_computation | custom fusion | bytes 4724736 | tf_op jit(solution)/shard_map/gather | solution.py:465
  207.2 3.9 %all-to-all-done.2.pay_ref = bf16[64,40,128]{2,1,0:T(8,128)(2,1)S(1)} async-done(((bf16[64,40,128]{2,1,0:T(8,128)(2,1)}), bf16[64,40,128]{2,1,0:T(8,128)(2,1)S(1)}, u32[]{:S(2)}, u32[]{:S(2)}) %all-to-all-start.2) | async-done | bytes 655392 | tf_op jit(solution)/shard_map/all_to_all | solution.py:454
  212.0 11.1 %slab_grad.1 = (bf16[128,768]{1,0:T(8,128)(2,1)}, bf16[128,768]{1,0:T(8,128)(2,1)}, bf16[1664,768]{1,0:T(8,128)(2,1)}) custom-call(s32[2]{0:T(128)} %pad_add_fusion.1.spot_ref, bf16[64,40,128]{2,1,0:T(8,128)(2,1)} %copy-done.2, bf16[64,128,768]{2,1,0:T(8,128)(2,1)} %bitcast.17, bf16[1536,768]{1,0:T(8,128)(2,1)} %gather_fusion, s32[1,1664]{1,0:T(1,128)} %pad_add_fusion.loc_ref), custom_call_target="tpu_custom_call" | custom-call | tf_op jit(solution)/shard_map/slab_grad/pallas_call | solution.py:475
  226.3 4.5 %shard_map.86.near_ref = f32[512,768]{1,0:T(8,128)} custom-call(s32[2]{0:T(128)} %pad_add_fusion.1.spot_ref, bf16[1664,768]{1,0:T(8,128)(2,1)} %get-tuple-element.26.terms_ref, s32[1,1664]{1,0:T(1,128)} %pad_add_fusion.loc_ref), custom_call_target="tpu_custom_call" | custom-call | flops 2000000000 | bytes 6000000 | tf_op jit(solution)/shard_map/pallas_call | solution.py:496
  233.5 2.5 merge.1
  238.2 4.5 %query_grad.1 = f32[128,768]{1,0:T(8,128)} custom-call(s32[2]{0:T(128)} %pad_add_fusion.1.spot_ref, bf16[256,768]{1,0:T(8,128)(2,1)} %stack.13.refs_0_, bf16[256,768]{1,0:T(8,128)(2,1)} %copy-done.3, bf16[256,768]{1,0:T(8,128)(2,1)} %copy-done.4, bf16[256,768]{1,0:T(8,128)(2,1)} %copy-done.5, bf16[256,768]{1,0:T(8,128)(2,1)} %collective-permute-done.10.refs_4_, ...), custom_call_target="tpu_custom_call" | custom-call | flops 700000000 | bytes 7000000 | tf_op jit(solution)/shard_map/query_grad/pallas_call | solution.py:455
  242.7 3.5 %shard_map.85 = f32[256,768]{1,0:T(8,128)} custom-call(s32[2]{0:T(128)} %pad_add_fusion.1.spot_ref, bf16[1664,768]{1,0:T(8,128)(2,1)} %get-tuple-element.26.terms_ref, s32[1,1664]{1,0:T(1,128)} %pad_add_fusion.loc_ref), custom_call_target="tpu_custom_call" | custom-call | flops 2000000000 | bytes 6000000 | tf_op jit(solution)/shard_map/pallas_call | solution.py:496
  247.1 2.9 %collective-permute-done.16 = bf16[256,768]{1,0:T(8,128)(2,1)S(1)} collective-permute-done((bf16[256,768]{1,0:T(8,128)(2,1)}, bf16[256,768]{1,0:T(8,128)(2,1)S(1)}, u32[]{:S(2)}, u32[]{:S(2)}) %collective-permute-start.16) | collective-permute-done | bytes 393248 | tf_op jit(solution)/shard_map/ppermute | solution.py:512
  (80 shorter events, 33.9 us)
Async XLA Ops:
  7.2 187.2 %all-gather.3.cloned.1.call-start = ((), (), s32[]{:S(2)}) async-start(), calls=%async_computation.3 | async-start | bytes 12779520 | tf_op jit(solution)/shard_map/all_gather | solution.py:379
  39.7 133.2 %all-to-all-start.1 = ((bf16[64,24,768]{2,1,0:T(8,128)(2,1)}), bf16[64,24,768]{2,1,0:T(8,128)(2,1)S(1)}, u32[]{:S(2)}, u32[]{:S(2)}) async-start(bf16[64,24,768]{2,1,0:T(8,128)(2,1)} %bitcast.20), calls=%async_computation.1 | async-start | bytes 4718592 | tf_op jit(solution)/shard_map/all_to_all | solution.py:415
  50.0 67.4 %collective-permute-start = (bf16[32,768]{1,0:T(8,128)(2,1)}, bf16[32,768]{1,0:T(8,128)(2,1)S(1)}, u32[]{:S(2)}, u32[]{:S(2)}) collective-permute-start(bf16[32,768]{1,0:T(8,128)(2,1)} %prep.1.refs_0_), channel_id=1, source_target_pairs={{0,8},{4,12},{8,16},{12,20},{16,24},{20,28},{24,32},{28,36},{32,40... | collective-permute-start | bytes 147464 | tf_op jit(solution)/shard_map/ppermute | solution.py:350
  51.5 72.8 %collective-permute-start.1 = (bf16[32,768]{1,0:T(8,128)(2,1)}, bf16[32,768]{1,0:T(8,128)(2,1)S(1)}, u32[]{:S(2)}, u32[]{:S(2)}) collective-permute-start(bf16[32,768]{1,0:T(8,128)(2,1)} %prep.1.refs_0_), channel_id=1, source_target_pairs={{0,16},{4,20},{8,24},{12,28},{16,32},{20,36},{24,40},{28,44},{32,4... | collective-permute-start | bytes 147464 | tf_op jit(solution)/shard_map/ppermute | solution.py:350
  53.9 70.9 %collective-permute-start.2 = (bf16[32,768]{1,0:T(8,128)(2,1)}, bf16[32,768]{1,0:T(8,128)(2,1)S(1)}, u32[]{:S(2)}, u32[]{:S(2)}) collective-permute-start(bf16[32,768]{1,0:T(8,128)(2,1)} %prep.1.refs_0_), channel_id=1, source_target_pairs={{0,24},{4,28},{8,32},{12,36},{16,40},{20,44},{24,48},{28,52},{32,5... | collective-permute-start | bytes 147464 | tf_op jit(solution)/shard_map/ppermute | solution.py:350
  56.6 74.9 %collective-permute-start.3 = (bf16[32,768]{1,0:T(8,128)(2,1)}, bf16[32,768]{1,0:T(8,128)(2,1)S(1)}, u32[]{:S(2)}, u32[]{:S(2)}) collective-permute-start(bf16[32,768]{1,0:T(8,128)(2,1)} %prep.1.refs_0_), channel_id=1, source_target_pairs={{0,32},{4,36},{8,40},{12,44},{16,48},{20,52},{24,56},{28,60},{32,0... | collective-permute-start | bytes 147464 | tf_op jit(solution)/shard_map/ppermute | solution.py:350
  58.9 72.6 %collective-permute-start.4 = (bf16[32,768]{1,0:T(8,128)(2,1)}, bf16[32,768]{1,0:T(8,128)(2,1)S(1)}, u32[]{:S(2)}, u32[]{:S(2)}) collective-permute-start(bf16[32,768]{1,0:T(8,128)(2,1)} %prep.1.refs_0_), channel_id=1, source_target_pairs={{0,40},{4,44},{8,48},{12,52},{16,56},{20,60},{24,0},{28,4},{32,8},... | collective-permute-start | bytes 147464 | tf_op jit(solution)/shard_map/ppermute | solution.py:350
  117.4 14.1 %collective-permute-start.5 = (bf16[32,768]{1,0:T(8,128)(2,1)}, bf16[32,768]{1,0:T(8,128)(2,1)S(1)}, u32[]{:S(2)}, u32[]{:S(2)}) collective-permute-start(bf16[32,768]{1,0:T(8,128)(2,1)} %prep.1.refs_0_), channel_id=1, source_target_pairs={{0,48},{4,52},{8,56},{12,60},{16,0},{20,4},{24,8},{28,12},{32,16},... | collective-permute-start | bytes 147464 | tf_op jit(solution)/shard_map/ppermute | solution.py:350
  124.3 7.2 %collective-permute-start.6 = (bf16[32,768]{1,0:T(8,128)(2,1)}, bf16[32,768]{1,0:T(8,128)(2,1)S(1)}, u32[]{:S(2)}, u32[]{:S(2)}) collective-permute-start(bf16[32,768]{1,0:T(8,128)(2,1)} %prep.1.refs_0_), channel_id=1, source_target_pairs={{0,56},{4,60},{8,0},{12,4},{16,8},{20,12},{24,16},{28,20},{32,24},... | collective-permute-start | bytes 147464 | tf_op jit(solution)/shard_map/ppermute | solution.py:350
  134.6 12.2 %collective-permute-start.7 = (bf16[256,768]{1,0:T(8,128)(2,1)}, bf16[256,768]{1,0:T(8,128)(2,1)S(1)}, u32[]{:S(2)}, u32[]{:S(2)}) collective-permute-start(bf16[256,768]{1,0:T(8,128)(2,1)} %stack.13.refs_0_), channel_id=1, source_target_pairs={{0,64},{4,68},{8,72},{12,76},{16,80},{20,84},{24,88},{28,92},{32,9... | collective-permute-start | bytes 1179656 | tf_op jit(solution)/shard_map/ppermute | solution.py:350
  135.4 13.7 %collective-permute-start.8 = (bf16[256,768]{1,0:T(8,128)(2,1)}, bf16[256,768]{1,0:T(8,128)(2,1)S(1)}, u32[]{:S(2)}, u32[]{:S(2)}) collective-permute-start(bf16[256,768]{1,0:T(8,128)(2,1)} %stack.13.refs_0_), channel_id=1, source_target_pairs={{0,128},{4,132},{8,136},{12,140},{16,144},{20,148},{24,152},{28,15... | collective-permute-start | bytes 1179656 | tf_op jit(solution)/shard_map/ppermute | solution.py:350
  136.8 17.6 %collective-permute-start.9 = (bf16[256,768]{1,0:T(8,128)(2,1)}, bf16[256,768]{1,0:T(8,128)(2,1)S(1)}, u32[]{:S(2)}, u32[]{:S(2)}) collective-permute-start(bf16[256,768]{1,0:T(8,128)(2,1)} %stack.13.refs_0_), channel_id=1, source_target_pairs={{0,192},{4,196},{8,200},{12,204},{16,208},{20,212},{24,216},{28,22... | collective-permute-start | bytes 1179656 | tf_op jit(solution)/shard_map/ppermute | solution.py:350
  136.8 41.8 %collective-permute-start.10 = (bf16[256,768]{1,0:T(8,128)(2,1)}, bf16[256,768]{1,0:T(8,128)(2,1)}, u32[]{:S(2)}, u32[]{:S(2)}) collective-permute-start(bf16[256,768]{1,0:T(8,128)(2,1)} %stack.13.refs_0_), channel_id=1, source_target_pairs={{0,4},{4,0},{8,12},{12,8},{16,20},{20,16},{24,28},{28,24},{32,36},... | collective-permute-start | bytes 1179656 | tf_op jit(solution)/shard_map/ppermute | solution.py:350
  146.8 31.8 %copy-start.3 = (bf16[256,768]{1,0:T(8,128)(2,1)}, bf16[256,768]{1,0:T(8,128)(2,1)S(1)}, u32[]{:S(2)}) copy-start(bf16[256,768]{1,0:T(8,128)(2,1)S(1)} %collective-permute-done.7.refs_1_) | copy-start | bytes 1179652
  146.8 31.8 %collective-permute-start.11 = (bf16[256,768]{1,0:T(8,128)(2,1)S(1)}, bf16[256,768]{1,0:T(8,128)(2,1)}, u32[]{:S(2)}, u32[]{:S(2)}) collective-permute-start(bf16[256,768]{1,0:T(8,128)(2,1)S(1)} %collective-permute-done.7.refs_1_), channel_id=1, source_target_pairs={{0,4},{4,0},{8,12},{12,8},{16,20},{20,16},{24,28},{28,24},{32,36},... | collective-permute-start | bytes 1179656 | tf_op jit(solution)/shard_map/ppermute | solution.py:350
  149.1 29.5 %copy-start.4 = (bf16[256,768]{1,0:T(8,128)(2,1)}, bf16[256,768]{1,0:T(8,128)(2,1)S(1)}, u32[]{:S(2)}) copy-start(bf16[256,768]{1,0:T(8,128)(2,1)S(1)} %collective-permute-done.8.refs_2_) | copy-start | bytes 1179652
  149.1 29.5 %collective-permute-start.12 = (bf16[256,768]{1,0:T(8,128)(2,1)S(1)}, bf16[256,768]{1,0:T(8,128)(2,1)}, u32[]{:S(2)}, u32[]{:S(2)}) collective-permute-start(bf16[256,768]{1,0:T(8,128)(2,1)S(1)} %collective-permute-done.8.refs_2_), channel_id=1, source_target_pairs={{0,4},{4,0},{8,12},{12,8},{16,20},{20,16},{24,28},{28,24},{32,36},... | collective-permute-start | bytes 1179656 | tf_op jit(solution)/shard_map/ppermute | solution.py:350
  154.4 24.3 %copy-start.5 = (bf16[256,768]{1,0:T(8,128)(2,1)}, bf16[256,768]{1,0:T(8,128)(2,1)S(1)}, u32[]{:S(2)}) copy-start(bf16[256,768]{1,0:T(8,128)(2,1)S(1)} %collective-permute-done.9.refs_3_) | copy-start | bytes 1179652
  154.4 24.2 %collective-permute-start.13 = (bf16[256,768]{1,0:T(8,128)(2,1)S(1)}, bf16[256,768]{1,0:T(8,128)(2,1)}, u32[]{:S(2)}, u32[]{:S(2)}) collective-permute-start(bf16[256,768]{1,0:T(8,128)(2,1)S(1)} %collective-permute-done.9.refs_3_), channel_id=1, source_target_pairs={{0,4},{4,0},{8,12},{12,8},{16,20},{20,16},{24,28},{28,24},{32,36},... | collective-permute-start | bytes 1179656 | tf_op jit(solution)/shard_map/ppermute | solution.py:350
  183.7 27.4 %all-to-all-start.2 = ((bf16[64,40,128]{2,1,0:T(8,128)(2,1)}), bf16[64,40,128]{2,1,0:T(8,128)(2,1)S(1)}, u32[]{:S(2)}, u32[]{:S(2)}) async-start(bf16[64,40,128]{2,1,0:T(8,128)(2,1)} %get-tuple-element.24.refs_8_), calls=%async_computation.2 | async-start | bytes 1310720 | tf_op jit(solution)/shard_map/all_to_all | solution.py:454
  223.1 9.0 %collective-permute-start.14 = (bf16[128,768]{1,0:T(8,128)(2,1)}, bf16[128,768]{1,0:T(8,128)(2,1)S(1)}, u32[]{:S(2)}, u32[]{:S(2)}) collective-permute-start(bf16[128,768]{1,0:T(8,128)(2,1)} %get-tuple-element.27), channel_id=1, source_target_pairs={{0,1},{1,2},{2,3},{3,0},{4,5},{5,6},{6,7},{7,4},{8,9},{9,10},{10,1... | collective-permute-start | bytes 589832 | tf_op jit(solution)/shard_map/ppermute | solution.py:492
  224.5 7.6 %collective-permute-start.15 = (bf16[128,768]{1,0:T(8,128)(2,1)}, bf16[128,768]{1,0:T(8,128)(2,1)S(1)}, u32[]{:S(2)}, u32[]{:S(2)}) collective-permute-start(bf16[128,768]{1,0:T(8,128)(2,1)} %get-tuple-element.28), channel_id=1, source_target_pairs={{0,3},{1,0},{2,1},{3,2},{4,7},{5,4},{6,5},{7,6},{8,11},{9,8},{10,9... | collective-permute-start | bytes 589832 | tf_op jit(solution)/shard_map/ppermute | solution.py:493
  236.0 11.2 %collective-permute-start.17 = (bf16[256,768]{1,0:T(8,128)(2,1)}, bf16[256,768]{1,0:T(8,128)(2,1)S(1)}, u32[]{:S(2)}, u32[]{:S(2)}) collective-permute-start(bf16[256,768]{1,0:T(8,128)(2,1)} %get-tuple-element.30), channel_id=1, source_target_pairs={{0,3},{1,0},{2,1},{3,2},{4,7},{5,4},{6,5},{7,6},{8,11},{9,8},{10,9... | collective-permute-start | bytes 1179656 | tf_op jit(solution)/shard_map/ppermute | solution.py:513
  238.2 11.8 %collective-permute-start.16 = (bf16[256,768]{1,0:T(8,128)(2,1)}, bf16[256,768]{1,0:T(8,128)(2,1)S(1)}, u32[]{:S(2)}, u32[]{:S(2)}) collective-permute-start(bf16[256,768]{1,0:T(8,128)(2,1)} %get-tuple-element.29), channel_id=1, source_target_pairs={{0,1},{1,2},{2,3},{3,0},{4,5},{5,6},{6,7},{7,4},{8,9},{9,10},{10,1... | collective-permute-start | bytes 1179656 | tf_op jit(solution)/shard_map/ppermute | solution.py:512
  (13 other events, 63.0 us)
Sparse Core Ops, SparseCore 0:
  10.7 129.9 all-gather.2

commit v5 on v4

--- a/solution.py
+++ b/solution.py
@@ -12,7 +12,7 @@
 COLD = 8
 LANES = 128
 X_SIZE, Z_SIZE, CORES = 4, 8, 2
-PIECES = X_SIZE * CORES
+PIECES = 1 + (X_SIZE - 1) * CORES
 RADIX = 256
 F32 = jnp.float32
 BF16 = jnp.bfloat16
@@ -106,7 +106,7 @@
 
 
 def prep_kernel(per_owner, spot_ref, hot_ref, loc_ref, slab_ref, out_ref, col_scr):
-    hot_each = out_ref.shape[0]
+    hot_each = out_ref.shape[0] * 2 // 3
     high_rows = loc_ref.shape[0]
     ids = hot_ref[pl.ds(spot_ref[0] * hot_each // LANES, 1), :]
     high_hot = one_hot(iota((high_rows, LANES), 0) == (ids // LANES))
@@ -121,14 +121,22 @@
     start = pl.multiple_of(spot_ref[0] * hot_each % LANES, hot_each)
     cols = jnp.concatenate([col_scr[pl.ds(start, hot_each), :]] * (per_owner // LANES), axis=1)
     picks = one_hot(iota((hot_each, per_owner), 1).astype(F32) == cols)
-    out_ref[...] = jnp.dot(picks, slab_ref[...], preferred_element_type=F32).astype(BF16)
-
-
-def owner_of(spot_ref, piece, d):
-    x = (spot_ref[0] // (Z_SIZE * CORES) - piece % X_SIZE) & (X_SIZE - 1)
-    z = (spot_ref[0] // CORES - d) & (Z_SIZE - 1)
-    core = (spot_ref[0] + piece // X_SIZE) & (CORES - 1)
-    return (x * Z_SIZE + z) * CORES + core
+    out_ref[0:hot_each, :] = jnp.dot(picks, slab_ref[...], preferred_element_type=F32).astype(BF16)
+    out_ref[hot_each:, :] = jnp.zeros((hot_each // 2, out_ref.shape[1]), BF16)
+
+
+def hot_pieces(spot_ref, hot_refs):
+    base = hot_refs[0]
+    size = base.shape[0] // CORES
+    x, core = spot_ref[0] // (Z_SIZE * CORES), spot_ref[0] & (CORES - 1)
+
+    def owners(dx, c):
+        return [(((x - dx) & (X_SIZE - 1)) * Z_SIZE + z) * CORES + c for z in range(Z_SIZE)]
+
+    for c in range(CORES):
+        yield base[c * size : (c + 1) * size, :], owners(0, c)
+    for n, ref in enumerate(hot_refs[1:]):
+        yield ref[...], owners(n % (X_SIZE - 1) + 1, core ^ (n // (X_SIZE - 1)))
 
 
 def fetch_kernel(capacity, asked_ref, slab_ref, out_ref, picks):
@@ -209,10 +217,10 @@
     hot_each = hot_scr.shape[0] // groups
     q = q_ref[...]
     top = jnp.max(cold_ref[...], axis=0, keepdims=True)
-    for piece, hot_ref in enumerate(hot_refs):
-        got = scale * lax.dot_general(hot_ref[...], q, ROWS_DOT, preferred_element_type=F32)
-        for d in range(Z_SIZE):
-            start = pl.multiple_of(owner_of(spot_ref, piece, d) * hot_each, hot_each)
+    for rows, owners in hot_pieces(spot_ref, hot_refs):
+        got = scale * lax.dot_general(rows, q, ROWS_DOT, preferred_element_type=F32)
+        for d, owner in enumerate(owners):
+            start = pl.multiple_of(owner * hot_each, hot_each)
             hot_scr[pl.ds(start, hot_each), :] = got[d * hot_each : (d + 1) * hot_each]
         top = jnp.maximum(top, jnp.max(got, axis=0, keepdims=True))
     cold = cold_ref[...]
@@ -252,13 +260,12 @@
     hot_refs = refs[:PIECES]
     pay_ref, found_ref, weight_ref, place_ref, out_ref = refs[PIECES:]
     q_rows = out_ref.shape[0]
-    hot_each = hot_refs[0].shape[0] // Z_SIZE
+    hot_each = hot_refs[0].shape[0] // (Z_SIZE * CORES)
     acc = jnp.zeros(out_ref.shape, F32)
     first = (((0,), (0,)), ((), ()))
-    for piece, hot_ref in enumerate(hot_refs):
-        owners = [owner_of(spot_ref, piece, d) for d in range(Z_SIZE)]
+    for rows, owners in hot_pieces(spot_ref, hot_refs):
         coef = jnp.concatenate([pay_ref[o, 0:hot_each, :] for o in owners], axis=0)
-        acc = acc + lax.dot_general(coef, hot_ref[...], first, preferred_element_type=F32)
+        acc = acc + lax.dot_general(coef, rows, first, preferred_element_type=F32)
     chunk = 256
     place = place_ref[...]
     weight = weight_ref[...]
@@ -325,13 +332,6 @@
     out_ref[...] = jnp.dot(at, terms_ref[...], preferred_element_type=F32)
 
 
-def stack_kernel(*refs):
-    out_ref = refs[-1]
-    size = refs[0].shape[0]
-    for n, ref in enumerate(refs[:-1]):
-        out_ref[n * size : (n + 1) * size, :] = ref[...]
-
-
 def merge_kernel(near_ref, first_ref, second_ref, after_ref, before_ref):
     half = first_ref.shape[0]
     after_ref[0:half, :] = (near_ref[0:half, :] + first_ref[...].astype(F32)).astype(BF16)
@@ -349,16 +349,14 @@
     def shift(array, dx, dz, dc):
         return lax.ppermute(array, "corpus", [(member(x, z, c), member(x + dx, z + dz, c + dc)) for x, z, c in spots])
 
-    pieces = [rows] + [shift(rows, 0, d, 0) for d in range(1, Z_SIZE)]
-    rows = pl.pallas_call(
-        stack_kernel,
-        out_shape=jax.ShapeDtypeStruct((Z_SIZE * rows.shape[0], rows.shape[1]), BF16),
-        in_specs=[VMEM_SPEC] * Z_SIZE,
-        out_specs=VMEM_SPEC,
-        name="stack",
-    )(*pieces)
-    pieces = [rows] + [shift(rows, d, 0, 0) for d in range(1, X_SIZE)]
-    return pieces + [shift(p, 0, 0, 1) for p in pieces]
+    groups = [[member(x, z, c) for c in range(CORES) for z in range(Z_SIZE)] for x in range(X_SIZE)]
+    base = lax.all_gather(rows, "corpus", axis=0, tiled=False, axis_index_groups=groups)
+    hot_each, feat = rows.shape[0] * 2 // 3, rows.shape[1]
+    mine = lax.dynamic_slice_in_dim(base, lax.axis_index("corpus") % CORES * Z_SIZE, Z_SIZE)
+    mine = mine[:, :hot_each].reshape(-1, feat)
+    base = base[:, :hot_each].reshape(-1, feat)
+    moved = [shift(mine, d, 0, 0) for d in range(1, X_SIZE)]
+    return [base] + moved + [shift(m, 0, 0, 1) for m in moved]
 
 
 def shards(queries, teacher, slab, candidates, hot_ids, location):
@@ -376,8 +374,17 @@
     spot = jnp.stack([corpus_idx, rep_idx]).astype(jnp.int32)
     loc_table = location.reshape(-1, LANES)
     hot_table = hot_ids.reshape(-1, LANES)
+    own_rows = pl.pallas_call(
+        functools.partial(prep_kernel, per_owner),
+        out_shape=jax.ShapeDtypeStruct((hot_each * 3 // 2, feat), BF16),
+        in_specs=[SMEM_SPEC] + [VMEM_SPEC] * 3,
+        out_specs=VMEM_SPEC,
+        scratch_shapes=[pltpu.VMEM((LANES, LANES), F32)],
+        name="prep",
+    )(spot, hot_table, loc_table, slab)
+    cand_t, own_rows = lax.optimization_barrier((candidates.T, own_rows))
+    hot_rows = gather_hot(own_rows)
     gathered = lax.all_gather(queries, "corpus", axis=0, tiled=False)
-    cand_t = candidates.T
     req, place, sel = pl.pallas_call(
         functools.partial(request_kernel, per_owner, groups),
         out_shape=(
@@ -390,15 +397,6 @@
         scratch_shapes=[pltpu.VMEM((cand_count, q_rows), F32)],
         name="request",
     )(cand_t, hot_ids.reshape(1, hot_total), loc_table)
-    own_rows = pl.pallas_call(
-        functools.partial(prep_kernel, per_owner),
-        out_shape=jax.ShapeDtypeStruct((hot_each, feat), BF16),
-        in_specs=[SMEM_SPEC] + [VMEM_SPEC] * 3,
-        out_specs=VMEM_SPEC,
-        scratch_shapes=[pltpu.VMEM((LANES, LANES), F32)],
-        name="prep",
-    )(spot, hot_table, loc_table, slab)
-    hot_rows = gather_hot(own_rows)
     asked = lax.all_to_all(req.reshape(groups, 1, LANES), "corpus", split_axis=0, concat_axis=0, tiled=True)
     asked = asked.reshape(groups, LANES)
     slots = groups * capacity

time: 260 us -> 228 us (0.88)
  waiting for transfers between devices: 92.2 us -> 70.2 us
  starting transfers between devices: 39.1 us -> 28.1 us
    ppermute x14 -> x6, waiting for transfers between devices: 82.5 us -> 33.5 us  [shift(): lax.ppermute(array, 'corpus', [(member(x, z, c), member(x + dx, z + dz, c...]
    all_gather x1, waiting for transfers between devices: 0.01 us -> 28.8 us  [shards(): gathered = lax.all_gather(queries, 'corpus', axis=0, tiled=False)]
    ppermute x14 -> x6, starting transfers between devices: 18.8 us -> 3.2 us  [shift(): lax.ppermute(array, 'corpus', [(member(x, z, c), member(x + dx, z + dz, c...]
    all_to_all x1, starting transfers between devices: 8.09 us -> 12.6 us  [shards(): got = lax.all_to_all(pay, 'corpus', split_axis=0, concat_axis=0, tiled=True)]
    all_to_all x1, waiting for transfers between devices: 3.91 us -> 0.01 us  [shards(): got = lax.all_to_all(pay, 'corpus', split_axis=0, concat_axis=0, tiled=True)]
    slice x0 -> x2, local copies, waits for them, and re-layouts: none -> 3.09 us  [the longest x1 2.06 us: gather_hot(): base = base[:, :hot_each].reshape(-1, feat)]
  transfers between devices with their start and end apart: 21 -> 14, of which waited for: 10 -> 9; matrix products, arithmetic and copies ran while one was open for 6% -> 8% of each run, Pallas kernels for 22% -> 23%
where the time goes in v5:
time: 228 us; the launch traced here: 226 us
  waiting for transfers between devices  70.2 us (31%)
  Pallas kernels  69.3 us (30%)
  starting transfers between devices  28.1 us (12%)
  local copies, waits for them, and re-layouts  20.5 us (9%)
  blocking collectives  19.7 us (9%)
  between operations  14.2 us (6%)
  other arithmetic  4.36 us (2%)
    ppermute x6, waiting for transfers between devices, shift(): lax.ppermute(array, 'corpus', [(member(x, z, c), member(x + dx, z + dz, c...  33.5 us
    all_gather x1, waiting for transfers between devices, shards(): gathered = lax.all_gather(queries, 'corpus', axis=0, tiled=False)  28.8 us
    all_to_all x1, blocking collectives, shards(): lax.all_to_all(req.reshape(groups, 1, LANES), 'corpus', split_axis=0, con...  19.7 us
    pallas_call x1, Pallas kernels, shards(): pl.pallas_call(count_kernel, out_shape=(jax.ShapeDtypeStruct((hot_total,...  18.5 us
    gather x1, local copies, waits for them, and re-layouts, shards(): gathered.reshape(-1, feat)  12.9 us
    all_to_all x1, starting transfers between devices, shards(): got = lax.all_to_all(pay, 'corpus', split_axis=0, concat_axis=0, tiled=True)  12.6 us
    pallas_call x1, Pallas kernels, shards(): pl.pallas_call(functools.partial(slab_kernel, scale, capacity, reps), gri...  11.1 us
    pallas_call x2, Pallas kernels, land(): pl.pallas_call(functools.partial(near_kernel, reps, shifts), out_shape=ja...  8.01 us
  transfers between devices with their start and end apart: 14, of which 9 were waited for; matrix products, arithmetic and copies ran while one was open for 8% of the time, Pallas kernels for 23%

profile of v5, /device:TPU:6, one launch (start us, length us, event | category | flops | bytes accessed | tf_op | source)
XLA Modules:
  0.0 226.3 jit_solution(16100807001935571945)
XLA Ops:
  7.9 3.1 %prep.1 = bf16[48,768]{1,0:T(8,128)(2,1)} custom-call(s32[2]{0:T(128)} %pad_add_fusion.1.spot_ref, s32[16,128]{1,0:T(8,128)} %bitcast.35, s32[512,128]{1,0:T(8,128)} %bitcast.26, bf16[1024,768]{1,0:T(8,128)(2,1)} %slab_ref.3), custom_call_target="tpu_custom_call" | custom-call | tf_op jit(solution)/shard_map/prep/pallas_call | solution.py:377
  11.7 6.2 %request.1 = (s32[64,128]{1,0:T(8,128)}, s32[16,128]{1,0:T(8,128)}, s32[64,128]{1,0:T(8,128)}) custom-call(s32[64,128]{1,0:T(8,128)} %bitcast.38, s32[1,2048]{1,0:T(1,128)} %bitcast.36, s32[512,128]{1,0:T(8,128)} %bitcast.27), custom_call_target="tpu_custom_call" | custom-call | tf_op jit(solution)/shard_map/request/pallas_call | solution.py:388
  18.0 19.7 %all_to_all.15 = s32[64,1,128]{2,1,0:T(1,128)} all-to-all(s32[64,1,128]{2,1,0:T(1,128)} %bitcast.40), channel_id=1, replica_groups=mesh['corpus'=64,'rep'=4] {'corpus'}, dimensions={0} | all-to-all | bytes 65536 | tf_op jit(solution)/shard_map/all_to_all | solution.py:400
  37.6 5.9 %fetch.1 = bf16[1536,768]{1,0:T(8,128)(2,1)} custom-call(s32[64,128]{1,0:T(8,128)} %bitcast.33, bf16[1024,768]{1,0:T(8,128)(2,1)} %slab_ref.3), custom_call_target="tpu_custom_call" | custom-call | tf_op jit(solution)/shard_map/fetch/pallas_call | solution.py:404
  43.6 6.7 %all-to-all-start.1 = ((bf16[64,24,768]{2,1,0:T(8,128)(2,1)}), bf16[64,24,768]{2,1,0:T(8,128)(2,1)S(1)}, u32[]{:S(2)}, u32[]{:S(2)}) async-start(bf16[64,24,768]{2,1,0:T(8,128)(2,1)} %bitcast.23), calls=%async_computation.1 | async-start | bytes 4718592 | tf_op jit(solution)/shard_map/all_to_all | solution.py:413
  50.3 2.2 all-gather.5.cloned.1.call-done
  54.3 2.4 %collective-permute-start.1 = (bf16[256,768]{1,0:T(8,128)(2,1)S(1)}, bf16[256,768]{1,0:T(8,128)(2,1)S(1)}, u32[]{:S(2)}, u32[]{:S(2)}) collective-permute-start(bf16[256,768]{1,0:T(8,128)(2,1)S(1)} %bitcast.31), channel_id=1, source_target_pairs={{0,128},{4,132},{8,136},{12,140},{16,144},{20,148},{24,152},{28,15... | collective-permute-start | bytes 1179656 | tf_op jit(solution)/shard_map/ppermute | solution.py:350
  56.7 17.1 %collective-permute-done.refs_1_ = bf16[256,768]{1,0:T(8,128)(2,1)S(1)} collective-permute-done((bf16[256,768]{1,0:T(8,128)(2,1)S(1)}, bf16[256,768]{1,0:T(8,128)(2,1)S(1)}, u32[]{:S(2)}, u32[]{:S(2)}) %collective-permute-start) | collective-permute-done | bytes 393248 | tf_op jit(solution)/shard_map/ppermute | solution.py:350
  73.8 2.3 %collective-permute-done.1.refs_2_ = bf16[256,768]{1,0:T(8,128)(2,1)S(1)} collective-permute-done((bf16[256,768]{1,0:T(8,128)(2,1)S(1)}, bf16[256,768]{1,0:T(8,128)(2,1)S(1)}, u32[]{:S(2)}, u32[]{:S(2)}) %collective-permute-start.1) | collective-permute-done | bytes 393248 | tf_op jit(solution)/shard_map/ppermute | solution.py:350
  76.0 14.1 %collective-permute-done.2.refs_3_ = bf16[256,768]{1,0:T(8,128)(2,1)S(1)} collective-permute-done((bf16[256,768]{1,0:T(8,128)(2,1)S(1)}, bf16[256,768]{1,0:T(8,128)(2,1)S(1)}, u32[]{:S(2)}, u32[]{:S(2)}) %collective-permute-start.2) | collective-permute-done | bytes 393248 | tf_op jit(solution)/shard_map/ppermute | solution.py:350
  90.3 18.5 %count.1 = (f32[2048,128]{1,0:T(8,128)}, f32[2048,128]{1,0:T(8,128)}, f32[16,128]{1,0:T(8,128)}) custom-call(s32[64,128]{1,0:T(8,128)} %bitcast.39, f32[64,128]{1,0:T(8,128)} %bitcast.41, s32[16,128]{1,0:T(8,128)} %bitcast.37, s32[64,128]{1,0:T(8,128)} %get-tuple-element.23.sel_ref), custom_call_target="tpu_custom_call" | custom-call | flops 80000000 | bytes 3000000 | tf_op jit(solution)/shard_map/count/pallas_call | solution.py:415
  113.3 4.2 %cold.1.refs_7_ = f32[8,128]{1,0:T(8,128)} custom-call(bf16[128,768]{1,0:T(8,128)(2,1)} %q_ref.3, bf16[1536,768]{1,0:T(8,128)(2,1)} %bitcast.21, s32[16,128]{1,0:T(8,128)} %get-tuple-element.22.place_ref.refs_10_), custom_call_target="tpu_custom_call" | custom-call | tf_op jit(solution)/shard_map/cold/pallas_call | solution.py:433
  117.6 5.1 %score.1 = (f32[1,128]{1,0:T(1,128)}, bf16[64,40,128]{2,1,0:T(8,128)(2,1)}, f32[8,128]{1,0:T(8,128)}) custom-call(s32[2]{0:T(128)} %pad_add_fusion.1.spot_ref, bf16[128,768]{1,0:T(8,128)(2,1)} %q_ref.3, bf16[512,768]{1,0:T(8,128)(2,1)} %bitcast.24, bf16[256,768]{1,0:T(8,128)(2,1)} %copy-done.3, bf16[256,768]{1,0:T(8,128)(2,1)} %copy-done.4, ...), custom_call_target="tpu_custom_call" | custom-call | tf_op jit(solution)/shard_map/score/pallas_call | solution.py:440
  122.7 12.6 %all-to-all-start.2 = ((bf16[64,40,128]{2,1,0:T(8,128)(2,1)}), bf16[64,40,128]{2,1,0:T(8,128)(2,1)S(1)}, u32[]{:S(2)}, u32[]{:S(2)}) async-start(bf16[64,40,128]{2,1,0:T(8,128)(2,1)} %get-tuple-element.28.refs_7_), calls=%async_computation.2 | async-start | bytes 1310720 | tf_op jit(solution)/shard_map/all_to_all | solution.py:452
  137.8 28.8 %all-gather.7.cloned.1.call-done = bf16[8192,768]{1,0:T(8,128)(2,1)} async-done(((bf16[128,768]{1,0:T(8,128)(2,1)}), bf16[8192,768]{1,0:T(8,128)(2,1)}) %all-gather.7.cloned.1.call-update) | async-done | bytes 12582928 | tf_op jit(solution)/shard_map/all_gather | solution.py:387
  166.6 12.9 %gather_fusion = bf16[1536,768]{1,0:T(8,128)(2,1)} fusion(bf16[8192,768]{1,0:T(8,128)(2,1)} %all-gather.7.cloned.1.call-done, s32[2048]{0:T(1024)S(1)} %pad_clamp_fusion), kind=kCustom, calls=%fused_computation | custom fusion | bytes 4724736 | tf_op jit(solution)/shard_map/gather | solution.py:463
  180.3 11.1 %slab_grad.1 = (bf16[128,768]{1,0:T(8,128)(2,1)}, bf16[128,768]{1,0:T(8,128)(2,1)}, bf16[1664,768]{1,0:T(8,128)(2,1)}) custom-call(s32[2]{0:T(128)} %pad_add_fusion.1.spot_ref, bf16[64,40,128]{2,1,0:T(8,128)(2,1)} %copy-done.2, bf16[64,128,768]{2,1,0:T(8,128)(2,1)} %bitcast.20, bf16[1536,768]{1,0:T(8,128)(2,1)} %gather_fusion, s32[1,1664]{1,0:T(1,128)} %pad_add_fusion.loc_ref), custom_call_target="tpu_custom_call" | custom-call | tf_op jit(solution)/shard_map/slab_grad/pallas_call | solution.py:473
  194.7 4.5 %shard_map.86.near_ref = f32[512,768]{1,0:T(8,128)} custom-call(s32[2]{0:T(128)} %pad_add_fusion.1.spot_ref, bf16[1664,768]{1,0:T(8,128)(2,1)} %get-tuple-element.30.terms_ref, s32[1,1664]{1,0:T(1,128)} %pad_add_fusion.loc_ref), custom_call_target="tpu_custom_call" | custom-call | flops 2000000000 | bytes 6000000 | tf_op jit(solution)/shard_map/pallas_call | solution.py:494
  201.3 2.5 %merge.1 = (bf16[256,768]{1,0:T(8,128)(2,1)}, bf16[256,768]{1,0:T(8,128)(2,1)}) custom-call(f32[512,768]{1,0:T(8,128)} %shard_map.86.near_ref, bf16[128,768]{1,0:T(8,128)(2,1)} %copy-done.7, bf16[128,768]{1,0:T(8,128)(2,1)} %copy-done.8), custom_call_target="tpu_custom_call" | custom-call | tf_op jit(solution)/shard_map/merge/pallas_call | solution.py:503
  203.8 2.3 %collective-permute-start.9 = (bf16[256,768]{1,0:T(8,128)(2,1)}, bf16[256,768]{1,0:T(8,128)(2,1)S(1)}, u32[]{:S(2)}, u32[]{:S(2)}) collective-permute-start(bf16[256,768]{1,0:T(8,128)(2,1)} %get-tuple-element.34), channel_id=1, source_target_pairs={{0,3},{1,0},{2,1},{3,2},{4,7},{5,4},{6,5},{7,6},{8,11},{9,8},{10,9... | collective-permute-start | bytes 1179656 | tf_op jit(solution)/shard_map/ppermute | solution.py:511
  206.1 4.6 %query_grad.1 = f32[128,768]{1,0:T(8,128)} custom-call(s32[2]{0:T(128)} %pad_add_fusion.1.spot_ref, bf16[512,768]{1,0:T(8,128)(2,1)} %bitcast.25, bf16[256,768]{1,0:T(8,128)(2,1)} %copy-done.3, bf16[256,768]{1,0:T(8,128)(2,1)} %copy-done.4, bf16[256,768]{1,0:T(8,128)(2,1)} %copy-done.5, bf16[256,768]{1,0:T(8,128)(2,1)} %collective-permute-done.3.refs_4_, ...), custom_call_target="tpu_custom_call" | custom-call | flops 700000000 | bytes 7000000 | tf_op jit(solution)/shard_map/query_grad/pallas_call | solution.py:453
  210.7 3.5 %shard_map.85 = f32[256,768]{1,0:T(8,128)} custom-call(s32[2]{0:T(128)} %pad_add_fusion.1.spot_ref, bf16[1664,768]{1,0:T(8,128)(2,1)} %get-tuple-element.30.terms_ref, s32[1,1664]{1,0:T(1,128)} %pad_add_fusion.loc_ref), custom_call_target="tpu_custom_call" | custom-call | flops 2000000000 | bytes 6000000 | tf_op jit(solution)/shard_map/pallas_call | solution.py:494
  214.4 2.9 %collective-permute-done.8 = bf16[256,768]{1,0:T(8,128)(2,1)S(1)} collective-permute-done((bf16[256,768]{1,0:T(8,128)(2,1)}, bf16[256,768]{1,0:T(8,128)(2,1)S(1)}, u32[]{:S(2)}, u32[]{:S(2)}) %collective-permute-start.8) | collective-permute-done | bytes 393248 | tf_op jit(solution)/shard_map/ppermute | solution.py:510
  217.4 2.1 convert_add_fusion
  (54 shorter events, 16.7 us)
Async XLA Ops:
  7.2 45.4 %all-gather.5.cloned.1.call-start = ((), (), s32[]{:S(2)}) async-start(), calls=%async_computation.3 | async-start | bytes 1253376 | tf_op jit(solution)/shard_map/all_gather | solution.py:353
  11.0 155.6 %all-gather.7.cloned.1.call-start = ((), (), s32[]{:S(2)}) async-start(), calls=%async_computation.4 | async-start | bytes 12779520 | tf_op jit(solution)/shard_map/all_gather | solution.py:387
  43.6 68.4 %all-to-all-start.1 = ((bf16[64,24,768]{2,1,0:T(8,128)(2,1)}), bf16[64,24,768]{2,1,0:T(8,128)(2,1)S(1)}, u32[]{:S(2)}, u32[]{:S(2)}) async-start(bf16[64,24,768]{2,1,0:T(8,128)(2,1)} %bitcast.23), calls=%async_computation.1 | async-start | bytes 4718592 | tf_op jit(solution)/shard_map/all_to_all | solution.py:413
  53.6 20.2 %collective-permute-start = (bf16[256,768]{1,0:T(8,128)(2,1)S(1)}, bf16[256,768]{1,0:T(8,128)(2,1)S(1)}, u32[]{:S(2)}, u32[]{:S(2)}) collective-permute-start(bf16[256,768]{1,0:T(8,128)(2,1)S(1)} %bitcast.30), channel_id=1, source_target_pairs={{0,64},{4,68},{8,72},{12,76},{16,80},{20,84},{24,88},{28,92},{32,9... | collective-permute-start | bytes 1179656 | tf_op jit(solution)/shard_map/ppermute | solution.py:350
  54.3 21.7 %collective-permute-start.1 = (bf16[256,768]{1,0:T(8,128)(2,1)S(1)}, bf16[256,768]{1,0:T(8,128)(2,1)S(1)}, u32[]{:S(2)}, u32[]{:S(2)}) collective-permute-start(bf16[256,768]{1,0:T(8,128)(2,1)S(1)} %bitcast.31), channel_id=1, source_target_pairs={{0,128},{4,132},{8,136},{12,140},{16,144},{20,148},{24,152},{28,15... | collective-permute-start | bytes 1179656 | tf_op jit(solution)/shard_map/ppermute | solution.py:350
  56.7 33.5 %collective-permute-start.2 = (bf16[256,768]{1,0:T(8,128)(2,1)S(1)}, bf16[256,768]{1,0:T(8,128)(2,1)S(1)}, u32[]{:S(2)}, u32[]{:S(2)}) collective-permute-start(bf16[256,768]{1,0:T(8,128)(2,1)S(1)} %bitcast.32), channel_id=1, source_target_pairs={{0,192},{4,196},{8,200},{12,204},{16,208},{20,212},{24,216},{28,22... | collective-permute-start | bytes 1179656 | tf_op jit(solution)/shard_map/ppermute | solution.py:350
  73.8 43.8 %copy-start.3 = (bf16[256,768]{1,0:T(8,128)(2,1)}, bf16[256,768]{1,0:T(8,128)(2,1)S(1)}, u32[]{:S(2)}) copy-start(bf16[256,768]{1,0:T(8,128)(2,1)S(1)} %collective-permute-done.refs_1_) | copy-start | bytes 1179652
  73.8 43.8 %collective-permute-start.3 = (bf16[256,768]{1,0:T(8,128)(2,1)S(1)}, bf16[256,768]{1,0:T(8,128)(2,1)}, u32[]{:S(2)}, u32[]{:S(2)}) collective-permute-start(bf16[256,768]{1,0:T(8,128)(2,1)S(1)} %collective-permute-done.refs_1_), channel_id=1, source_target_pairs={{0,4},{4,0},{8,12},{12,8},{16,20},{20,16},{24,28},{28,24},{32,36},... | collective-permute-start | bytes 1179656 | tf_op jit(solution)/shard_map/ppermute | solution.py:350
  76.0 41.5 %copy-start.4 = (bf16[256,768]{1,0:T(8,128)(2,1)}, bf16[256,768]{1,0:T(8,128)(2,1)S(1)}, u32[]{:S(2)}) copy-start(bf16[256,768]{1,0:T(8,128)(2,1)S(1)} %collective-permute-done.1.refs_2_) | copy-start | bytes 1179652
  76.0 41.5 %collective-permute-start.4 = (bf16[256,768]{1,0:T(8,128)(2,1)S(1)}, bf16[256,768]{1,0:T(8,128)(2,1)}, u32[]{:S(2)}, u32[]{:S(2)}) collective-permute-start(bf16[256,768]{1,0:T(8,128)(2,1)S(1)} %collective-permute-done.1.refs_2_), channel_id=1, source_target_pairs={{0,4},{4,0},{8,12},{12,8},{16,20},{20,16},{24,28},{28,24},{32,36},... | collective-permute-start | bytes 1179656 | tf_op jit(solution)/shard_map/ppermute | solution.py:350
  90.2 27.4 %copy-start.5 = (bf16[256,768]{1,0:T(8,128)(2,1)}, bf16[256,768]{1,0:T(8,128)(2,1)S(1)}, u32[]{:S(2)}) copy-start(bf16[256,768]{1,0:T(8,128)(2,1)S(1)} %collective-permute-done.2.refs_3_) | copy-start | bytes 1179652
  90.2 27.4 %collective-permute-start.5 = (bf16[256,768]{1,0:T(8,128)(2,1)S(1)}, bf16[256,768]{1,0:T(8,128)(2,1)}, u32[]{:S(2)}, u32[]{:S(2)}) collective-permute-start(bf16[256,768]{1,0:T(8,128)(2,1)S(1)} %collective-permute-done.2.refs_3_), channel_id=1, source_target_pairs={{0,4},{4,0},{8,12},{12,8},{16,20},{20,16},{24,28},{28,24},{32,36},... | collective-permute-start | bytes 1179656 | tf_op jit(solution)/shard_map/ppermute | solution.py:350
  112.0 1.4 copy-start
  117.6 18.5 %copy-start.1 = (s32[65536]{0:T(1024)S(1)}, s32[65536]{0:T(1024)}, u32[]{:S(2)}) copy-start(s32[65536]{0:T(1024)} %param.11) | copy-start | bytes 786436
  117.6 19.3 %copy-start.6 = (s32[64,1,128]{2,1,0:T(1,128)S(1)}, s32[64,1,128]{2,1,0:T(1,128)}, u32[]{:S(2)}) copy-start(s32[64,1,128]{2,1,0:T(1,128)} %all_to_all.15) | copy-start | bytes 98308
  122.7 56.8 %all-to-all-start.2 = ((bf16[64,40,128]{2,1,0:T(8,128)(2,1)}), bf16[64,40,128]{2,1,0:T(8,128)(2,1)S(1)}, u32[]{:S(2)}, u32[]{:S(2)}) async-start(bf16[64,40,128]{2,1,0:T(8,128)(2,1)} %get-tuple-element.28.refs_7_), calls=%async_computation.2 | async-start | bytes 1310720 | tf_op jit(solution)/shard_map/all_to_all | solution.py:452
  179.5 0.8 copy-start.2
  191.4 8.5 %collective-permute-start.6 = (bf16[128,768]{1,0:T(8,128)(2,1)}, bf16[128,768]{1,0:T(8,128)(2,1)S(1)}, u32[]{:S(2)}, u32[]{:S(2)}) collective-permute-start(bf16[128,768]{1,0:T(8,128)(2,1)} %get-tuple-element.31), channel_id=1, source_target_pairs={{0,1},{1,2},{2,3},{3,0},{4,5},{5,6},{6,7},{7,4},{8,9},{9,10},{10,1... | collective-permute-start | bytes 589832 | tf_op jit(solution)/shard_map/ppermute | solution.py:490
  192.8 7.1 %collective-permute-start.7 = (bf16[128,768]{1,0:T(8,128)(2,1)}, bf16[128,768]{1,0:T(8,128)(2,1)S(1)}, u32[]{:S(2)}, u32[]{:S(2)}) collective-permute-start(bf16[128,768]{1,0:T(8,128)(2,1)} %get-tuple-element.32), channel_id=1, source_target_pairs={{0,3},{1,0},{2,1},{3,2},{4,7},{5,4},{6,5},{7,6},{8,11},{9,8},{10,9... | collective-permute-start | bytes 589832 | tf_op jit(solution)/shard_map/ppermute | solution.py:491
  199.9 0.7 copy-start.7
  200.6 0.7 copy-start.8
  203.8 10.6 %collective-permute-start.9 = (bf16[256,768]{1,0:T(8,128)(2,1)}, bf16[256,768]{1,0:T(8,128)(2,1)S(1)}, u32[]{:S(2)}, u32[]{:S(2)}) collective-permute-start(bf16[256,768]{1,0:T(8,128)(2,1)} %get-tuple-element.34), channel_id=1, source_target_pairs={{0,3},{1,0},{2,1},{3,2},{4,7},{5,4},{6,5},{7,6},{8,11},{9,8},{10,9... | collective-permute-start | bytes 1179656 | tf_op jit(solution)/shard_map/ppermute | solution.py:511
  206.1 11.3 %collective-permute-start.8 = (bf16[256,768]{1,0:T(8,128)(2,1)}, bf16[256,768]{1,0:T(8,128)(2,1)S(1)}, u32[]{:S(2)}, u32[]{:S(2)}) collective-permute-start(bf16[256,768]{1,0:T(8,128)(2,1)} %get-tuple-element.33), channel_id=1, source_target_pairs={{0,1},{1,2},{2,3},{3,0},{4,5},{5,6},{6,7},{7,4},{8,9},{9,10},{10,1... | collective-permute-start | bytes 1179656 | tf_op jit(solution)/shard_map/ppermute | solution.py:510
Sparse Core Ops, SparseCore 0:
  11.1 41.4 all-gather.4
  55.3 111.2 all-gather.6
